TPU v7x, 32 devices: a whole 2x2x4 slice. The times are simulated.
32 devices in a mesh: depth: 2 (over core), freq: 16 (over z, y, x).
Axes of the slice: x: 2, y: 2, z: 4, core: 2. Of those that a mesh axis runs over, the one named last changes fastest.
Arguments:
- p_top: bfloat16 [16, 1024, 128], P('freq'), may hold values from -6 to 6
- upgoing: bfloat16 [2, 16, 1024, 128], P('depth', 'freq'), may hold values from -6 to 6
- extrapolator: bfloat16 [2, 16, 2, 1024, 1024], P('depth', 'freq'), may hold values from -0.125 to 0.125
- reflectivity: bfloat16 [2, 1024, 1024], P('depth', 'freq'), may hold values from -0.1875 to 0.1875
Outputs:
- wavefields: bfloat16 [2, 16, 1024, 128], P('depth', 'freq')
- images: float32 [2, 1024, 1024], P('depth', 'freq')
All inputs are finite; a program needn't handle non-finite values.
Results may differ from a plain program's by a relative error of at most 0.014.
Values may be sent and summed in bfloat16 or wider, within the bound.
No kernel may reach another device: no remote copies, remote signals or barrier semaphores. Data moves between devices by JAX's collectives and lax.ppermute only.
A program may use at most 64 MiB of HBM per device.

v0:
```python
import functools

import jax
import jax.numpy as jnp
from jax import lax
from jax.experimental import pallas as pl
from jax.experimental.pallas import tpu as pltpu
from jax.sharding import PartitionSpec as P


VMEM = pl.BlockSpec(memory_space=pltpu.VMEM)
MIB = 1 << 20


def plane_size(devices):
    size = 1
    while 4 * size * size <= devices:
        size *= 2
    return size


def swap(value, by):
    devices = lax.axis_size("freq")
    return lax.ppermute(value, "freq", [(i, i ^ by) for i in range(devices)])


def lower(value, by):
    levels, devices = lax.axis_size("depth"), lax.axis_size("freq")
    pairs = [
        (d * devices + i, (d + 1) * devices + (i ^ by) if d + 1 < levels else i)
        for d in range(levels)
        for i in range(devices)
    ]
    return lax.ppermute(value, ("depth", "freq"), pairs)


def raise_top(value, by):
    levels, devices = lax.axis_size("depth"), lax.axis_size("freq")
    pairs = [((devices if levels > 1 else 0) + i, i ^ by) for i in range(devices)]
    if levels > 1:
        pairs += [(i, devices + i) for i in range(devices)]
    return lax.ppermute(value, ("depth", "freq"), pairs)


def params(limit):
    return pltpu.CompilerParams(vmem_limit_bytes=limit)


def stage_kernel(count, *refs):
    sources, targets, sems = refs[:count], refs[count : 2 * count], refs[2 * count]
    copies = [pltpu.make_async_copy(a, b, sems.at[k]) for k, (a, b) in enumerate(zip(sources, targets))]
    for copy in copies:
        copy.start()
    for copy in copies:
        copy.wait()


def stage(*arrays):
    count = len(arrays)
    size = sum(a.size * a.dtype.itemsize for a in arrays)
    return pl.pallas_call(
        functools.partial(stage_kernel, count),
        out_shape=[jax.ShapeDtypeStruct(a.shape, a.dtype) for a in arrays],
        in_specs=[pl.BlockSpec(memory_space=pltpu.HBM)] * count,
        out_specs=[VMEM] * count,
        scratch_shapes=[pltpu.SemaphoreType.DMA((count,))],
        compiler_params=params(16 * MIB),
        cost_estimate=pl.CostEstimate(flops=0, bytes_accessed=2 * size, transcendentals=0),
        name="stage_inputs",
    )(*arrays)


def pieces_kernel(line, plane, *refs):
    blocks, ups, outs = refs[:line], refs[line : line + plane], refs[line + plane :]
    rows = jnp.concatenate([b[...] for b in blocks], axis=0)
    for up, out in zip(ups, outs):
        out[...] = jnp.dot(rows, up[...], preferred_element_type=jnp.float32).astype(out.dtype)


def rq_pieces(blocks, ups):
    line, plane = len(blocks), len(ups)
    rows, nx = blocks[0].shape
    cols = ups[0].shape[1]
    tall = line * rows
    out_shape = [jax.ShapeDtypeStruct((tall, cols), jnp.float32)]
    out_shape += [jax.ShapeDtypeStruct((tall, cols), jnp.bfloat16)] * (plane - 1)
    return pl.pallas_call(
        functools.partial(pieces_kernel, line, plane),
        out_shape=out_shape,
        in_specs=[VMEM] * (line + plane),
        out_specs=[VMEM] * plane,
        compiler_params=params(16 * MIB),
        cost_estimate=pl.CostEstimate(
            flops=2 * tall * nx * cols * plane, bytes_accessed=2 * nx * (tall + plane * cols), transcendentals=0
        ),
        name="rq_pieces",
    )(*blocks, *ups)


def advance_kernel(line, plane, *refs):
    top, moved, pieces, weights = refs[0], refs[1], refs[2 : 2 + plane], refs[2 + plane]
    out, diff = refs[-2:]
    me = lax.axis_index("freq")
    first = lax.axis_index("depth") == 0
    rows = top.shape[0] // (line * plane)
    cols = top.shape[1]
    for z in range(line):
        for q in range(plane):
            at = pl.multiple_of((me ^ (z * plane + q)) * rows, rows)
            rq = pieces[q][z * rows : (z + 1) * rows, :].astype(jnp.float32)
            field = jnp.where(first, top[pl.ds(at, rows), :], moved[pl.ds(at, rows), :]).astype(jnp.float32)
            diff[pl.ds(at, rows), :] = (field - rq).astype(jnp.bfloat16)
    straight = diff[...]
    half = cols // 2
    turned = jnp.concatenate([-straight[:, half:], straight[:, :half]], axis=1)
    out[...] = (
        jnp.dot(weights[0], straight, preferred_element_type=jnp.float32)
        + jnp.dot(weights[1], turned, preferred_element_type=jnp.float32)
    ).astype(jnp.bfloat16)


def advance(top, moved, pieces, weights, line, plane):
    nx, cols = top.shape
    return pl.pallas_call(
        functools.partial(advance_kernel, line, plane),
        out_shape=jax.ShapeDtypeStruct((nx, cols), jnp.bfloat16),
        in_specs=[VMEM] * (3 + plane),
        out_specs=VMEM,
        scratch_shapes=[pltpu.VMEM((nx, cols), jnp.bfloat16)],
        compiler_params=params(24 * MIB),
        cost_estimate=pl.CostEstimate(flops=4 * nx * nx * cols, bytes_accessed=4 * nx * nx, transcendentals=0),
        name="advance",
    )(top, moved, *pieces, weights)


def picture_kernel(line, plane, *refs):
    ups, tops, fields, outs = refs[:plane], refs[plane : 2 * plane], refs[2 * plane : 3 * plane], refs[3 * plane :]
    me = lax.axis_index("freq")
    first = lax.axis_index("depth") == 0
    rows = outs[0].shape[0]
    left = jnp.concatenate(
        [
            jnp.concatenate(
                [up[pl.ds(pl.multiple_of((me ^ (z * plane)) * rows, rows), rows), :] for z in range(line)],
                axis=0,
            )
            for up in ups
        ],
        axis=1,
    )
    right = jnp.concatenate([jnp.where(first, t[...], f[...]) for t, f in zip(tops, fields)], axis=1)
    total = lax.dot_general(left, right, (((1,), (1,)), ((), ())), preferred_element_type=jnp.float32)
    for z, out in enumerate(outs):
        out[...] = total[z * rows : (z + 1) * rows].astype(out.dtype)


def picture_parts(ups, tops, fields, line):
    plane = len(ups)
    nx, cols = ups[0].shape
    rows = nx // (line * plane)
    out_shape = [jax.ShapeDtypeStruct((rows, nx), jnp.float32)]
    out_shape += [jax.ShapeDtypeStruct((rows, nx), jnp.bfloat16)] * (line - 1)
    return pl.pallas_call(
        functools.partial(picture_kernel, line, plane),
        out_shape=out_shape,
        in_specs=[VMEM] * (3 * plane),
        out_specs=[VMEM] * line,
        compiler_params=params(24 * MIB),
        cost_estimate=pl.CostEstimate(
            flops=2 * line * rows * nx * cols * plane, bytes_accessed=4 * nx * cols * plane, transcendentals=0
        ),
        name="picture_parts",
    )(*ups, *tops, *fields)


def local(p_top, upgoing, extrapolator, reflectivity):
    return program(p_top[0], upgoing[0, 0], extrapolator[0, 0], reflectivity[0])


def program(top, upper, weights, own_rows):
    sections = lax.axis_size("depth")
    devices = lax.axis_size("freq")
    plane = plane_size(devices)
    line = devices // plane

    blocks = [swap(own_rows, z * plane) for z in range(1, line)]
    ups = [swap(upper, q) for q in range(1, plane)]
    tops = [raise_top(top, q) for q in range(1, plane)]
    top, upper, weights, own_rows = stage(top, upper, weights, own_rows)
    blocks, ups, tops = [own_rows] + blocks, [upper] + ups, [top] + tops
    pieces = rq_pieces(blocks, ups)
    pieces = [pieces[0]] + [swap(pieces[q], q) for q in range(1, plane)]

    moved = top
    for _ in range(1, sections):
        below = advance(top, moved, pieces, weights, line, plane)
        moved = lower(below, 0)
    fields = [moved] + [lower(below, q) for q in range(1, plane)]
    parts = picture_parts(ups, tops, fields, line)
    total = parts[0]
    for z in range(1, line):
        total = total + swap(parts[z], z * plane).astype(jnp.float32)
    scale = (float(upper.shape[1]) * devices) ** (-0.5)
    below = advance(top, moved, pieces, weights, line, plane)
    return (below[None, None], (total * scale)[None])


def solution(mesh):
    in_specs = (
        P("freq", None, None),
        P("depth", "freq", None, None),
        P("depth", "freq", None, None, None),
        P("depth", "freq", None),
    )
    out_specs = (P("depth", "freq", None, None), P("depth", "freq", None))
    return jax.shard_map(local, mesh=mesh, in_specs=in_specs, out_specs=out_specs, check_vma=False)
```

profile of v0, /device:TPU:0, one launch (start us, length us, event | category | flops | bytes accessed | tf_op | source)
XLA Modules:
  0.0 58.5 jit_solution(5244514617831423014)
XLA Ops:
  0.6 3.1 %collective-permute-start = (bf16[64,1024]{1,0:T(8,128)(2,1)}, bf16[64,1024]{1,0:T(8,128)(2,1)S(1)}, u32[]{:S(2)}, u32[]{:S(2)}) collective-permute-start(bf16[64,1024]{1,0:T(8,128)(2,1)} %bitcast.12), channel_id=1, source_target_pairs={{0,4},{1,5},{2,6},{3,7},{4,0},{5,1},{6,2},{7,3},{8,12},{9,13},{10,... | collective-permute-start | bytes 393224 | tf_op jit(solution)/shard_map/ppermute | solution.py:24
  3.7 1.5 %collective-permute-start.3 = (bf16[1024,128]{1,0:T(8,128)(2,1)}, bf16[1024,128]{1,0:T(8,128)(2,1)S(1)}, u32[]{:S(2)}, u32[]{:S(2)}) collective-permute-start(bf16[1024,128]{1,0:T(8,128)(2,1)} %bitcast.8), channel_id=1, source_target_pairs={{0,1},{1,0},{2,3},{3,2},{4,5},{5,4},{6,7},{7,6},{8,9},{9,8},{10,11... | collective-permute-start | bytes 786440 | tf_op jit(solution)/shard_map/ppermute | solution.py:24
  5.2 1.5 %collective-permute-start.4 = (bf16[1024,128]{1,0:T(8,128)(2,1)}, bf16[1024,128]{1,0:T(8,128)(2,1)S(1)}, u32[]{:S(2)}, u32[]{:S(2)}) collective-permute-start(bf16[1024,128]{1,0:T(8,128)(2,1)} %bitcast.9), channel_id=1, source_target_pairs={{0,2},{1,3},{2,0},{3,1},{4,6},{5,7},{6,4},{7,5},{8,10},{9,11},{10,... | collective-permute-start | bytes 786440 | tf_op jit(solution)/shard_map/ppermute | solution.py:24
  6.8 0.5 collective-permute-start.5
  7.2 2.6 %collective-permute-start.1 = (bf16[64,1024]{1,0:T(8,128)(2,1)}, bf16[64,1024]{1,0:T(8,128)(2,1)S(1)}, u32[]{:S(2)}, u32[]{:S(2)}) collective-permute-start(bf16[64,1024]{1,0:T(8,128)(2,1)} %bitcast.13), channel_id=1, source_target_pairs={{0,8},{1,9},{2,10},{3,11},{4,12},{5,13},{6,14},{7,15},{8,0},{9,1},... | collective-permute-start | bytes 393224 | tf_op jit(solution)/shard_map/ppermute | solution.py:24
  9.8 0.0 collective-permute-done.refs_1_
  9.8 1.4 %collective-permute-start.2 = (bf16[64,1024]{1,0:T(8,128)(2,1)}, bf16[64,1024]{1,0:T(8,128)(2,1)S(1)}, u32[]{:S(2)}, u32[]{:S(2)}) collective-permute-start(bf16[64,1024]{1,0:T(8,128)(2,1)} %bitcast.14), channel_id=1, source_target_pairs={{0,12},{1,13},{2,14},{3,15},{4,8},{5,9},{6,10},{7,11},{8,4},{9,5},... | collective-permute-start | bytes 393224 | tf_op jit(solution)/shard_map/ppermute | solution.py:24
  11.2 7.3 %collective-permute-done.1.refs_2_ = bf16[64,1024]{1,0:T(8,128)(2,1)S(1)} collective-permute-done((bf16[64,1024]{1,0:T(8,128)(2,1)}, bf16[64,1024]{1,0:T(8,128)(2,1)S(1)}, u32[]{:S(2)}, u32[]{:S(2)}) %collective-permute-start.1) | collective-permute-done | bytes 131104 | tf_op jit(solution)/shard_map/ppermute | solution.py:24
  18.5 0.0 collective-permute-start.10
  18.5 0.0 collective-permute-done.2.refs_3_
  18.5 2.0 %collective-permute-start.11 = (bf16[1024,128]{1,0:T(8,128)(2,1)}, bf16[1024,128]{1,0:T(8,128)(2,1)S(1)}, u32[]{:S(2)}, u32[]{:S(2)}) collective-permute-start(bf16[1024,128]{1,0:T(8,128)(2,1)} %bitcast.refs_0_), channel_id=1, source_target_pairs={{16,2},{17,3},{18,0},{19,1},{20,6},{21,7},{22,4},{23,5},{24,10},{2... | collective-permute-start | bytes 786440 | tf_op jit(solution)/shard_map/ppermute | solution.py:42
  20.5 0.0 copy-start
  20.5 2.2 %copy-done = bf16[1,1,2,1024,1024]{4,3,2,1,0:T(8,128)(2,1)S(1)} copy-done((bf16[1,1,2,1024,1024]{4,3,2,1,0:T(8,128)(2,1)S(1)}, bf16[1,1,2,1024,1024]{4,3,2,1,0:T(8,128)(2,1)}, u32[]{:S(2)}) %copy-start) | copy-done | bytes 4194328
  22.7 0.0 copy-start.1
  22.7 0.9 %copy-done.1 = bf16[1,1,1024,128]{3,2,1,0:T(8,128)(2,1)S(1)} copy-done((bf16[1,1,1024,128]{3,2,1,0:T(8,128)(2,1)S(1)}, bf16[1,1,1024,128]{3,2,1,0:T(8,128)(2,1)}, u32[]{:S(2)}) %copy-start.1) | copy-done | bytes 262168
  23.7 0.0 copy-start.2
  23.7 0.9 %copy-done.2 = bf16[1,64,1024]{2,1,0:T(8,128)(2,1)S(1)} copy-done((bf16[1,64,1024]{2,1,0:T(8,128)(2,1)S(1)}, bf16[1,64,1024]{2,1,0:T(8,128)(2,1)}, u32[]{:S(2)}) %copy-start.2) | copy-done | bytes 131096
  24.6 1.0 %stage_inputs.1 = (bf16[1024,128]{1,0:T(8,128)(2,1)S(1)}, bf16[1024,128]{1,0:T(8,128)(2,1)S(1)}, bf16[2,1024,1024]{2,1,0:T(8,128)(2,1)S(1)}, bf16[64,1024]{1,0:T(8,128)(2,1)S(1)}) custom-call(bf16[1024,128]{1,0:T(8,128)(2,1)} %bitcast.refs_0_, bf16[1024,128]{1,0:T(8,128)(2,1)S(1)} %bitcast.11, bf16[2,1024,1024]{2,1,0:T(8,128)(2,1)S(1)} %bitcast.7, ...), custom_call_target="tpu_custom_call" | custom-call | bytes 9699328 | tf_op jit(solution)/shard_map/stage_inputs/pallas_call | solution.py:61
  25.6 0.0 collective-permute-done.3.refs_5_.refs_1_
  25.6 0.0 collective-permute-done.4.refs_6_.refs_2_
  25.6 0.0 collective-permute-done.5.refs_7_.refs_3_
  25.6 0.7 %rq_pieces.1 = (f32[256,128]{1,0:T(8,128)S(1)}, bf16[256,128]{1,0:T(8,128)(2,1)S(1)}, bf16[256,128]{1,0:T(8,128)(2,1)S(1)}, bf16[256,128]{1,0:T(8,128)(2,1)S(1)}) custom-call(bf16[64,1024]{1,0:T(8,128)(2,1)S(1)} %get-tuple-element.15.refs_0_, bf16[64,1024]{1,0:T(8,128)(2,1)S(1)} %collective-permute-done.refs_1_, ...), custom_call_target="tpu_custom_call" | custom-call | flops 268435456 | bytes 1572864 | tf_op jit(solution)/shard_map/rq_pieces/pallas_call | solution.py:87
  26.3 0.2 collective-permute-start.6
  26.5 2.0 %collective-permute-start.7 = (bf16[256,128]{1,0:T(8,128)(2,1)S(1)}, bf16[256,128]{1,0:T(8,128)(2,1)S(1)}, u32[]{:S(2)}, u32[]{:S(2)}) collective-permute-start(bf16[256,128]{1,0:T(8,128)(2,1)S(1)} %get-tuple-element.19), channel_id=1, source_target_pairs={{0,2},{1,3},{2,0},{3,1},{4,6},{5,7},{6,4},{7,5},{8,10},{9,11},{10,... | collective-permute-start | bytes 196616 | tf_op jit(solution)/shard_map/ppermute | solution.py:24
  28.4 1.4 %collective-permute-start.8 = (bf16[256,128]{1,0:T(8,128)(2,1)S(1)}, bf16[256,128]{1,0:T(8,128)(2,1)S(1)}, u32[]{:S(2)}, u32[]{:S(2)}) collective-permute-start(bf16[256,128]{1,0:T(8,128)(2,1)S(1)} %get-tuple-element.20), channel_id=1, source_target_pairs={{0,3},{1,2},{2,1},{3,0},{4,7},{5,6},{6,5},{7,4},{8,11},{9,10},{10,... | collective-permute-start | bytes 196616 | tf_op jit(solution)/shard_map/ppermute | solution.py:24
  29.9 0.8 %collective-permute-done.6.refs_3_ = bf16[256,128]{1,0:T(8,128)(2,1)S(1)} collective-permute-done((bf16[256,128]{1,0:T(8,128)(2,1)S(1)}, bf16[256,128]{1,0:T(8,128)(2,1)S(1)}, u32[]{:S(2)}, u32[]{:S(2)}) %collective-permute-start.6) | collective-permute-done | bytes 65568 | tf_op jit(solution)/shard_map/ppermute | solution.py:24
  30.6 0.0 collective-permute-start.12
  30.6 0.6 %collective-permute-done.7.refs_4_ = bf16[256,128]{1,0:T(8,128)(2,1)S(1)} collective-permute-done((bf16[256,128]{1,0:T(8,128)(2,1)S(1)}, bf16[256,128]{1,0:T(8,128)(2,1)S(1)}, u32[]{:S(2)}, u32[]{:S(2)}) %collective-permute-start.7) | collective-permute-done | bytes 65568 | tf_op jit(solution)/shard_map/ppermute | solution.py:24
  31.3 2.3 %collective-permute-done.8.refs_5_ = bf16[256,128]{1,0:T(8,128)(2,1)S(1)} collective-permute-done((bf16[256,128]{1,0:T(8,128)(2,1)S(1)}, bf16[256,128]{1,0:T(8,128)(2,1)S(1)}, u32[]{:S(2)}, u32[]{:S(2)}) %collective-permute-start.8) | collective-permute-done | bytes 65568 | tf_op jit(solution)/shard_map/ppermute | solution.py:24
  33.6 1.4 %advance.2 = bf16[1024,128]{1,0:T(8,128)(2,1)S(1)} custom-call(bf16[1024,128]{1,0:T(8,128)(2,1)S(1)} %get-tuple-element.14.refs_0_.refs_1_.refs_4_, bf16[1024,128]{1,0:T(8,128)(2,1)S(1)} %get-tuple-element.14.refs_0_.refs_1_.refs_4_, f32[256,128]{1,0:T(8,128)S(1)} %get-tuple-element.17.refs_2_, bf16[256,128]{1,0:T(8,128)(2,1)S(1)} %collective-permute-done.6.refs_3_, ...), custom_call_target="tpu_custom_call" | custom-call | flops 536870912 | bytes 4194304 | tf_op jit(solution)/shard_map/advance/pallas_call | solution.py:124
  35.0 0.1 collective-permute-start.9
  35.1 1.6 %collective-permute-start.13 = (bf16[1024,128]{1,0:T(8,128)(2,1)S(1)}, bf16[1024,128]{1,0:T(8,128)(2,1)S(1)}, u32[]{:S(2)}, u32[]{:S(2)}) collective-permute-start(bf16[1024,128]{1,0:T(8,128)(2,1)S(1)} %advance.2), channel_id=1, source_target_pairs={{0,17},{1,16},{2,19},{3,18},{4,21},{5,20},{6,23},{7,22},{8,25},{9,... | collective-permute-start | bytes 786440 | tf_op jit(solution)/shard_map/ppermute | solution.py:34
  36.6 0.0 collective-permute-done.10.refs_5_
  36.7 0.0 collective-permute-start.14
  36.7 0.0 collective-permute-done.11.refs_6_
  36.7 0.7 %collective-permute-start.15 = (bf16[1024,128]{1,0:T(8,128)(2,1)S(1)}, bf16[1024,128]{1,0:T(8,128)(2,1)S(1)}, u32[]{:S(2)}, u32[]{:S(2)}) collective-permute-start(bf16[1024,128]{1,0:T(8,128)(2,1)S(1)} %advance.2), channel_id=1, source_target_pairs={{0,19},{1,18},{2,17},{3,16},{4,23},{5,22},{6,21},{7,20},{8,27},{9,... | collective-permute-start | bytes 786440 | tf_op jit(solution)/shard_map/ppermute | solution.py:34
  37.4 0.1 collective-permute-done.12.refs_7_
  37.5 0.0 collective-permute-done.9.refs_1_.refs_8_
  37.5 3.0 %collective-permute-done.13.refs_9_ = bf16[1024,128]{1,0:T(8,128)(2,1)S(1)} collective-permute-done((bf16[1024,128]{1,0:T(8,128)(2,1)S(1)}, bf16[1024,128]{1,0:T(8,128)(2,1)S(1)}, u32[]{:S(2)}, u32[]{:S(2)}) %collective-permute-start.13) | collective-permute-done | bytes 262176 | tf_op jit(solution)/shard_map/ppermute | solution.py:34
  40.5 0.0 collective-permute-done.14.refs_10_
  40.5 2.8 %collective-permute-done.15.refs_11_ = bf16[1024,128]{1,0:T(8,128)(2,1)S(1)} collective-permute-done((bf16[1024,128]{1,0:T(8,128)(2,1)S(1)}, bf16[1024,128]{1,0:T(8,128)(2,1)S(1)}, u32[]{:S(2)}, u32[]{:S(2)}) %collective-permute-start.15) | collective-permute-done | bytes 262176 | tf_op jit(solution)/shard_map/ppermute | solution.py:34
  43.4 0.5 picture_parts.1
  43.8 2.8 %collective-permute-start.18 = (bf16[64,1024]{1,0:T(8,128)(2,1)S(1)}, bf16[64,1024]{1,0:T(8,128)(2,1)S(1)}, u32[]{:S(2)}, u32[]{:S(2)}) collective-permute-start(bf16[64,1024]{1,0:T(8,128)(2,1)S(1)} %get-tuple-element.25), channel_id=1, source_target_pairs={{0,12},{1,13},{2,14},{3,15},{4,8},{5,9},{6,10},{7,11},{8,4},{9,5},... | collective-permute-start | bytes 393224 | tf_op jit(solution)/shard_map/ppermute | solution.py:24
  46.7 0.0 collective-permute-start.17
  46.7 1.6 %collective-permute-start.16 = (bf16[64,1024]{1,0:T(8,128)(2,1)S(1)}, bf16[64,1024]{1,0:T(8,128)(2,1)S(1)}, u32[]{:S(2)}, u32[]{:S(2)}) collective-permute-start(bf16[64,1024]{1,0:T(8,128)(2,1)S(1)} %get-tuple-element.23), channel_id=1, source_target_pairs={{0,4},{1,5},{2,6},{3,7},{4,0},{5,1},{6,2},{7,3},{8,12},{9,13},{10,... | collective-permute-start | bytes 393224 | tf_op jit(solution)/shard_map/ppermute | solution.py:24
  48.3 2.1 %advance.3 = bf16[1024,128]{1,0:T(8,128)(2,1)} custom-call(bf16[1024,128]{1,0:T(8,128)(2,1)S(1)} %get-tuple-element.14.refs_0_.refs_1_.refs_4_, bf16[1024,128]{1,0:T(8,128)(2,1)S(1)} %collective-permute-done.9.refs_1_.refs_8_, f32[256,128]{1,0:T(8,128)S(1)} %get-tuple-element.17.refs_2_, bf16[256,128]{1,0:T(8,128)(2,1)S(1)} %collective-permute-done.6.refs_3_, ...), custom_call_target="tpu_custom_call" | custom-call | flops 536870912 | bytes 4194304 | tf_op jit(solution)/shard_map/advance/pallas_call | solution.py:124
  50.4 1.8 %collective-permute-done.18 = bf16[64,1024]{1,0:T(8,128)(2,1)S(1)} collective-permute-done((bf16[64,1024]{1,0:T(8,128)(2,1)S(1)}, bf16[64,1024]{1,0:T(8,128)(2,1)S(1)}, u32[]{:S(2)}, u32[]{:S(2)}) %collective-permute-start.18) | collective-permute-done | bytes 131104 | tf_op jit(solution)/shard_map/ppermute | solution.py:24
  52.2 5.6 %collective-permute-done.17 = bf16[64,1024]{1,0:T(8,128)(2,1)S(1)} collective-permute-done((bf16[64,1024]{1,0:T(8,128)(2,1)S(1)}, bf16[64,1024]{1,0:T(8,128)(2,1)S(1)}, u32[]{:S(2)}, u32[]{:S(2)}) %collective-permute-start.17) | collective-permute-done | bytes 131104 | tf_op jit(solution)/shard_map/ppermute | solution.py:24
  57.8 0.0 collective-permute-done.16
  57.8 0.8 %multiply_bitcast_fusion = f32[1,64,1024]{2,1,0:T(8,128)} fusion(bf16[64,1024]{1,0:T(8,128)(2,1)S(1)} %collective-permute-done.18, bf16[64,1024]{1,0:T(8,128)(2,1)S(1)} %collective-permute-done.17, f32[64,1024]{1,0:T(8,128)S(1)} %get-tuple-element.22, bf16[64,1024]{1,0:T(8,128)(2,1)S(1)} %collective-permute-done.16), kind=kLoop, calls=%fused_computation | loop fusion | flops 458752 | bytes 917504 | tf_op jit(solution)/shard_map/broadcast_in_dim | solution.py:205
Async XLA Ops:
  0.6 9.2 %collective-permute-start = (bf16[64,1024]{1,0:T(8,128)(2,1)}, bf16[64,1024]{1,0:T(8,128)(2,1)S(1)}, u32[]{:S(2)}, u32[]{:S(2)}) collective-permute-start(bf16[64,1024]{1,0:T(8,128)(2,1)} %bitcast.12), channel_id=1, source_target_pairs={{0,4},{1,5},{2,6},{3,7},{4,0},{5,1},{6,2},{7,3},{8,12},{9,13},{10,... | collective-permute-start | bytes 393224 | tf_op jit(solution)/shard_map/ppermute | solution.py:24
  3.7 21.8 %collective-permute-start.3 = (bf16[1024,128]{1,0:T(8,128)(2,1)}, bf16[1024,128]{1,0:T(8,128)(2,1)S(1)}, u32[]{:S(2)}, u32[]{:S(2)}) collective-permute-start(bf16[1024,128]{1,0:T(8,128)(2,1)} %bitcast.8), channel_id=1, source_target_pairs={{0,1},{1,0},{2,3},{3,2},{4,5},{5,4},{6,7},{7,6},{8,9},{9,8},{10,11... | collective-permute-start | bytes 786440 | tf_op jit(solution)/shard_map/ppermute | solution.py:24
  5.2 20.3 %collective-permute-start.4 = (bf16[1024,128]{1,0:T(8,128)(2,1)}, bf16[1024,128]{1,0:T(8,128)(2,1)S(1)}, u32[]{:S(2)}, u32[]{:S(2)}) collective-permute-start(bf16[1024,128]{1,0:T(8,128)(2,1)} %bitcast.9), channel_id=1, source_target_pairs={{0,2},{1,3},{2,0},{3,1},{4,6},{5,7},{6,4},{7,5},{8,10},{9,11},{10,... | collective-permute-start | bytes 786440 | tf_op jit(solution)/shard_map/ppermute | solution.py:24
  6.8 18.8 %collective-permute-start.5 = (bf16[1024,128]{1,0:T(8,128)(2,1)}, bf16[1024,128]{1,0:T(8,128)(2,1)S(1)}, u32[]{:S(2)}, u32[]{:S(2)}) collective-permute-start(bf16[1024,128]{1,0:T(8,128)(2,1)} %bitcast.10), channel_id=1, source_target_pairs={{0,3},{1,2},{2,1},{3,0},{4,7},{5,6},{6,5},{7,4},{8,11},{9,10},{10,... | collective-permute-start | bytes 786440 | tf_op jit(solution)/shard_map/ppermute | solution.py:24
  7.2 11.2 %collective-permute-start.1 = (bf16[64,1024]{1,0:T(8,128)(2,1)}, bf16[64,1024]{1,0:T(8,128)(2,1)S(1)}, u32[]{:S(2)}, u32[]{:S(2)}) collective-permute-start(bf16[64,1024]{1,0:T(8,128)(2,1)} %bitcast.13), channel_id=1, source_target_pairs={{0,8},{1,9},{2,10},{3,11},{4,12},{5,13},{6,14},{7,15},{8,0},{9,1},... | collective-permute-start | bytes 393224 | tf_op jit(solution)/shard_map/ppermute | solution.py:24
  9.8 8.7 %collective-permute-start.2 = (bf16[64,1024]{1,0:T(8,128)(2,1)}, bf16[64,1024]{1,0:T(8,128)(2,1)S(1)}, u32[]{:S(2)}, u32[]{:S(2)}) collective-permute-start(bf16[64,1024]{1,0:T(8,128)(2,1)} %bitcast.14), channel_id=1, source_target_pairs={{0,12},{1,13},{2,14},{3,15},{4,8},{5,9},{6,10},{7,11},{8,4},{9,5},... | collective-permute-start | bytes 393224 | tf_op jit(solution)/shard_map/ppermute | solution.py:24
  18.5 18.2 %collective-permute-start.10 = (bf16[1024,128]{1,0:T(8,128)(2,1)}, bf16[1024,128]{1,0:T(8,128)(2,1)S(1)}, u32[]{:S(2)}, u32[]{:S(2)}) collective-permute-start(bf16[1024,128]{1,0:T(8,128)(2,1)} %bitcast.refs_0_), channel_id=1, source_target_pairs={{16,1},{17,0},{18,3},{19,2},{20,5},{21,4},{22,7},{23,6},{24,9},{25... | collective-permute-start | bytes 786440 | tf_op jit(solution)/shard_map/ppermute | solution.py:42
  18.5 18.2 %collective-permute-start.11 = (bf16[1024,128]{1,0:T(8,128)(2,1)}, bf16[1024,128]{1,0:T(8,128)(2,1)S(1)}, u32[]{:S(2)}, u32[]{:S(2)}) collective-permute-start(bf16[1024,128]{1,0:T(8,128)(2,1)} %bitcast.refs_0_), channel_id=1, source_target_pairs={{16,2},{17,3},{18,0},{19,1},{20,6},{21,7},{22,4},{23,5},{24,10},{2... | collective-permute-start | bytes 786440 | tf_op jit(solution)/shard_map/ppermute | solution.py:42
  20.5 2.2 %copy-start = (bf16[1,1,2,1024,1024]{4,3,2,1,0:T(8,128)(2,1)S(1)}, bf16[1,1,2,1024,1024]{4,3,2,1,0:T(8,128)(2,1)}, u32[]{:S(2)}) copy-start(bf16[1,1,2,1024,1024]{4,3,2,1,0:T(8,128)(2,1)} %param.6) | copy-start | bytes 12582916
  22.7 0.9 %copy-start.1 = (bf16[1,1,1024,128]{3,2,1,0:T(8,128)(2,1)S(1)}, bf16[1,1,1024,128]{3,2,1,0:T(8,128)(2,1)}, u32[]{:S(2)}) copy-start(bf16[1,1,1024,128]{3,2,1,0:T(8,128)(2,1)} %param.5) | copy-start | bytes 786436
  23.7 0.9 %copy-start.2 = (bf16[1,64,1024]{2,1,0:T(8,128)(2,1)S(1)}, bf16[1,64,1024]{2,1,0:T(8,128)(2,1)}, u32[]{:S(2)}) copy-start(bf16[1,64,1024]{2,1,0:T(8,128)(2,1)} %param.7) | copy-start | bytes 393220
  26.3 4.3 %collective-permute-start.6 = (bf16[256,128]{1,0:T(8,128)(2,1)S(1)}, bf16[256,128]{1,0:T(8,128)(2,1)S(1)}, u32[]{:S(2)}, u32[]{:S(2)}) collective-permute-start(bf16[256,128]{1,0:T(8,128)(2,1)S(1)} %get-tuple-element.18), channel_id=1, source_target_pairs={{0,1},{1,0},{2,3},{3,2},{4,5},{5,4},{6,7},{7,6},{8,9},{9,8},{10,11... | collective-permute-start | bytes 196616 | tf_op jit(solution)/shard_map/ppermute | solution.py:24
  26.5 4.8 %collective-permute-start.7 = (bf16[256,128]{1,0:T(8,128)(2,1)S(1)}, bf16[256,128]{1,0:T(8,128)(2,1)S(1)}, u32[]{:S(2)}, u32[]{:S(2)}) collective-permute-start(bf16[256,128]{1,0:T(8,128)(2,1)S(1)} %get-tuple-element.19), channel_id=1, source_target_pairs={{0,2},{1,3},{2,0},{3,1},{4,6},{5,7},{6,4},{7,5},{8,10},{9,11},{10,... | collective-permute-start | bytes 196616 | tf_op jit(solution)/shard_map/ppermute | solution.py:24
  28.4 5.2 %collective-permute-start.8 = (bf16[256,128]{1,0:T(8,128)(2,1)S(1)}, bf16[256,128]{1,0:T(8,128)(2,1)S(1)}, u32[]{:S(2)}, u32[]{:S(2)}) collective-permute-start(bf16[256,128]{1,0:T(8,128)(2,1)S(1)} %get-tuple-element.20), channel_id=1, source_target_pairs={{0,3},{1,2},{2,1},{3,0},{4,7},{5,6},{6,5},{7,4},{8,11},{9,10},{10,... | collective-permute-start | bytes 196616 | tf_op jit(solution)/shard_map/ppermute | solution.py:24
  30.6 6.9 %collective-permute-start.12 = (bf16[1024,128]{1,0:T(8,128)(2,1)}, bf16[1024,128]{1,0:T(8,128)(2,1)S(1)}, u32[]{:S(2)}, u32[]{:S(2)}) collective-permute-start(bf16[1024,128]{1,0:T(8,128)(2,1)} %bitcast.refs_0_), channel_id=1, source_target_pairs={{16,3},{17,2},{18,1},{19,0},{20,7},{21,6},{22,5},{23,4},{24,11},{2... | collective-permute-start | bytes 786440 | tf_op jit(solution)/shard_map/ppermute | solution.py:42
  35.0 2.6 %collective-permute-start.9 = (bf16[1024,128]{1,0:T(8,128)(2,1)S(1)}, bf16[1024,128]{1,0:T(8,128)(2,1)S(1)}, u32[]{:S(2)}, u32[]{:S(2)}) collective-permute-start(bf16[1024,128]{1,0:T(8,128)(2,1)S(1)} %advance.2), channel_id=1, source_target_pairs={{0,16},{1,17},{2,18},{3,19},{4,20},{5,21},{6,22},{7,23},{8,24},{9,... | collective-permute-start | bytes 786440 | tf_op jit(solution)/shard_map/ppermute | solution.py:34
  35.1 5.5 %collective-permute-start.13 = (bf16[1024,128]{1,0:T(8,128)(2,1)S(1)}, bf16[1024,128]{1,0:T(8,128)(2,1)S(1)}, u32[]{:S(2)}, u32[]{:S(2)}) collective-permute-start(bf16[1024,128]{1,0:T(8,128)(2,1)S(1)} %advance.2), channel_id=1, source_target_pairs={{0,17},{1,16},{2,19},{3,18},{4,21},{5,20},{6,23},{7,22},{8,25},{9,... | collective-permute-start | bytes 786440 | tf_op jit(solution)/shard_map/ppermute | solution.py:34
  36.7 3.9 %collective-permute-start.14 = (bf16[1024,128]{1,0:T(8,128)(2,1)S(1)}, bf16[1024,128]{1,0:T(8,128)(2,1)S(1)}, u32[]{:S(2)}, u32[]{:S(2)}) collective-permute-start(bf16[1024,128]{1,0:T(8,128)(2,1)S(1)} %advance.2), channel_id=1, source_target_pairs={{0,18},{1,19},{2,16},{3,17},{4,22},{5,23},{6,20},{7,21},{8,26},{9,... | collective-permute-start | bytes 786440 | tf_op jit(solution)/shard_map/ppermute | solution.py:34
  36.7 6.7 %collective-permute-start.15 = (bf16[1024,128]{1,0:T(8,128)(2,1)S(1)}, bf16[1024,128]{1,0:T(8,128)(2,1)S(1)}, u32[]{:S(2)}, u32[]{:S(2)}) collective-permute-start(bf16[1024,128]{1,0:T(8,128)(2,1)S(1)} %advance.2), channel_id=1, source_target_pairs={{0,19},{1,18},{2,17},{3,16},{4,23},{5,22},{6,21},{7,20},{8,27},{9,... | collective-permute-start | bytes 786440 | tf_op jit(solution)/shard_map/ppermute | solution.py:34
  43.8 8.4 %collective-permute-start.18 = (bf16[64,1024]{1,0:T(8,128)(2,1)S(1)}, bf16[64,1024]{1,0:T(8,128)(2,1)S(1)}, u32[]{:S(2)}, u32[]{:S(2)}) collective-permute-start(bf16[64,1024]{1,0:T(8,128)(2,1)S(1)} %get-tuple-element.25), channel_id=1, source_target_pairs={{0,12},{1,13},{2,14},{3,15},{4,8},{5,9},{6,10},{7,11},{8,4},{9,5},... | collective-permute-start | bytes 393224 | tf_op jit(solution)/shard_map/ppermute | solution.py:24
  46.7 11.1 %collective-permute-start.17 = (bf16[64,1024]{1,0:T(8,128)(2,1)S(1)}, bf16[64,1024]{1,0:T(8,128)(2,1)S(1)}, u32[]{:S(2)}, u32[]{:S(2)}) collective-permute-start(bf16[64,1024]{1,0:T(8,128)(2,1)S(1)} %get-tuple-element.24), channel_id=1, source_target_pairs={{0,8},{1,9},{2,10},{3,11},{4,12},{5,13},{6,14},{7,15},{8,0},{9,1},... | collective-permute-start | bytes 393224 | tf_op jit(solution)/shard_map/ppermute | solution.py:24
  46.7 11.1 %collective-permute-start.16 = (bf16[64,1024]{1,0:T(8,128)(2,1)S(1)}, bf16[64,1024]{1,0:T(8,128)(2,1)S(1)}, u32[]{:S(2)}, u32[]{:S(2)}) collective-permute-start(bf16[64,1024]{1,0:T(8,128)(2,1)S(1)} %get-tuple-element.23), channel_id=1, source_target_pairs={{0,4},{1,5},{2,6},{3,7},{4,0},{5,1},{6,2},{7,3},{8,12},{9,13},{10,... | collective-permute-start | bytes 393224 | tf_op jit(solution)/shard_map/ppermute | solution.py:24
where the time goes:
time: 59.4 us; the launch traced here: 58.5 us
  waiting for transfers between devices  24.3 us (41%)
  starting transfers between devices  23 us (39%)
  Pallas kernels  5.64 us (9%)
  local copies, waits for them, and re-layouts  4.04 us (7%)
  other arithmetic  0.77 us (1%)
  between operations  0.71 us (1%)
    ppermute x12, starting transfers between devices, swap(): return lax.ppermute(value, 'freq', [(i, i ^ by) for i in range(devices)])  18.6 us
    ppermute x12, waiting for transfers between devices, swap(): return lax.ppermute(value, 'freq', [(i, i ^ by) for i in range(devices)])  18.4 us
    ppermute x4, waiting for transfers between devices, lower(): return lax.ppermute(value, ('depth', 'freq'), pairs)  5.81 us
    unnamed x6, local copies, waits for them, and re-layouts  4.04 us
    pallas_call x2, Pallas kernels, advance(): pl.pallas_call(functools.partial(advance_kernel, line, plane), out_shape=...  3.47 us
    ppermute x4, starting transfers between devices, lower(): return lax.ppermute(value, ('depth', 'freq'), pairs)  2.42 us
    ppermute x3, starting transfers between devices, raise_top(): return lax.ppermute(value, ('depth', 'freq'), pairs)  2.04 us
  transfers between devices with their start and end apart: 19, of which 9 were waited for; matrix products, arithmetic and copies ran while one was open for 0% of the time, Pallas kernels for 9%

commit v1 on v0

--- a/solution.py
+++ b/solution.py
@@ -10,6 +10,7 @@
 
 VMEM = pl.BlockSpec(memory_space=pltpu.VMEM)
 MIB = 1 << 20
+STAGE_LIMIT = 44 * MIB
 
 
 def plane_size(devices):
@@ -42,32 +43,55 @@
     return lax.ppermute(value, ("depth", "freq"), pairs)
 
 
+def reduce_step(value, k, plane, line):
+    levels, devices = lax.axis_size("depth"), lax.axis_size("freq")
+    pairs = []
+    for d in range(levels):
+        if k < (line if d else plane):
+            by = k * plane if d else k
+            pairs += [(d * devices + i, d * devices + (i ^ by)) for i in range(devices)]
+    return lax.ppermute(value, ("depth", "freq"), pairs)
+
+
 def params(limit):
     return pltpu.CompilerParams(vmem_limit_bytes=limit)
 
 
-def stage_kernel(count, *refs):
-    sources, targets, sems = refs[:count], refs[count : 2 * count], refs[2 * count]
-    copies = [pltpu.make_async_copy(a, b, sems.at[k]) for k, (a, b) in enumerate(zip(sources, targets))]
+def stage_kernel(count, plane, line, *refs):
+    sources, other = refs[:count], refs[count]
+    targets, loads = refs[count + 1 : 2 * count + 1], refs[2 * count + 1 : -1]
+    sems = refs[-1]
+    copies = list(zip(sources, targets))
+    at_plane = lax.axis_index("freq") // plane
+    nx = other.shape[0]
+    tall = nx // line
+    for z, load in enumerate(loads, 1):
+        rows = pl.ds(pl.multiple_of((at_plane ^ z) * tall, tall), tall)
+        copies += [(sources[0], load.at[pl.ds(0, nx)]), (other.at[rows], load.at[pl.ds(nx, tall)])]
+    copies = [pltpu.make_async_copy(a, b, sems.at[k]) for k, (a, b) in enumerate(copies)]
     for copy in copies:
         copy.start()
     for copy in copies:
         copy.wait()
 
 
-def stage(*arrays):
+def stage(arrays, other, plane, line):
     count = len(arrays)
+    nx, cols = other.shape
     size = sum(a.size * a.dtype.itemsize for a in arrays)
-    return pl.pallas_call(
-        functools.partial(stage_kernel, count),
-        out_shape=[jax.ShapeDtypeStruct(a.shape, a.dtype) for a in arrays],
-        in_specs=[pl.BlockSpec(memory_space=pltpu.HBM)] * count,
-        out_specs=[VMEM] * count,
-        scratch_shapes=[pltpu.SemaphoreType.DMA((count,))],
-        compiler_params=params(16 * MIB),
+    out_shape = [jax.ShapeDtypeStruct(a.shape, a.dtype) for a in arrays]
+    out_shape += [jax.ShapeDtypeStruct((nx + nx // line, cols), other.dtype)] * (line - 1)
+    outs = pl.pallas_call(
+        functools.partial(stage_kernel, count, plane, line),
+        out_shape=out_shape,
+        in_specs=[pl.BlockSpec(memory_space=pl.ANY)] * (count + 1),
+        out_specs=[VMEM] * len(out_shape),
+        scratch_shapes=[pltpu.SemaphoreType.DMA((count + 2 * (line - 1),))],
+        compiler_params=params(STAGE_LIMIT),
         cost_estimate=pl.CostEstimate(flops=0, bytes_accessed=2 * size, transcendentals=0),
         name="stage_inputs",
-    )(*arrays)
+    )(*arrays, other)
+    return outs[:count], outs[count:]
 
 
 def pieces_kernel(line, plane, *refs):
@@ -133,44 +157,61 @@
     )(top, moved, *pieces, weights)
 
 
+def side_by_side(parts):
+    return jnp.concatenate(parts, axis=1)
+
+
+def stacked_rows(ref, starts, rows):
+    return jnp.concatenate([ref[pl.ds(pl.multiple_of(s, rows), rows), :] for s in starts], axis=0)
+
+
 def picture_kernel(line, plane, *refs):
-    ups, tops, fields, outs = refs[:plane], refs[plane : 2 * plane], refs[2 * plane : 3 * plane], refs[3 * plane :]
+    ups, fields, refs = refs[:plane], refs[plane : 2 * plane], refs[2 * plane :]
+    top, loads, outs = refs[0], refs[1:line], refs[line:]
     me = lax.axis_index("freq")
     first = lax.axis_index("depth") == 0
+    nx = top.shape[0]
     rows = outs[0].shape[0]
-    left = jnp.concatenate(
-        [
-            jnp.concatenate(
-                [up[pl.ds(pl.multiple_of((me ^ (z * plane)) * rows, rows), rows), :] for z in range(line)],
-                axis=0,
-            )
-            for up in ups
-        ],
-        axis=1,
-    )
-    right = jnp.concatenate([jnp.where(first, t[...], f[...]) for t, f in zip(tops, fields)], axis=1)
-    total = lax.dot_general(left, right, (((1,), (1,)), ((), ())), preferred_element_type=jnp.float32)
-    for z, out in enumerate(outs):
-        out[...] = total[z * rows : (z + 1) * rows].astype(out.dtype)
-
-
-def picture_parts(ups, tops, fields, line):
-    plane = len(ups)
-    nx, cols = ups[0].shape
+
+    def write(left, right, count):
+        total = lax.dot_general(left, right, (((1,), (1,)), ((), ())), preferred_element_type=jnp.float32)
+        for k, out in enumerate(outs):
+            if k < count:
+                out[...] = total[k * rows : (k + 1) * rows].astype(out.dtype)
+
+    @pl.when(first)
+    def _():
+        inner = me % plane
+        starts = [(me ^ q) * rows for q in range(plane)]
+        lefts = [stacked_rows(ups[0], starts, rows)]
+        lefts += [stacked_rows(load, [nx + (inner ^ q) * rows for q in range(plane)], rows) for load in loads]
+        rights = [top[...]] + [load[:nx, :] for load in loads]
+        write(side_by_side(lefts), side_by_side(rights), plane)
+
+    @pl.when(jnp.logical_not(first))
+    def _():
+        starts = [(me ^ (z * plane)) * rows for z in range(line)]
+        lefts = [stacked_rows(up, starts, rows) for up in ups]
+        write(side_by_side(lefts), side_by_side([f[...] for f in fields]), line)
+
+
+def picture_parts(ups, fields, top, loads, plane, line):
+    nx, cols = top.shape
     rows = nx // (line * plane)
+    count = max(line, plane)
     out_shape = [jax.ShapeDtypeStruct((rows, nx), jnp.float32)]
-    out_shape += [jax.ShapeDtypeStruct((rows, nx), jnp.bfloat16)] * (line - 1)
+    out_shape += [jax.ShapeDtypeStruct((rows, nx), jnp.bfloat16)] * (count - 1)
     return pl.pallas_call(
         functools.partial(picture_kernel, line, plane),
         out_shape=out_shape,
-        in_specs=[VMEM] * (3 * plane),
-        out_specs=[VMEM] * line,
+        in_specs=[VMEM] * (2 * plane + line),
+        out_specs=[VMEM] * count,
         compiler_params=params(24 * MIB),
         cost_estimate=pl.CostEstimate(
             flops=2 * line * rows * nx * cols * plane, bytes_accessed=4 * nx * cols * plane, transcendentals=0
         ),
         name="picture_parts",
-    )(*ups, *tops, *fields)
+    )(*ups, *fields, top, *loads)
 
 
 def local(p_top, upgoing, extrapolator, reflectivity):
@@ -183,11 +224,12 @@
     plane = plane_size(devices)
     line = devices // plane
 
+    other = lower(upper, 0)
     blocks = [swap(own_rows, z * plane) for z in range(1, line)]
     ups = [swap(upper, q) for q in range(1, plane)]
-    tops = [raise_top(top, q) for q in range(1, plane)]
-    top, upper, weights, own_rows = stage(top, upper, weights, own_rows)
-    blocks, ups, tops = [own_rows] + blocks, [upper] + ups, [top] + tops
+    (top, upper, weights, own_rows), loads = stage((top, upper, weights, own_rows), other, plane, line)
+    loads = [raise_top(load, z * plane) for z, load in enumerate(loads, 1)]
+    blocks, ups = [own_rows] + blocks, [upper] + ups
     pieces = rq_pieces(blocks, ups)
     pieces = [pieces[0]] + [swap(pieces[q], q) for q in range(1, plane)]
 
@@ -196,10 +238,10 @@
         below = advance(top, moved, pieces, weights, line, plane)
         moved = lower(below, 0)
     fields = [moved] + [lower(below, q) for q in range(1, plane)]
-    parts = picture_parts(ups, tops, fields, line)
+    parts = picture_parts(ups, fields, top, loads, plane, line)
     total = parts[0]
-    for z in range(1, line):
-        total = total + swap(parts[z], z * plane).astype(jnp.float32)
+    for k in range(1, len(parts)):
+        total = total + reduce_step(parts[k], k, plane, line).astype(jnp.float32)
     scale = (float(upper.shape[1]) * devices) ** (-0.5)
     below = advance(top, moved, pieces, weights, line, plane)
     return (below[None, None], (total * scale)[None])

time: 59.4 us -> 59 us (level); the launches traced: 58.5 us -> 58.8 us
  starting transfers between devices: 23 us -> 25.7 us
  waiting for transfers between devices: 24.3 us -> 21.8 us
  Pallas kernels: 5.64 us -> 6.97 us
  local copies, waits for them, and re-layouts: 4.04 us -> 2.8 us
    ppermute x12 -> x9, waiting for transfers between devices: 18.4 us -> 9.24 us  [swap(): return lax.ppermute(value, 'freq', [(i, i ^ by) for i in range(devices)])]
    ppermute x12 -> x9, starting transfers between devices: 18.6 us -> 13.8 us  [swap(): return lax.ppermute(value, 'freq', [(i, i ^ by) for i in range(devices)])]
    ppermute x3, waiting for transfers between devices: 0.14 us -> 4.54 us  [raise_top(): return lax.ppermute(value, ('depth', 'freq'), pairs)]
    ppermute x0 -> x3, starting transfers between devices: none -> 3.55 us  [reduce_step(): return lax.ppermute(value, ('depth', 'freq'), pairs)]
    ppermute x3, starting transfers between devices: 2.04 us -> 4.39 us  [raise_top(): return lax.ppermute(value, ('depth', 'freq'), pairs)]
    ppermute x0 -> x3, waiting for transfers between devices: none -> 2.34 us  [reduce_step(): return lax.ppermute(value, ('depth', 'freq'), pairs)]
    ppermute x4 -> x5, starting transfers between devices: 2.42 us -> 3.94 us  [lower(): return lax.ppermute(value, ('depth', 'freq'), pairs)]
    pallas_call x1, Pallas kernels: 0.99 us -> 2.32 us  [stage(): pl.pallas_call(functools.partial(stage_kernel, count, plane, line), out_s...]
  transfers between devices with their start and end apart: 19 -> 20, of which waited for: 9 -> 10; matrix products, arithmetic and copies ran while one was open for 0% -> 0% of each run, Pallas kernels for 9% -> 8%
where the time goes in v1:
time: 59 us; the launch traced here: 58.8 us
  starting transfers between devices  25.7 us (44%)
  waiting for transfers between devices  21.8 us (37%)
  Pallas kernels  6.97 us (12%)
  local copies, waits for them, and re-layouts  2.8 us (5%)
  other arithmetic  0.77 us (1%)
  between operations  0.7 us (1%)
    ppermute x9, starting transfers between devices, swap(): return lax.ppermute(value, 'freq', [(i, i ^ by) for i in range(devices)])  13.8 us
    ppermute x9, waiting for transfers between devices, swap(): return lax.ppermute(value, 'freq', [(i, i ^ by) for i in range(devices)])  9.24 us
    ppermute x5, waiting for transfers between devices, lower(): return lax.ppermute(value, ('depth', 'freq'), pairs)  5.72 us
    ppermute x3, waiting for transfers between devices, raise_top(): return lax.ppermute(value, ('depth', 'freq'), pairs)  4.54 us
    ppermute x3, starting transfers between devices, raise_top(): return lax.ppermute(value, ('depth', 'freq'), pairs)  4.39 us
    ppermute x5, starting transfers between devices, lower(): return lax.ppermute(value, ('depth', 'freq'), pairs)  3.94 us
    ppermute x3, starting transfers between devices, reduce_step(): return lax.ppermute(value, ('depth', 'freq'), pairs)  3.55 us
    pallas_call x2, Pallas kernels, advance(): pl.pallas_call(functools.partial(advance_kernel, line, plane), out_shape=...  3.47 us
  transfers between devices with their start and end apart: 20, of which 10 were waited for; matrix products, arithmetic and copies ran while one was open for 0% of the time, Pallas kernels for 8%

profile of v1, /device:TPU:0, one launch (start us, length us, event | category | flops | bytes accessed | tf_op | source)
XLA Modules:
  0.0 58.8 jit_solution(993086204240375758)
XLA Ops:
  0.6 0.6 collective-permute-start
  1.2 2.6 %collective-permute-start.1 = (bf16[64,1024]{1,0:T(8,128)(2,1)}, bf16[64,1024]{1,0:T(8,128)(2,1)S(1)}, u32[]{:S(2)}, u32[]{:S(2)}) collective-permute-start(bf16[64,1024]{1,0:T(8,128)(2,1)} %bitcast.13), channel_id=1, source_target_pairs={{0,4},{1,5},{2,6},{3,7},{4,0},{5,1},{6,2},{7,3},{8,12},{9,13},{10,... | collective-permute-start | bytes 393224 | tf_op jit(solution)/shard_map/ppermute | solution.py:25
  3.8 1.5 %collective-permute-start.4 = (bf16[1024,128]{1,0:T(8,128)(2,1)}, bf16[1024,128]{1,0:T(8,128)(2,1)S(1)}, u32[]{:S(2)}, u32[]{:S(2)}) collective-permute-start(bf16[1024,128]{1,0:T(8,128)(2,1)} %bitcast.9), channel_id=1, source_target_pairs={{0,1},{1,0},{2,3},{3,2},{4,5},{5,4},{6,7},{7,6},{8,9},{9,8},{10,11... | collective-permute-start | bytes 786440 | tf_op jit(solution)/shard_map/ppermute | solution.py:25
  5.3 1.5 %collective-permute-start.5 = (bf16[1024,128]{1,0:T(8,128)(2,1)}, bf16[1024,128]{1,0:T(8,128)(2,1)S(1)}, u32[]{:S(2)}, u32[]{:S(2)}) collective-permute-start(bf16[1024,128]{1,0:T(8,128)(2,1)} %bitcast.10), channel_id=1, source_target_pairs={{0,2},{1,3},{2,0},{3,1},{4,6},{5,7},{6,4},{7,5},{8,10},{9,11},{10,... | collective-permute-start | bytes 786440 | tf_op jit(solution)/shard_map/ppermute | solution.py:25
  6.8 0.5 collective-permute-start.6
  7.3 0.8 %collective-permute-done.1.refs_1_ = bf16[64,1024]{1,0:T(8,128)(2,1)S(1)} collective-permute-done((bf16[64,1024]{1,0:T(8,128)(2,1)}, bf16[64,1024]{1,0:T(8,128)(2,1)S(1)}, u32[]{:S(2)}, u32[]{:S(2)}) %collective-permute-start.1) | collective-permute-done | bytes 131104 | tf_op jit(solution)/shard_map/ppermute | solution.py:25
  8.1 2.8 %collective-permute-start.2 = (bf16[64,1024]{1,0:T(8,128)(2,1)}, bf16[64,1024]{1,0:T(8,128)(2,1)S(1)}, u32[]{:S(2)}, u32[]{:S(2)}) collective-permute-start(bf16[64,1024]{1,0:T(8,128)(2,1)} %bitcast.14), channel_id=1, source_target_pairs={{0,8},{1,9},{2,10},{3,11},{4,12},{5,13},{6,14},{7,15},{8,0},{9,1},... | collective-permute-start | bytes 393224 | tf_op jit(solution)/shard_map/ppermute | solution.py:25
  10.9 0.0 collective-permute-done.refs_4_
  10.9 1.3 %collective-permute-start.3 = (bf16[64,1024]{1,0:T(8,128)(2,1)}, bf16[64,1024]{1,0:T(8,128)(2,1)S(1)}, u32[]{:S(2)}, u32[]{:S(2)}) collective-permute-start(bf16[64,1024]{1,0:T(8,128)(2,1)} %bitcast.15), channel_id=1, source_target_pairs={{0,12},{1,13},{2,14},{3,15},{4,8},{5,9},{6,10},{7,11},{8,4},{9,5},... | collective-permute-start | bytes 393224 | tf_op jit(solution)/shard_map/ppermute | solution.py:25
  12.2 0.0 copy-start
  12.2 0.9 %copy-done = bf16[1,1024,128]{2,1,0:T(8,128)(2,1)S(1)} copy-done((bf16[1,1024,128]{2,1,0:T(8,128)(2,1)S(1)}, bf16[1,1024,128]{2,1,0:T(8,128)(2,1)}, u32[]{:S(2)}) %copy-start) | copy-done | bytes 262168
  13.2 0.0 copy-start.1
  13.2 0.9 %copy-done.1 = bf16[1,1,1024,128]{3,2,1,0:T(8,128)(2,1)S(1)} copy-done((bf16[1,1,1024,128]{3,2,1,0:T(8,128)(2,1)S(1)}, bf16[1,1,1024,128]{3,2,1,0:T(8,128)(2,1)}, u32[]{:S(2)}) %copy-start.1) | copy-done | bytes 262168
  14.1 0.0 copy-start.2
  14.1 0.9 %copy-done.2 = bf16[1,64,1024]{2,1,0:T(8,128)(2,1)S(1)} copy-done((bf16[1,64,1024]{2,1,0:T(8,128)(2,1)S(1)}, bf16[1,64,1024]{2,1,0:T(8,128)(2,1)}, u32[]{:S(2)}) %copy-start.2) | copy-done | bytes 131096
  15.0 2.3 %stage_inputs.1 = (bf16[1024,128]{1,0:T(8,128)(2,1)S(1)}, bf16[1024,128]{1,0:T(8,128)(2,1)S(1)}, bf16[2,1024,1024]{2,1,0:T(8,128)(2,1)S(1)}, bf16[64,1024]{1,0:T...) custom-call(bf16[1024,128]{1,0:T(8,128)(2,1)S(1)} %bitcast.7, ...), custom_call_target="tpu_custom_call" | custom-call | bytes 9699328 | tf_op jit(solution)/shard_map/stage_inputs/pallas_call | solution.py:84
  17.4 3.7 %collective-permute-done.2.refs_2_ = bf16[64,1024]{1,0:T(8,128)(2,1)S(1)} collective-permute-done((bf16[64,1024]{1,0:T(8,128)(2,1)}, bf16[64,1024]{1,0:T(8,128)(2,1)S(1)}, u32[]{:S(2)}, u32[]{:S(2)}) %collective-permute-start.2) | collective-permute-done | bytes 131104 | tf_op jit(solution)/shard_map/ppermute | solution.py:25
  21.1 0.0 collective-permute-done.3.refs_3_
  21.1 0.0 collective-permute-done.4.refs_5_.refs_1_
  21.1 0.0 collective-permute-done.5.refs_6_.refs_2_
  21.1 0.0 collective-permute-done.6.refs_7_.refs_3_
  21.1 0.7 %rq_pieces.1 = (f32[256,128]{1,0:T(8,128)S(1)}, bf16[256,128]{1,0:T(8,128)(2,1)S(1)}, bf16[256,128]{1,0:T(8,128)(2,1)S(1)}, bf16[256,128]{1,0:T(8,128)(2,1)S(1)}) custom-call(bf16[64,1024]{1,0:T(8,128)(2,1)S(1)} %get-tuple-element.18.refs_0_, bf16[64,1024]{1,0:T(8,128)(2,1)S(1)} %collective-permute-done.1.refs_1_, ...), custom_call_target="tpu_custom_call" | custom-call | flops 268435456 | bytes 1572864 | tf_op jit(solution)/shard_map/rq_pieces/pallas_call | solution.py:111
  21.8 1.6 %collective-permute-start.7 = (bf16[256,128]{1,0:T(8,128)(2,1)S(1)}, bf16[256,128]{1,0:T(8,128)(2,1)S(1)}, u32[]{:S(2)}, u32[]{:S(2)}) collective-permute-start(bf16[256,128]{1,0:T(8,128)(2,1)S(1)} %get-tuple-element.21), channel_id=1, source_target_pairs={{0,1},{1,0},{2,3},{3,2},{4,5},{5,4},{6,7},{7,6},{8,9},{9,8},{10,11... | collective-permute-start | bytes 196616 | tf_op jit(solution)/shard_map/ppermute | solution.py:25
  23.4 1.5 %collective-permute-start.8 = (bf16[256,128]{1,0:T(8,128)(2,1)S(1)}, bf16[256,128]{1,0:T(8,128)(2,1)S(1)}, u32[]{:S(2)}, u32[]{:S(2)}) collective-permute-start(bf16[256,128]{1,0:T(8,128)(2,1)S(1)} %get-tuple-element.22), channel_id=1, source_target_pairs={{0,2},{1,3},{2,0},{3,1},{4,6},{5,7},{6,4},{7,5},{8,10},{9,11},{10,... | collective-permute-start | bytes 196616 | tf_op jit(solution)/shard_map/ppermute | solution.py:25
  24.9 0.5 collective-permute-start.9
  25.4 0.8 %collective-permute-done.7.refs_3_ = bf16[256,128]{1,0:T(8,128)(2,1)S(1)} collective-permute-done((bf16[256,128]{1,0:T(8,128)(2,1)S(1)}, bf16[256,128]{1,0:T(8,128)(2,1)S(1)}, u32[]{:S(2)}, u32[]{:S(2)}) %collective-permute-start.7) | collective-permute-done | bytes 65568 | tf_op jit(solution)/shard_map/ppermute | solution.py:25
  26.2 1.5 %collective-permute-done.8.refs_4_ = bf16[256,128]{1,0:T(8,128)(2,1)S(1)} collective-permute-done((bf16[256,128]{1,0:T(8,128)(2,1)S(1)}, bf16[256,128]{1,0:T(8,128)(2,1)S(1)}, u32[]{:S(2)}, u32[]{:S(2)}) %collective-permute-start.8) | collective-permute-done | bytes 65568 | tf_op jit(solution)/shard_map/ppermute | solution.py:25
  27.7 2.4 %collective-permute-done.9.refs_5_ = bf16[256,128]{1,0:T(8,128)(2,1)S(1)} collective-permute-done((bf16[256,128]{1,0:T(8,128)(2,1)S(1)}, bf16[256,128]{1,0:T(8,128)(2,1)S(1)}, u32[]{:S(2)}, u32[]{:S(2)}) %collective-permute-start.9) | collective-permute-done | bytes 65568 | tf_op jit(solution)/shard_map/ppermute | solution.py:25
  30.1 1.4 %advance.2 = bf16[1024,128]{1,0:T(8,128)(2,1)S(1)} custom-call(bf16[1024,128]{1,0:T(8,128)(2,1)S(1)} %get-tuple-element.17.refs_0_.refs_1_.refs_8_, bf16[1024,128]{1,0:T(8,128)(2,1)S(1)} %get-tuple-element.17.refs_0_.refs_1_.refs_8_, f32[256,128]{1,0:T(8,128)S(1)} %get-tuple-element.20.refs_2_, bf16[256,128]{1,0:T(8,128)(2,1)S(1)} %collective-permute-done.7.refs_3_, ...), custom_call_target="tpu_custom_call" | custom-call | flops 536870912 | bytes 4194304 | tf_op jit(solution)/shard_map/advance/pallas_call | solution.py:148
  31.5 0.1 collective-permute-start.10
  31.5 0.6 %collective-permute-start.11 = (bf16[1024,128]{1,0:T(8,128)(2,1)S(1)}, bf16[1024,128]{1,0:T(8,128)(2,1)S(1)}, u32[]{:S(2)}, u32[]{:S(2)}) collective-permute-start(bf16[1024,128]{1,0:T(8,128)(2,1)S(1)} %advance.2), channel_id=1, source_target_pairs={{0,17},{1,16},{2,19},{3,18},{4,21},{5,20},{6,23},{7,22},{8,25},{9,... | collective-permute-start | bytes 786440 | tf_op jit(solution)/shard_map/ppermute | solution.py:35
  32.2 0.0 collective-permute-start.14
  32.2 2.6 %collective-permute-start.15 = (bf16[1280,128]{1,0:T(8,128)(2,1)S(1)}, bf16[1280,128]{1,0:T(8,128)(2,1)S(1)}, u32[]{:S(2)}, u32[]{:S(2)}) collective-permute-start(bf16[1280,128]{1,0:T(8,128)(2,1)S(1)} %get-tuple-element.26), channel_id=1, source_target_pairs={{16,8},{17,9},{18,10},{19,11},{20,12},{21,13},{22,14},{23,15},{24,... | collective-permute-start | bytes 983048 | tf_op jit(solution)/shard_map/ppermute | solution.py:43
  34.8 1.8 %collective-permute-start.16 = (bf16[1280,128]{1,0:T(8,128)(2,1)S(1)}, bf16[1280,128]{1,0:T(8,128)(2,1)S(1)}, u32[]{:S(2)}, u32[]{:S(2)}) collective-permute-start(bf16[1280,128]{1,0:T(8,128)(2,1)S(1)} %get-tuple-element.27), channel_id=1, source_target_pairs={{16,12},{17,13},{18,14},{19,15},{20,8},{21,9},{22,10},{23,11},{24,... | collective-permute-start | bytes 983048 | tf_op jit(solution)/shard_map/ppermute | solution.py:43
  36.6 0.0 collective-permute-done.10.refs_1_.refs_4_
  36.6 1.7 %collective-permute-start.12 = (bf16[1024,128]{1,0:T(8,128)(2,1)S(1)}, bf16[1024,128]{1,0:T(8,128)(2,1)S(1)}, u32[]{:S(2)}, u32[]{:S(2)}) collective-permute-start(bf16[1024,128]{1,0:T(8,128)(2,1)S(1)} %advance.2), channel_id=1, source_target_pairs={{0,18},{1,19},{2,16},{3,17},{4,22},{5,23},{6,20},{7,21},{8,26},{9,... | collective-permute-start | bytes 786440 | tf_op jit(solution)/shard_map/ppermute | solution.py:35
  38.3 0.0 collective-permute-done.11.refs_5_
  38.3 1.0 %collective-permute-start.13 = (bf16[1024,128]{1,0:T(8,128)(2,1)S(1)}, bf16[1024,128]{1,0:T(8,128)(2,1)S(1)}, u32[]{:S(2)}, u32[]{:S(2)}) collective-permute-start(bf16[1024,128]{1,0:T(8,128)(2,1)S(1)} %advance.2), channel_id=1, source_target_pairs={{0,19},{1,18},{2,17},{3,16},{4,23},{5,22},{6,21},{7,20},{8,27},{9,... | collective-permute-start | bytes 786440 | tf_op jit(solution)/shard_map/ppermute | solution.py:35
  39.3 5.7 %collective-permute-done.12.refs_6_ = bf16[1024,128]{1,0:T(8,128)(2,1)S(1)} collective-permute-done((bf16[1024,128]{1,0:T(8,128)(2,1)S(1)}, bf16[1024,128]{1,0:T(8,128)(2,1)S(1)}, u32[]{:S(2)}, u32[]{:S(2)}) %collective-permute-start.12) | collective-permute-done | bytes 262176 | tf_op jit(solution)/shard_map/ppermute | solution.py:35
  45.0 0.0 collective-permute-done.13.refs_7_
  45.0 0.0 collective-permute-done.14.refs_9_
  45.0 0.0 collective-permute-done.15.refs_10_
  45.0 4.5 %collective-permute-done.16.refs_11_ = bf16[1280,128]{1,0:T(8,128)(2,1)S(1)} collective-permute-done((bf16[1280,128]{1,0:T(8,128)(2,1)S(1)}, bf16[1280,128]{1,0:T(8,128)(2,1)S(1)}, u32[]{:S(2)}, u32[]{:S(2)}) %collective-permute-start.16) | collective-permute-done | bytes 327712 | tf_op jit(solution)/shard_map/ppermute | solution.py:43
  49.5 0.5 picture_parts.1
  50.0 1.5 %collective-permute-start.19 = (bf16[64,1024]{1,0:T(8,128)(2,1)S(1)}, bf16[64,1024]{1,0:T(8,128)(2,1)S(1)}, u32[]{:S(2)}, u32[]{:S(2)}) collective-permute-start(bf16[64,1024]{1,0:T(8,128)(2,1)S(1)} %get-tuple-element.31), channel_id=1, source_target_pairs={{0,3},{1,2},{2,1},{3,0},{4,7},{5,6},{6,5},{7,4},{8,11},{9,10},{10,... | collective-permute-start | bytes 393224 | tf_op jit(solution)/shard_map/ppermute | solution.py:53
  51.5 1.5 %collective-permute-start.18 = (bf16[64,1024]{1,0:T(8,128)(2,1)S(1)}, bf16[64,1024]{1,0:T(8,128)(2,1)S(1)}, u32[]{:S(2)}, u32[]{:S(2)}) collective-permute-start(bf16[64,1024]{1,0:T(8,128)(2,1)S(1)} %get-tuple-element.30), channel_id=1, source_target_pairs={{0,2},{1,3},{2,0},{3,1},{4,6},{5,7},{6,4},{7,5},{8,10},{9,11},{10,... | collective-permute-start | bytes 393224 | tf_op jit(solution)/shard_map/ppermute | solution.py:53
  53.0 0.5 collective-permute-start.17
  53.6 2.1 %advance.3 = bf16[1024,128]{1,0:T(8,128)(2,1)} custom-call(bf16[1024,128]{1,0:T(8,128)(2,1)S(1)} %get-tuple-element.17.refs_0_.refs_1_.refs_8_, bf16[1024,128]{1,0:T(8,128)(2,1)S(1)} %collective-permute-done.10.refs_1_.refs_4_, f32[256,128]{1,0:T(8,128)S(1)} %get-tuple-element.20.refs_2_, bf16[256,128]{1,0:T(8,128)(2,1)S(1)} %collective-permute-done.7.refs_3_, ...), custom_call_target="tpu_custom_call" | custom-call | flops 536870912 | bytes 4194304 | tf_op jit(solution)/shard_map/advance/pallas_call | solution.py:148
  55.6 0.4 collective-permute-done.19
  56.0 1.3 %collective-permute-done.18 = bf16[64,1024]{1,0:T(8,128)(2,1)S(1)} collective-permute-done((bf16[64,1024]{1,0:T(8,128)(2,1)S(1)}, bf16[64,1024]{1,0:T(8,128)(2,1)S(1)}, u32[]{:S(2)}, u32[]{:S(2)}) %collective-permute-start.18) | collective-permute-done | bytes 131104 | tf_op jit(solution)/shard_map/ppermute | solution.py:53
  57.3 0.7 %collective-permute-done.17 = bf16[64,1024]{1,0:T(8,128)(2,1)S(1)} collective-permute-done((bf16[64,1024]{1,0:T(8,128)(2,1)S(1)}, bf16[64,1024]{1,0:T(8,128)(2,1)S(1)}, u32[]{:S(2)}, u32[]{:S(2)}) %collective-permute-start.17) | collective-permute-done | bytes 131104 | tf_op jit(solution)/shard_map/ppermute | solution.py:53
  58.0 0.8 %multiply_bitcast_fusion = f32[1,64,1024]{2,1,0:T(8,128)} fusion(bf16[64,1024]{1,0:T(8,128)(2,1)S(1)} %collective-permute-done.19, bf16[64,1024]{1,0:T(8,128)(2,1)S(1)} %collective-permute-done.18, f32[64,1024]{1,0:T(8,128)S(1)} %get-tuple-element.28, bf16[64,1024]{1,0:T(8,128)(2,1)S(1)} %collective-permute-done.17), kind=kLoop, calls=%fused_computation | loop fusion | flops 458752 | bytes 917504 | tf_op jit(solution)/shard_map/broadcast_in_dim | solution.py:247
Async XLA Ops:
  0.6 10.3 %collective-permute-start = (bf16[1024,128]{1,0:T(8,128)(2,1)}, bf16[1024,128]{1,0:T(8,128)(2,1)S(1)}, u32[]{:S(2)}, u32[]{:S(2)}) collective-permute-start(bf16[1024,128]{1,0:T(8,128)(2,1)} %bitcast.8), channel_id=1, source_target_pairs={{0,16},{1,17},{2,18},{3,19},{4,20},{5,21},{6,22},{7,23},{8,24},{9,... | collective-permute-start | bytes 786440 | tf_op jit(solution)/shard_map/ppermute | solution.py:35
  1.2 6.9 %collective-permute-start.1 = (bf16[64,1024]{1,0:T(8,128)(2,1)}, bf16[64,1024]{1,0:T(8,128)(2,1)S(1)}, u32[]{:S(2)}, u32[]{:S(2)}) collective-permute-start(bf16[64,1024]{1,0:T(8,128)(2,1)} %bitcast.13), channel_id=1, source_target_pairs={{0,4},{1,5},{2,6},{3,7},{4,0},{5,1},{6,2},{7,3},{8,12},{9,13},{10,... | collective-permute-start | bytes 393224 | tf_op jit(solution)/shard_map/ppermute | solution.py:25
  3.8 17.3 %collective-permute-start.4 = (bf16[1024,128]{1,0:T(8,128)(2,1)}, bf16[1024,128]{1,0:T(8,128)(2,1)S(1)}, u32[]{:S(2)}, u32[]{:S(2)}) collective-permute-start(bf16[1024,128]{1,0:T(8,128)(2,1)} %bitcast.9), channel_id=1, source_target_pairs={{0,1},{1,0},{2,3},{3,2},{4,5},{5,4},{6,7},{7,6},{8,9},{9,8},{10,11... | collective-permute-start | bytes 786440 | tf_op jit(solution)/shard_map/ppermute | solution.py:25
  5.3 15.8 %collective-permute-start.5 = (bf16[1024,128]{1,0:T(8,128)(2,1)}, bf16[1024,128]{1,0:T(8,128)(2,1)S(1)}, u32[]{:S(2)}, u32[]{:S(2)}) collective-permute-start(bf16[1024,128]{1,0:T(8,128)(2,1)} %bitcast.10), channel_id=1, source_target_pairs={{0,2},{1,3},{2,0},{3,1},{4,6},{5,7},{6,4},{7,5},{8,10},{9,11},{10,... | collective-permute-start | bytes 786440 | tf_op jit(solution)/shard_map/ppermute | solution.py:25
  6.8 14.3 %collective-permute-start.6 = (bf16[1024,128]{1,0:T(8,128)(2,1)}, bf16[1024,128]{1,0:T(8,128)(2,1)S(1)}, u32[]{:S(2)}, u32[]{:S(2)}) collective-permute-start(bf16[1024,128]{1,0:T(8,128)(2,1)} %bitcast.11), channel_id=1, source_target_pairs={{0,3},{1,2},{2,1},{3,0},{4,7},{5,6},{6,5},{7,4},{8,11},{9,10},{10,... | collective-permute-start | bytes 786440 | tf_op jit(solution)/shard_map/ppermute | solution.py:25
  8.1 13.0 %collective-permute-start.2 = (bf16[64,1024]{1,0:T(8,128)(2,1)}, bf16[64,1024]{1,0:T(8,128)(2,1)S(1)}, u32[]{:S(2)}, u32[]{:S(2)}) collective-permute-start(bf16[64,1024]{1,0:T(8,128)(2,1)} %bitcast.14), channel_id=1, source_target_pairs={{0,8},{1,9},{2,10},{3,11},{4,12},{5,13},{6,14},{7,15},{8,0},{9,1},... | collective-permute-start | bytes 393224 | tf_op jit(solution)/shard_map/ppermute | solution.py:25
  10.9 10.2 %collective-permute-start.3 = (bf16[64,1024]{1,0:T(8,128)(2,1)}, bf16[64,1024]{1,0:T(8,128)(2,1)S(1)}, u32[]{:S(2)}, u32[]{:S(2)}) collective-permute-start(bf16[64,1024]{1,0:T(8,128)(2,1)} %bitcast.15), channel_id=1, source_target_pairs={{0,12},{1,13},{2,14},{3,15},{4,8},{5,9},{6,10},{7,11},{8,4},{9,5},... | collective-permute-start | bytes 393224 | tf_op jit(solution)/shard_map/ppermute | solution.py:25
  12.2 0.9 %copy-start = (bf16[1,1024,128]{2,1,0:T(8,128)(2,1)S(1)}, bf16[1,1024,128]{2,1,0:T(8,128)(2,1)}, u32[]{:S(2)}) copy-start(bf16[1,1024,128]{2,1,0:T(8,128)(2,1)} %param.4) | copy-start | bytes 786436
  13.2 0.9 %copy-start.1 = (bf16[1,1,1024,128]{3,2,1,0:T(8,128)(2,1)S(1)}, bf16[1,1,1024,128]{3,2,1,0:T(8,128)(2,1)}, u32[]{:S(2)}) copy-start(bf16[1,1,1024,128]{3,2,1,0:T(8,128)(2,1)} %param.5) | copy-start | bytes 786436
  14.1 0.9 %copy-start.2 = (bf16[1,64,1024]{2,1,0:T(8,128)(2,1)S(1)}, bf16[1,64,1024]{2,1,0:T(8,128)(2,1)}, u32[]{:S(2)}) copy-start(bf16[1,64,1024]{2,1,0:T(8,128)(2,1)} %param.7) | copy-start | bytes 393220
  21.8 4.4 %collective-permute-start.7 = (bf16[256,128]{1,0:T(8,128)(2,1)S(1)}, bf16[256,128]{1,0:T(8,128)(2,1)S(1)}, u32[]{:S(2)}, u32[]{:S(2)}) collective-permute-start(bf16[256,128]{1,0:T(8,128)(2,1)S(1)} %get-tuple-element.21), channel_id=1, source_target_pairs={{0,1},{1,0},{2,3},{3,2},{4,5},{5,4},{6,7},{7,6},{8,9},{9,8},{10,11... | collective-permute-start | bytes 196616 | tf_op jit(solution)/shard_map/ppermute | solution.py:25
  23.4 4.3 %collective-permute-start.8 = (bf16[256,128]{1,0:T(8,128)(2,1)S(1)}, bf16[256,128]{1,0:T(8,128)(2,1)S(1)}, u32[]{:S(2)}, u32[]{:S(2)}) collective-permute-start(bf16[256,128]{1,0:T(8,128)(2,1)S(1)} %get-tuple-element.22), channel_id=1, source_target_pairs={{0,2},{1,3},{2,0},{3,1},{4,6},{5,7},{6,4},{7,5},{8,10},{9,11},{10,... | collective-permute-start | bytes 196616 | tf_op jit(solution)/shard_map/ppermute | solution.py:25
  24.9 5.2 %collective-permute-start.9 = (bf16[256,128]{1,0:T(8,128)(2,1)S(1)}, bf16[256,128]{1,0:T(8,128)(2,1)S(1)}, u32[]{:S(2)}, u32[]{:S(2)}) collective-permute-start(bf16[256,128]{1,0:T(8,128)(2,1)S(1)} %get-tuple-element.23), channel_id=1, source_target_pairs={{0,3},{1,2},{2,1},{3,0},{4,7},{5,6},{6,5},{7,4},{8,11},{9,10},{10,... | collective-permute-start | bytes 196616 | tf_op jit(solution)/shard_map/ppermute | solution.py:25
  31.5 5.1 %collective-permute-start.10 = (bf16[1024,128]{1,0:T(8,128)(2,1)S(1)}, bf16[1024,128]{1,0:T(8,128)(2,1)S(1)}, u32[]{:S(2)}, u32[]{:S(2)}) collective-permute-start(bf16[1024,128]{1,0:T(8,128)(2,1)S(1)} %advance.2), channel_id=1, source_target_pairs={{0,16},{1,17},{2,18},{3,19},{4,20},{5,21},{6,22},{7,23},{8,24},{9,... | collective-permute-start | bytes 786440 | tf_op jit(solution)/shard_map/ppermute | solution.py:35
  31.5 6.7 %collective-permute-start.11 = (bf16[1024,128]{1,0:T(8,128)(2,1)S(1)}, bf16[1024,128]{1,0:T(8,128)(2,1)S(1)}, u32[]{:S(2)}, u32[]{:S(2)}) collective-permute-start(bf16[1024,128]{1,0:T(8,128)(2,1)S(1)} %advance.2), channel_id=1, source_target_pairs={{0,17},{1,16},{2,19},{3,18},{4,21},{5,20},{6,23},{7,22},{8,25},{9,... | collective-permute-start | bytes 786440 | tf_op jit(solution)/shard_map/ppermute | solution.py:35
  32.2 12.8 %collective-permute-start.14 = (bf16[1280,128]{1,0:T(8,128)(2,1)S(1)}, bf16[1280,128]{1,0:T(8,128)(2,1)S(1)}, u32[]{:S(2)}, u32[]{:S(2)}) collective-permute-start(bf16[1280,128]{1,0:T(8,128)(2,1)S(1)} %get-tuple-element.25), channel_id=1, source_target_pairs={{16,4},{17,5},{18,6},{19,7},{20,0},{21,1},{22,2},{23,3},{24,12},{2... | collective-permute-start | bytes 983048 | tf_op jit(solution)/shard_map/ppermute | solution.py:43
  32.2 12.8 %collective-permute-start.15 = (bf16[1280,128]{1,0:T(8,128)(2,1)S(1)}, bf16[1280,128]{1,0:T(8,128)(2,1)S(1)}, u32[]{:S(2)}, u32[]{:S(2)}) collective-permute-start(bf16[1280,128]{1,0:T(8,128)(2,1)S(1)} %get-tuple-element.26), channel_id=1, source_target_pairs={{16,8},{17,9},{18,10},{19,11},{20,12},{21,13},{22,14},{23,15},{24,... | collective-permute-start | bytes 983048 | tf_op jit(solution)/shard_map/ppermute | solution.py:43
  34.8 14.8 %collective-permute-start.16 = (bf16[1280,128]{1,0:T(8,128)(2,1)S(1)}, bf16[1280,128]{1,0:T(8,128)(2,1)S(1)}, u32[]{:S(2)}, u32[]{:S(2)}) collective-permute-start(bf16[1280,128]{1,0:T(8,128)(2,1)S(1)} %get-tuple-element.27), channel_id=1, source_target_pairs={{16,12},{17,13},{18,14},{19,15},{20,8},{21,9},{22,10},{23,11},{24,... | collective-permute-start | bytes 983048 | tf_op jit(solution)/shard_map/ppermute | solution.py:43
  36.6 8.4 %collective-permute-start.12 = (bf16[1024,128]{1,0:T(8,128)(2,1)S(1)}, bf16[1024,128]{1,0:T(8,128)(2,1)S(1)}, u32[]{:S(2)}, u32[]{:S(2)}) collective-permute-start(bf16[1024,128]{1,0:T(8,128)(2,1)S(1)} %advance.2), channel_id=1, source_target_pairs={{0,18},{1,19},{2,16},{3,17},{4,22},{5,23},{6,20},{7,21},{8,26},{9,... | collective-permute-start | bytes 786440 | tf_op jit(solution)/shard_map/ppermute | solution.py:35
  38.3 6.7 %collective-permute-start.13 = (bf16[1024,128]{1,0:T(8,128)(2,1)S(1)}, bf16[1024,128]{1,0:T(8,128)(2,1)S(1)}, u32[]{:S(2)}, u32[]{:S(2)}) collective-permute-start(bf16[1024,128]{1,0:T(8,128)(2,1)S(1)} %advance.2), channel_id=1, source_target_pairs={{0,19},{1,18},{2,17},{3,16},{4,23},{5,22},{6,21},{7,20},{8,27},{9,... | collective-permute-start | bytes 786440 | tf_op jit(solution)/shard_map/ppermute | solution.py:35
  50.0 6.0 %collective-permute-start.19 = (bf16[64,1024]{1,0:T(8,128)(2,1)S(1)}, bf16[64,1024]{1,0:T(8,128)(2,1)S(1)}, u32[]{:S(2)}, u32[]{:S(2)}) collective-permute-start(bf16[64,1024]{1,0:T(8,128)(2,1)S(1)} %get-tuple-element.31), channel_id=1, source_target_pairs={{0,3},{1,2},{2,1},{3,0},{4,7},{5,6},{6,5},{7,4},{8,11},{9,10},{10,... | collective-permute-start | bytes 393224 | tf_op jit(solution)/shard_map/ppermute | solution.py:53
  51.5 5.8 %collective-permute-start.18 = (bf16[64,1024]{1,0:T(8,128)(2,1)S(1)}, bf16[64,1024]{1,0:T(8,128)(2,1)S(1)}, u32[]{:S(2)}, u32[]{:S(2)}) collective-permute-start(bf16[64,1024]{1,0:T(8,128)(2,1)S(1)} %get-tuple-element.30), channel_id=1, source_target_pairs={{0,2},{1,3},{2,0},{3,1},{4,6},{5,7},{6,4},{7,5},{8,10},{9,11},{10,... | collective-permute-start | bytes 393224 | tf_op jit(solution)/shard_map/ppermute | solution.py:53
  53.0 5.0 %collective-permute-start.17 = (bf16[64,1024]{1,0:T(8,128)(2,1)S(1)}, bf16[64,1024]{1,0:T(8,128)(2,1)S(1)}, u32[]{:S(2)}, u32[]{:S(2)}) collective-permute-start(bf16[64,1024]{1,0:T(8,128)(2,1)S(1)} %get-tuple-element.29), channel_id=1, source_target_pairs={{0,1},{1,0},{2,3},{3,2},{4,5},{5,4},{6,7},{7,6},{8,9},{9,8},{10,11... | collective-permute-start | bytes 393224 | tf_op jit(solution)/shard_map/ppermute | solution.py:53

commit v2 on v1

v2 whole, which is shorter than its diff:
```python
import functools

import jax
import jax.numpy as jnp
from jax import lax
from jax.experimental import pallas as pl
from jax.experimental.pallas import tpu as pltpu
from jax.sharding import PartitionSpec as P


VMEM = pl.BlockSpec(memory_space=pltpu.VMEM)
MIB = 1 << 20
STAGE_LIMIT = 47 * MIB
HALVES = 1
TWO_STEP = False


def plane_size(devices):
    size = 1
    while 4 * size * size <= devices:
        size *= 2
    return size


def swap(value, by):
    devices = lax.axis_size("freq")
    return lax.ppermute(value, "freq", [(i, i ^ by) for i in range(devices)])


def lower(value, by):
    levels, devices = lax.axis_size("depth"), lax.axis_size("freq")
    pairs = [
        (d * devices + i, (d + 1) * devices + (i ^ by) if d + 1 < levels else i)
        for d in range(levels)
        for i in range(devices)
    ]
    return lax.ppermute(value, ("depth", "freq"), pairs)


def raise_top(value, by):
    levels, devices = lax.axis_size("depth"), lax.axis_size("freq")
    pairs = [((devices if levels > 1 else 0) + i, i ^ by) for i in range(devices)]
    if levels > 1:
        pairs += [(i, devices + i) for i in range(devices)]
    return lax.ppermute(value, ("depth", "freq"), pairs)


def reduce_step(value, k, plane, line):
    levels, devices = lax.axis_size("depth"), lax.axis_size("freq")
    pairs = []
    for d in range(levels):
        if k < (line if d else plane):
            by = k * plane if d else k
            pairs += [(d * devices + i, d * devices + (i ^ by)) for i in range(devices)]
    return lax.ppermute(value, ("depth", "freq"), pairs)


def params(limit):
    return pltpu.CompilerParams(vmem_limit_bytes=limit)


def copy_all(pairs, sems):
    copies = [pltpu.make_async_copy(a, b, sems.at[k]) for k, (a, b) in enumerate(pairs)]
    for copy in copies:
        copy.start()
    for copy in copies:
        copy.wait()


def weights_kernel(source, target, sems):
    tall = source.shape[1] // 2
    parts = [(k, pl.ds(h * tall, tall)) for k in range(2) for h in range(2)]
    copy_all([(source.at[p], target.at[p]) for p in parts], sems)


def stage_weights(weights):
    size = weights.size * weights.dtype.itemsize
    return pl.pallas_call(
        weights_kernel,
        out_shape=jax.ShapeDtypeStruct(weights.shape, weights.dtype),
        in_specs=[pl.BlockSpec(memory_space=pl.ANY)],
        out_specs=VMEM,
        scratch_shapes=[pltpu.SemaphoreType.DMA((4,))],
        compiler_params=params(STAGE_LIMIT),
        cost_estimate=pl.CostEstimate(flops=0, bytes_accessed=2 * size, transcendentals=0),
        name="stage_weights",
    )(weights)


def stage_kernel(count, plane, line, *refs):
    sources, other = refs[:count], refs[count]
    targets, loads = refs[count + 1 : 2 * count + 1], refs[2 * count + 1 : -1]
    copies = list(zip(sources, targets))
    at_plane = lax.axis_index("freq") // plane
    nx = other.shape[0]
    tall = nx // line
    for z, load in enumerate(loads, 1):
        rows = pl.ds(pl.multiple_of((at_plane ^ z) * tall, tall), tall)
        copies += [(sources[0], load.at[pl.ds(0, nx)]), (other.at[rows], load.at[pl.ds(nx, tall)])]
    copy_all(copies, refs[-1])


def stage(arrays, other, plane, line):
    count = len(arrays)
    nx, cols = other.shape
    size = sum(a.size * a.dtype.itemsize for a in arrays) + (line - 1) * (nx + nx // line) * cols * 2
    out_shape = [jax.ShapeDtypeStruct(a.shape, a.dtype) for a in arrays]
    out_shape += [jax.ShapeDtypeStruct((nx + nx // line, cols), other.dtype)] * (line - 1)
    outs = pl.pallas_call(
        functools.partial(stage_kernel, count, plane, line),
        out_shape=out_shape,
        in_specs=[pl.BlockSpec(memory_space=pl.ANY)] * (count + 1),
        out_specs=[VMEM] * len(out_shape),
        scratch_shapes=[pltpu.SemaphoreType.DMA((count + 2 * (line - 1),))],
        compiler_params=params(16 * MIB),
        cost_estimate=pl.CostEstimate(flops=0, bytes_accessed=2 * size, transcendentals=0),
        name="stage_inputs",
    )(*arrays, other)
    return outs[:count], outs[count:]


def pieces_kernel(line, cuts, *refs):
    blocks, refs = refs[:line], refs[line:]
    ups, outs, joined = refs[: sum(cuts)], refs[sum(cuts) : sum(cuts) + len(cuts)], list(refs[sum(cuts) + len(cuts) :])
    rows = jnp.concatenate([b[...] for b in blocks], axis=0)
    for cut, out in zip(cuts, outs):
        parts, ups = ups[:cut], ups[cut:]
        up = parts[0][...] if cut == 1 else jnp.concatenate([p[...] for p in parts], axis=0)
        if cut > 1:
            joined.pop(0)[...] = up
        out[...] = jnp.dot(rows, up, preferred_element_type=jnp.float32).astype(out.dtype)


def rq_pieces(blocks, ups):
    line, plane = len(blocks), len(ups)
    cuts = [len(parts) for parts in ups]
    rows, nx = blocks[0].shape
    cols = ups[0][0].shape[1]
    tall = line * rows
    out_shape = [jax.ShapeDtypeStruct((tall, cols), jnp.float32)]
    out_shape += [jax.ShapeDtypeStruct((tall, cols), jnp.bfloat16)] * (plane - 1)
    out_shape += [jax.ShapeDtypeStruct((nx, cols), jnp.bfloat16)] * sum(cut > 1 for cut in cuts)
    outs = pl.pallas_call(
        functools.partial(pieces_kernel, line, cuts),
        out_shape=out_shape,
        in_specs=[VMEM] * (line + sum(cuts)),
        out_specs=[VMEM] * len(out_shape),
        compiler_params=params(16 * MIB),
        cost_estimate=pl.CostEstimate(
            flops=2 * tall * nx * cols * plane, bytes_accessed=2 * nx * (tall + plane * cols), transcendentals=0
        ),
        name="rq_pieces",
    )(*blocks, *[part for parts in ups for part in parts])
    joined = list(outs[plane:])
    return list(outs[:plane]), [parts[0] if len(parts) == 1 else joined.pop(0) for parts in ups]


def gather_line(value, plane, line):
    found = {0: value}
    for z in range(1, line):
        far = z & (z - 1) if z.bit_count() == 2 else 0
        found[z] = swap(found[far], (z ^ far) * plane)
    return [found[z] for z in range(line)]


def gather_plane(value, plane):
    found = {0: [value]}
    tall = value.shape[0] // 2
    for q in range(1, plane):
        if not TWO_STEP or q.bit_count() != 2:
            found[q] = [swap(value, q)]
    for q in range(1, plane):
        if TWO_STEP and q.bit_count() == 2:
            low, high = q & -q, q & (q - 1)
            found[q] = [swap(found[high][0][:tall], low), swap(found[low][0][tall:], high)]
    return [found[q] for q in range(plane)]


def advance_kernel(line, plane, counts, *refs):
    top, moved, refs = refs[0], refs[1 : 1 + counts[0]], refs[1 + counts[0] :]
    pieces, weights, outs, diff = refs[:plane], refs[plane], refs[plane + 1 : -1], refs[-1]
    me = lax.axis_index("freq")
    first = lax.axis_index("depth") == 0
    rows = top.shape[0] // (line * plane)
    cols = top.shape[1]

    def subtract(field):
        for z in range(line):
            for q in range(plane):
                at = pl.multiple_of((me ^ (z * plane + q)) * rows, rows)
                rq = pieces[q][z * rows : (z + 1) * rows, :].astype(jnp.float32)
                diff[pl.ds(at, rows), :] = (field[pl.ds(at, rows), :].astype(jnp.float32) - rq).astype(jnp.bfloat16)

    @pl.when(first)
    def _():
        subtract(top)

    @pl.when(jnp.logical_not(first))
    def _():
        if not moved:
            diff[...] = jnp.zeros_like(diff)
            return
        tall = top.shape[0] // len(moved)
        for h, part in enumerate(moved):
            diff[h * tall : (h + 1) * tall, :] = part[...]
        subtract(diff)

    straight = diff[...]
    half = cols // 2
    turned = jnp.concatenate([-straight[:, half:], straight[:, :half]], axis=1)
    tall = top.shape[0] // counts[1]
    for h, out in enumerate(outs):
        part = slice(h * tall, (h + 1) * tall)
        out[...] = (
            jnp.dot(weights[0, part, :], straight, preferred_element_type=jnp.float32)
            + jnp.dot(weights[1, part, :], turned, preferred_element_type=jnp.float32)
        ).astype(jnp.bfloat16)


def advance(top, moved, pieces, weights, line, plane, parts):
    nx, cols = top.shape
    return pl.pallas_call(
        functools.partial(advance_kernel, line, plane, (len(moved), parts)),
        out_shape=[jax.ShapeDtypeStruct((nx // parts, cols), jnp.bfloat16)] * parts,
        in_specs=[VMEM] * (2 + len(moved) + plane),
        out_specs=[VMEM] * parts,
        scratch_shapes=[pltpu.VMEM((nx, cols), jnp.bfloat16)],
        compiler_params=params(24 * MIB),
        cost_estimate=pl.CostEstimate(flops=4 * nx * nx * cols, bytes_accessed=4 * nx * nx, transcendentals=0),
        name="advance",
    )(top, *moved, *pieces, weights)


def side_by_side(parts):
    return jnp.concatenate(parts, axis=1)


def stacked_rows(ref, starts, rows):
    return jnp.concatenate([ref[pl.ds(pl.multiple_of(s, rows), rows), :] for s in starts], axis=0)


def picture_kernel(line, plane, part, *refs):
    ups, fields, refs = refs[:plane], refs[plane : 2 * plane], refs[2 * plane :]
    top, loads, outs = refs[0], refs[1:line], refs[line:]
    me = lax.axis_index("freq")
    first = lax.axis_index("depth") == 0
    nx = top.shape[0]
    rows = outs[0].shape[0]

    def write(left, right, count):
        total = lax.dot_general(left, right, (((1,), (1,)), ((), ())), preferred_element_type=jnp.float32)
        for k, out in enumerate(outs):
            if k < count:
                out[...] = total[k * rows : (k + 1) * rows].astype(out.dtype)

    @pl.when(first)
    def _():
        inner = me % plane
        starts = [(me ^ q) * rows for q in range(plane)]
        lefts = [stacked_rows(ups[0], starts, rows)]
        lefts += [stacked_rows(load, [nx + (inner ^ q) * rows for q in range(plane)], rows) for load in loads]
        rights = [top[part, :]] + [load[part, :] for load in loads]
        write(side_by_side(lefts), side_by_side(rights), plane)

    @pl.when(jnp.logical_not(first))
    def _():
        starts = [(me ^ (z * plane)) * rows for z in range(line)]
        lefts = [stacked_rows(up, starts, rows) for up in ups]
        write(side_by_side(lefts), side_by_side([f[...] for f in fields]), line)


def picture_parts(ups, fields, top, loads, plane, line, h):
    nx, cols = top.shape
    rows = nx // (line * plane)
    wide = fields[0].shape[0]
    count = max(line, plane)
    out_shape = [jax.ShapeDtypeStruct((rows, wide), jnp.float32)]
    out_shape += [jax.ShapeDtypeStruct((rows, wide), jnp.bfloat16)] * (count - 1)
    return pl.pallas_call(
        functools.partial(picture_kernel, line, plane, slice(h * wide, (h + 1) * wide)),
        out_shape=out_shape,
        in_specs=[VMEM] * (2 * plane + line),
        out_specs=[VMEM] * count,
        compiler_params=params(24 * MIB),
        cost_estimate=pl.CostEstimate(
            flops=2 * line * rows * wide * cols * plane, bytes_accessed=4 * nx * cols * plane, transcendentals=0
        ),
        name="picture_parts",
    )(*ups, *fields, top, *loads)


def sum_kernel(scale, halves, count, *refs):
    out = refs[-1]
    wide = refs[0].shape[1]
    for h in range(halves):
        part = refs[h * count : (h + 1) * count]
        total = part[0][...]
        for ref in part[1:]:
            total = total + ref[...].astype(jnp.float32)
        out[:, h * wide : (h + 1) * wide] = total * scale


def summed(parts, scale):
    halves, count = len(parts), len(parts[0])
    rows, wide = parts[0][0].shape
    return pl.pallas_call(
        functools.partial(sum_kernel, scale, halves, count),
        out_shape=jax.ShapeDtypeStruct((rows, halves * wide), jnp.float32),
        in_specs=[VMEM] * (halves * count),
        out_specs=VMEM,
        compiler_params=params(8 * MIB),
        cost_estimate=pl.CostEstimate(flops=rows * wide * 8, bytes_accessed=rows * wide * 16, transcendentals=0),
        name="sum_parts",
    )(*[ref for part in parts for ref in part])


def local(p_top, upgoing, extrapolator, reflectivity):
    return program(p_top[0], upgoing[0, 0], extrapolator[0, 0], reflectivity[0])


def program(top, upper, weights, own_rows):
    sections = lax.axis_size("depth")
    devices = lax.axis_size("freq")
    plane = plane_size(devices)
    line = devices // plane

    blocks = gather_line(own_rows, plane, line)
    other = lower(upper, 0)
    ups = gather_plane(upper, plane)
    weights = stage_weights(weights)
    (top, upper, own_rows), loads = stage((top, upper, own_rows), other, plane, line)
    loads = [raise_top(load, z * plane) for z, load in enumerate(loads, 1)]
    blocks, ups = [own_rows] + blocks[1:], [[upper]] + ups[1:]
    pieces, ups = rq_pieces(blocks, ups)
    pieces = [pieces[0]] + [swap(pieces[q], q) for q in range(1, plane)]

    moved = []
    for _ in range(1, sections):
        below = advance(top, moved, pieces, weights, line, plane, HALVES)
        moved = [lower(half, 0) for half in below]
    scale = (float(upper.shape[1]) * devices) ** (-0.5)
    sums = []
    for h in range(HALVES):
        fields = [moved[h]] + [lower(below[h], q) for q in range(1, plane)]
        parts = picture_parts(ups, fields, top, loads, plane, line, h)
        sums.append([parts[0]] + [reduce_step(parts[k], k, plane, line) for k in range(1, len(parts))])
    (below,) = advance(top, moved, pieces, weights, line, plane, 1)
    return (below[None, None], summed(sums, scale)[None])


def solution(mesh):
    in_specs = (
        P("freq", None, None),
        P("depth", "freq", None, None),
        P("depth", "freq", None, None, None),
        P("depth", "freq", None),
    )
    out_specs = (P("depth", "freq", None, None), P("depth", "freq", None))
    return jax.shard_map(local, mesh=mesh, in_specs=in_specs, out_specs=out_specs, check_vma=False)
```

time: 59 us -> 58.6 us (level)
  the two profiles are of different devices: /device:TPU:0 before, /device:TPU:1 now
where the time goes in v2:
time: 58.6 us; the launch traced here: 58.4 us
  starting transfers between devices  26.1 us (45%)
  waiting for transfers between devices  20.5 us (35%)
  Pallas kernels  8.21 us (14%)
  local copies, waits for them, and re-layouts  2.8 us (5%)
  between operations  0.72 us (1%)
    ppermute x9, starting transfers between devices, swap(): return lax.ppermute(value, 'freq', [(i, i ^ by) for i in range(devices)])  10.6 us
    ppermute x5, waiting for transfers between devices, lower(): return lax.ppermute(value, ('depth', 'freq'), pairs)  8.9 us
    ppermute x9, waiting for transfers between devices, swap(): return lax.ppermute(value, 'freq', [(i, i ^ by) for i in range(devices)])  8.38 us
    ppermute x3, starting transfers between devices, reduce_step(): return lax.ppermute(value, ('depth', 'freq'), pairs)  7.76 us
    ppermute x3, starting transfers between devices, raise_top(): return lax.ppermute(value, ('depth', 'freq'), pairs)  4.57 us
    pallas_call x2, Pallas kernels, advance(): pl.pallas_call(functools.partial(advance_kernel, line, plane, (len(moved)...  3.44 us
    ppermute x3, waiting for transfers between devices, reduce_step(): return lax.ppermute(value, ('depth', 'freq'), pairs)  3.26 us
    ppermute x5, starting transfers between devices, lower(): return lax.ppermute(value, ('depth', 'freq'), pairs)  3.14 us
  transfers between devices with their start and end apart: 20, of which 7 were waited for; matrix products, arithmetic and copies ran while one was open for 0% of the time, Pallas kernels for 8%

profile of v2, /device:TPU:1, one launch (start us, length us, event | category | flops | bytes accessed | tf_op | source)
XLA Modules:
  0.0 58.4 jit_solution(10077127506343049548)
XLA Ops:
  0.6 0.1 collective-permute-start
  0.7 3.8 %collective-permute-start.2 = (bf16[64,1024]{1,0:T(8,128)(2,1)}, bf16[64,1024]{1,0:T(8,128)(2,1)S(1)}, u32[]{:S(2)}, u32[]{:S(2)}) collective-permute-start(bf16[64,1024]{1,0:T(8,128)(2,1)} %bitcast.12), channel_id=1, source_target_pairs={{0,8},{1,9},{2,10},{3,11},{4,12},{5,13},{6,14},{7,15},{8,0},{9,1},... | collective-permute-start | bytes 393224 | tf_op jit(solution)/shard_map/ppermute | solution.py:27
  4.5 1.2 %collective-permute-start.4 = (bf16[1024,128]{1,0:T(8,128)(2,1)}, bf16[1024,128]{1,0:T(8,128)(2,1)S(1)}, u32[]{:S(2)}, u32[]{:S(2)}) collective-permute-start(bf16[1024,128]{1,0:T(8,128)(2,1)} %bitcast.8), channel_id=1, source_target_pairs={{0,1},{1,0},{2,3},{3,2},{4,5},{5,4},{6,7},{7,6},{8,9},{9,8},{10,11... | collective-permute-start | bytes 786440 | tf_op jit(solution)/shard_map/ppermute | solution.py:27
  5.7 1.2 %collective-permute-start.5 = (bf16[1024,128]{1,0:T(8,128)(2,1)}, bf16[1024,128]{1,0:T(8,128)(2,1)S(1)}, u32[]{:S(2)}, u32[]{:S(2)}) collective-permute-start(bf16[1024,128]{1,0:T(8,128)(2,1)} %bitcast.9), channel_id=1, source_target_pairs={{0,2},{1,3},{2,0},{3,1},{4,6},{5,7},{6,4},{7,5},{8,10},{9,11},{10,... | collective-permute-start | bytes 786440 | tf_op jit(solution)/shard_map/ppermute | solution.py:27
  6.9 0.2 collective-permute-start.6
  7.1 4.2 %collective-permute-done.2.refs_2_ = bf16[64,1024]{1,0:T(8,128)(2,1)S(1)} collective-permute-done((bf16[64,1024]{1,0:T(8,128)(2,1)}, bf16[64,1024]{1,0:T(8,128)(2,1)S(1)}, u32[]{:S(2)}, u32[]{:S(2)}) %collective-permute-start.2) | collective-permute-done | bytes 131104 | tf_op jit(solution)/shard_map/ppermute | solution.py:27
  11.3 0.8 %collective-permute-start.1 = (bf16[64,1024]{1,0:T(8,128)(2,1)}, bf16[64,1024]{1,0:T(8,128)(2,1)S(1)}, u32[]{:S(2)}, u32[]{:S(2)}) collective-permute-start(bf16[64,1024]{1,0:T(8,128)(2,1)} %bitcast.13), channel_id=1, source_target_pairs={{0,4},{1,5},{2,6},{3,7},{4,0},{5,1},{6,2},{7,3},{8,12},{9,13},{10,... | collective-permute-start | bytes 393224 | tf_op jit(solution)/shard_map/ppermute | solution.py:27
  12.1 0.0 collective-permute-done.refs_3_
  12.1 0.7 %collective-permute-start.3 = (bf16[64,1024]{1,0:T(8,128)(2,1)S(1)}, bf16[64,1024]{1,0:T(8,128)(2,1)S(1)}, u32[]{:S(2)}, u32[]{:S(2)}) collective-permute-start(bf16[64,1024]{1,0:T(8,128)(2,1)S(1)} %collective-permute-done.2.refs_2_), channel_id=1, source_target_pairs={{0,4},{1,5},{2,6},{3,7},{4,0},{5,1},{6,2},{7,3},{8,12},{9,13},{10,... | collective-permute-start | bytes 393224 | tf_op jit(solution)/shard_map/ppermute | solution.py:27
  12.8 0.0 copy-start
  12.8 0.9 %copy-done = bf16[1,1024,128]{2,1,0:T(8,128)(2,1)S(1)} copy-done((bf16[1,1024,128]{2,1,0:T(8,128)(2,1)S(1)}, bf16[1,1024,128]{2,1,0:T(8,128)(2,1)}, u32[]{:S(2)}) %copy-start) | copy-done | bytes 262168
  13.7 0.0 copy-start.1
  13.7 0.9 %copy-done.1 = bf16[1,1,1024,128]{3,2,1,0:T(8,128)(2,1)S(1)} copy-done((bf16[1,1,1024,128]{3,2,1,0:T(8,128)(2,1)S(1)}, bf16[1,1,1024,128]{3,2,1,0:T(8,128)(2,1)}, u32[]{:S(2)}) %copy-start.1) | copy-done | bytes 262168
  14.7 0.0 copy-start.2
  14.7 0.9 %copy-done.2 = bf16[1,64,1024]{2,1,0:T(8,128)(2,1)S(1)} copy-done((bf16[1,64,1024]{2,1,0:T(8,128)(2,1)S(1)}, bf16[1,64,1024]{2,1,0:T(8,128)(2,1)}, u32[]{:S(2)}) %copy-start.2) | copy-done | bytes 131096
  15.6 0.6 %stage_inputs.1 = (bf16[1024,128]{1,0:T(8,128)(2,1)S(1)}, bf16[1024,128]{1,0:T(8,128)(2,1)S(1)}, bf16[64,1024]{1,0:T(8,128)(2,1)S(1)}, bf16[1280,128]{1,0:T(8,12...) custom-call(bf16[1024,128]{1,0:T(8,128)(2,1)S(1)} %bitcast.6, bf16[1024,128]{1,0:T(8,128)(2,1)S(1)} %bitcast.11, ...), custom_call_target="tpu_custom_call" | custom-call | bytes 3276800 | tf_op jit(solution)/shard_map/stage_inputs/pallas_call | solution.py:109
  16.2 0.0 collective-permute-done.1.refs_1_
  16.2 2.5 %collective-permute-done.3.refs_3_ = bf16[64,1024]{1,0:T(8,128)(2,1)S(1)} collective-permute-done((bf16[64,1024]{1,0:T(8,128)(2,1)S(1)}, bf16[64,1024]{1,0:T(8,128)(2,1)S(1)}, u32[]{:S(2)}, u32[]{:S(2)}) %collective-permute-start.3) | collective-permute-done | bytes 131104 | tf_op jit(solution)/shard_map/ppermute | solution.py:27
  18.7 0.0 collective-permute-done.4.refs_5_.refs_1_
  18.7 0.0 collective-permute-done.5.refs_6_.refs_2_
  18.7 0.1 collective-permute-done.6.refs_7_.refs_3_
  18.8 0.7 %rq_pieces.1 = (f32[256,128]{1,0:T(8,128)S(1)}, bf16[256,128]{1,0:T(8,128)(2,1)S(1)}, bf16[256,128]{1,0:T(8,128)(2,1)S(1)}, bf16[256,128]{1,0:T(8,128)(2,1)S(1)}) custom-call(bf16[64,1024]{1,0:T(8,128)(2,1)S(1)} %get-tuple-element.17.refs_0_, bf16[64,1024]{1,0:T(8,128)(2,1)S(1)} %collective-permute-done.1.refs_1_, ...), custom_call_target="tpu_custom_call" | custom-call | flops 268435456 | bytes 1572864 | tf_op jit(solution)/shard_map/rq_pieces/pallas_call | solution.py:143
  19.5 1.2 %collective-permute-start.7 = (bf16[256,128]{1,0:T(8,128)(2,1)S(1)}, bf16[256,128]{1,0:T(8,128)(2,1)S(1)}, u32[]{:S(2)}, u32[]{:S(2)}) collective-permute-start(bf16[256,128]{1,0:T(8,128)(2,1)S(1)} %get-tuple-element.20), channel_id=1, source_target_pairs={{0,1},{1,0},{2,3},{3,2},{4,5},{5,4},{6,7},{7,6},{8,9},{9,8},{10,11... | collective-permute-start | bytes 196616 | tf_op jit(solution)/shard_map/ppermute | solution.py:27
  20.8 0.7 %collective-permute-start.8 = (bf16[256,128]{1,0:T(8,128)(2,1)S(1)}, bf16[256,128]{1,0:T(8,128)(2,1)S(1)}, u32[]{:S(2)}, u32[]{:S(2)}) collective-permute-start(bf16[256,128]{1,0:T(8,128)(2,1)S(1)} %get-tuple-element.21), channel_id=1, source_target_pairs={{0,2},{1,3},{2,0},{3,1},{4,6},{5,7},{6,4},{7,5},{8,10},{9,11},{10,... | collective-permute-start | bytes 196616 | tf_op jit(solution)/shard_map/ppermute | solution.py:27
  21.5 0.8 %collective-permute-start.9 = (bf16[256,128]{1,0:T(8,128)(2,1)S(1)}, bf16[256,128]{1,0:T(8,128)(2,1)S(1)}, u32[]{:S(2)}, u32[]{:S(2)}) collective-permute-start(bf16[256,128]{1,0:T(8,128)(2,1)S(1)} %get-tuple-element.22), channel_id=1, source_target_pairs={{0,3},{1,2},{2,1},{3,0},{4,7},{5,6},{6,5},{7,4},{8,11},{9,10},{10,... | collective-permute-start | bytes 196616 | tf_op jit(solution)/shard_map/ppermute | solution.py:27
  22.2 2.2 %stage_weights.1.refs_5_.refs_6_ = bf16[2,1024,1024]{2,1,0:T(8,128)(2,1)S(1)} custom-call(bf16[2,1024,1024]{2,1,0:T(8,128)(2,1)} %bitcast.15), custom_call_target="tpu_custom_call" | custom-call | bytes 8388608 | tf_op jit(solution)/shard_map/stage_weights/pallas_call | solution.py:78
  24.5 0.0 collective-permute-done.7.refs_2_.refs_3_
  24.5 0.0 collective-permute-done.8.refs_3_.refs_4_
  24.5 1.6 %collective-permute-done.9.refs_4_.refs_5_ = bf16[256,128]{1,0:T(8,128)(2,1)S(1)} collective-permute-done((bf16[256,128]{1,0:T(8,128)(2,1)S(1)}, bf16[256,128]{1,0:T(8,128)(2,1)S(1)}, u32[]{:S(2)}, u32[]{:S(2)}) %collective-permute-start.9) | collective-permute-done | bytes 65568 | tf_op jit(solution)/shard_map/ppermute | solution.py:27
  26.1 1.3 %advance.2 = bf16[1024,128]{1,0:T(8,128)(2,1)S(1)} custom-call(bf16[1024,128]{1,0:T(8,128)(2,1)S(1)} %get-tuple-element.16.refs_0_.refs_8_, f32[256,128]{1,0:T(8,128)S(1)} %get-tuple-element.19.refs_1_.refs_2_, bf16[256,128]{1,0:T(8,128)(2,1)S(1)} %collective-permute-done.7.refs_2_.refs_3_, bf16[256,128]{1,0:T(8,128)(2,1)S(1)} %collective-permute-done.8.refs_3_.refs_4_, ...), custom_call_target="tpu_custom_call" | custom-call | flops 536870912 | bytes 4194304 | tf_op jit(solution)/shard_map/advance/pallas_call | solution.py:222
  27.4 3.0 %collective-permute-start.10 = (bf16[1024,128]{1,0:T(8,128)(2,1)S(1)}, bf16[1024,128]{1,0:T(8,128)(2,1)S(1)}, u32[]{:S(2)}, u32[]{:S(2)}) collective-permute-start(bf16[1024,128]{1,0:T(8,128)(2,1)S(1)} %advance.2), channel_id=1, source_target_pairs={{0,16},{1,17},{2,18},{3,19},{4,20},{5,21},{6,22},{7,23},{8,24},{9,... | collective-permute-start | bytes 786440 | tf_op jit(solution)/shard_map/ppermute | solution.py:37
  30.4 0.1 collective-permute-start.11
  30.5 2.0 %collective-permute-start.14 = (bf16[1280,128]{1,0:T(8,128)(2,1)S(1)}, bf16[1280,128]{1,0:T(8,128)(2,1)S(1)}, u32[]{:S(2)}, u32[]{:S(2)}) collective-permute-start(bf16[1280,128]{1,0:T(8,128)(2,1)S(1)} %get-tuple-element.23), channel_id=1, source_target_pairs={{16,4},{17,5},{18,6},{19,7},{20,0},{21,1},{22,2},{23,3},{24,12},{2... | collective-permute-start | bytes 983048 | tf_op jit(solution)/shard_map/ppermute | solution.py:45
  32.5 1.0 %collective-permute-start.15 = (bf16[1280,128]{1,0:T(8,128)(2,1)S(1)}, bf16[1280,128]{1,0:T(8,128)(2,1)S(1)}, u32[]{:S(2)}, u32[]{:S(2)}) collective-permute-start(bf16[1280,128]{1,0:T(8,128)(2,1)S(1)} %get-tuple-element.24), channel_id=1, source_target_pairs={{16,8},{17,9},{18,10},{19,11},{20,12},{21,13},{22,14},{23,15},{24,... | collective-permute-start | bytes 983048 | tf_op jit(solution)/shard_map/ppermute | solution.py:45
  33.5 1.6 %collective-permute-start.16 = (bf16[1280,128]{1,0:T(8,128)(2,1)S(1)}, bf16[1280,128]{1,0:T(8,128)(2,1)S(1)}, u32[]{:S(2)}, u32[]{:S(2)}) collective-permute-start(bf16[1280,128]{1,0:T(8,128)(2,1)S(1)} %get-tuple-element.25), channel_id=1, source_target_pairs={{16,12},{17,13},{18,14},{19,15},{20,8},{21,9},{22,10},{23,11},{24,... | collective-permute-start | bytes 983048 | tf_op jit(solution)/shard_map/ppermute | solution.py:45
  35.0 0.0 collective-permute-done.10.refs_1_.refs_4_
  35.0 0.0 collective-permute-start.12
  35.0 1.4 %collective-permute-done.11.refs_5_ = bf16[1024,128]{1,0:T(8,128)(2,1)S(1)} collective-permute-done((bf16[1024,128]{1,0:T(8,128)(2,1)S(1)}, bf16[1024,128]{1,0:T(8,128)(2,1)S(1)}, u32[]{:S(2)}, u32[]{:S(2)}) %collective-permute-start.11) | collective-permute-done | bytes 262176 | tf_op jit(solution)/shard_map/ppermute | solution.py:37
  36.5 0.0 collective-permute-start.13
  36.5 7.4 %collective-permute-done.12.refs_6_ = bf16[1024,128]{1,0:T(8,128)(2,1)S(1)} collective-permute-done((bf16[1024,128]{1,0:T(8,128)(2,1)S(1)}, bf16[1024,128]{1,0:T(8,128)(2,1)S(1)}, u32[]{:S(2)}, u32[]{:S(2)}) %collective-permute-start.12) | collective-permute-done | bytes 262176 | tf_op jit(solution)/shard_map/ppermute | solution.py:37
  43.9 0.0 collective-permute-done.13.refs_7_
  43.9 0.0 collective-permute-done.14.refs_9_
  43.9 0.0 collective-permute-done.15.refs_10_
  44.0 0.0 collective-permute-done.16.refs_11_
  44.0 0.5 picture_parts.1
  44.5 5.6 %collective-permute-start.17 = (bf16[64,1024]{1,0:T(8,128)(2,1)S(1)}, bf16[64,1024]{1,0:T(8,128)(2,1)S(1)}, u32[]{:S(2)}, u32[]{:S(2)}) collective-permute-start(bf16[64,1024]{1,0:T(8,128)(2,1)S(1)} %get-tuple-element.27), channel_id=1, source_target_pairs={{0,1},{1,0},{2,3},{3,2},{4,5},{5,4},{6,7},{7,6},{8,9},{9,8},{10,11... | collective-permute-start | bytes 393224 | tf_op jit(solution)/shard_map/ppermute | solution.py:55
  50.1 0.1 collective-permute-start.18
  50.1 2.1 %collective-permute-start.19 = (bf16[64,1024]{1,0:T(8,128)(2,1)S(1)}, bf16[64,1024]{1,0:T(8,128)(2,1)S(1)}, u32[]{:S(2)}, u32[]{:S(2)}) collective-permute-start(bf16[64,1024]{1,0:T(8,128)(2,1)S(1)} %get-tuple-element.29), channel_id=1, source_target_pairs={{0,3},{1,2},{2,1},{3,0},{4,7},{5,6},{6,5},{7,4},{8,11},{9,10},{10,... | collective-permute-start | bytes 393224 | tf_op jit(solution)/shard_map/ppermute | solution.py:55
  52.2 2.1 %advance.3 = bf16[1024,128]{1,0:T(8,128)(2,1)} custom-call(bf16[1024,128]{1,0:T(8,128)(2,1)S(1)} %get-tuple-element.16.refs_0_.refs_8_, bf16[1024,128]{1,0:T(8,128)(2,1)S(1)} %collective-permute-done.10.refs_1_.refs_4_, f32[256,128]{1,0:T(8,128)S(1)} %get-tuple-element.19.refs_1_.refs_2_, bf16[256,128]{1,0:T(8,128)(2,1)S(1)} %collective-permute-done.7.refs_2_.refs_3_, ...), custom_call_target="tpu_custom_call" | custom-call | flops 536870912 | bytes 4194304 | tf_op jit(solution)/shard_map/advance/pallas_call | solution.py:222
  54.3 0.0 collective-permute-done.17.refs_1_
  54.3 3.3 %collective-permute-done.18.refs_2_ = bf16[64,1024]{1,0:T(8,128)(2,1)S(1)} collective-permute-done((bf16[64,1024]{1,0:T(8,128)(2,1)S(1)}, bf16[64,1024]{1,0:T(8,128)(2,1)S(1)}, u32[]{:S(2)}, u32[]{:S(2)}) %collective-permute-start.18) | collective-permute-done | bytes 131104 | tf_op jit(solution)/shard_map/ppermute | solution.py:55
  57.6 0.0 collective-permute-done.19.refs_3_
  57.6 0.8 %sum_parts.1 = f32[64,1024]{1,0:T(8,128)} custom-call(f32[64,1024]{1,0:T(8,128)S(1)} %get-tuple-element.26.refs_0_, bf16[64,1024]{1,0:T(8,128)(2,1)S(1)} %collective-permute-done.17.refs_1_, bf16[64,1024]{1,0:T(8,128)(2,1)S(1)} %collective-permute-done.18.refs_2_, bf16[64,1024]{1,0:T(8,128)(2,1)S(1)} %collective-permute-done.19.refs_3_), custom_call_target="tpu_custom_call" | custom-call | flops 524288 | bytes 1048576 | tf_op jit(solution)/shard_map/sum_parts/pallas_call | solution.py:306
Async XLA Ops:
  0.6 11.4 %collective-permute-start = (bf16[1024,128]{1,0:T(8,128)(2,1)}, bf16[1024,128]{1,0:T(8,128)(2,1)S(1)}, u32[]{:S(2)}, u32[]{:S(2)}) collective-permute-start(bf16[1024,128]{1,0:T(8,128)(2,1)} %bitcast.7), channel_id=1, source_target_pairs={{0,16},{1,17},{2,18},{3,19},{4,20},{5,21},{6,22},{7,23},{8,24},{9,... | collective-permute-start | bytes 786440 | tf_op jit(solution)/shard_map/ppermute | solution.py:37
  0.7 10.6 %collective-permute-start.2 = (bf16[64,1024]{1,0:T(8,128)(2,1)}, bf16[64,1024]{1,0:T(8,128)(2,1)S(1)}, u32[]{:S(2)}, u32[]{:S(2)}) collective-permute-start(bf16[64,1024]{1,0:T(8,128)(2,1)} %bitcast.12), channel_id=1, source_target_pairs={{0,8},{1,9},{2,10},{3,11},{4,12},{5,13},{6,14},{7,15},{8,0},{9,1},... | collective-permute-start | bytes 393224 | tf_op jit(solution)/shard_map/ppermute | solution.py:27
  4.5 14.2 %collective-permute-start.4 = (bf16[1024,128]{1,0:T(8,128)(2,1)}, bf16[1024,128]{1,0:T(8,128)(2,1)S(1)}, u32[]{:S(2)}, u32[]{:S(2)}) collective-permute-start(bf16[1024,128]{1,0:T(8,128)(2,1)} %bitcast.8), channel_id=1, source_target_pairs={{0,1},{1,0},{2,3},{3,2},{4,5},{5,4},{6,7},{7,6},{8,9},{9,8},{10,11... | collective-permute-start | bytes 786440 | tf_op jit(solution)/shard_map/ppermute | solution.py:27
  5.7 13.0 %collective-permute-start.5 = (bf16[1024,128]{1,0:T(8,128)(2,1)}, bf16[1024,128]{1,0:T(8,128)(2,1)S(1)}, u32[]{:S(2)}, u32[]{:S(2)}) collective-permute-start(bf16[1024,128]{1,0:T(8,128)(2,1)} %bitcast.9), channel_id=1, source_target_pairs={{0,2},{1,3},{2,0},{3,1},{4,6},{5,7},{6,4},{7,5},{8,10},{9,11},{10,... | collective-permute-start | bytes 786440 | tf_op jit(solution)/shard_map/ppermute | solution.py:27
  6.9 11.9 %collective-permute-start.6 = (bf16[1024,128]{1,0:T(8,128)(2,1)}, bf16[1024,128]{1,0:T(8,128)(2,1)S(1)}, u32[]{:S(2)}, u32[]{:S(2)}) collective-permute-start(bf16[1024,128]{1,0:T(8,128)(2,1)} %bitcast.10), channel_id=1, source_target_pairs={{0,3},{1,2},{2,1},{3,0},{4,7},{5,6},{6,5},{7,4},{8,11},{9,10},{10,... | collective-permute-start | bytes 786440 | tf_op jit(solution)/shard_map/ppermute | solution.py:27
  11.3 4.9 %collective-permute-start.1 = (bf16[64,1024]{1,0:T(8,128)(2,1)}, bf16[64,1024]{1,0:T(8,128)(2,1)S(1)}, u32[]{:S(2)}, u32[]{:S(2)}) collective-permute-start(bf16[64,1024]{1,0:T(8,128)(2,1)} %bitcast.13), channel_id=1, source_target_pairs={{0,4},{1,5},{2,6},{3,7},{4,0},{5,1},{6,2},{7,3},{8,12},{9,13},{10,... | collective-permute-start | bytes 393224 | tf_op jit(solution)/shard_map/ppermute | solution.py:27
  12.1 6.6 %collective-permute-start.3 = (bf16[64,1024]{1,0:T(8,128)(2,1)S(1)}, bf16[64,1024]{1,0:T(8,128)(2,1)S(1)}, u32[]{:S(2)}, u32[]{:S(2)}) collective-permute-start(bf16[64,1024]{1,0:T(8,128)(2,1)S(1)} %collective-permute-done.2.refs_2_), channel_id=1, source_target_pairs={{0,4},{1,5},{2,6},{3,7},{4,0},{5,1},{6,2},{7,3},{8,12},{9,13},{10,... | collective-permute-start | bytes 393224 | tf_op jit(solution)/shard_map/ppermute | solution.py:27
  12.8 0.9 %copy-start = (bf16[1,1024,128]{2,1,0:T(8,128)(2,1)S(1)}, bf16[1,1024,128]{2,1,0:T(8,128)(2,1)}, u32[]{:S(2)}) copy-start(bf16[1,1024,128]{2,1,0:T(8,128)(2,1)} %param.4) | copy-start | bytes 786436
  13.7 0.9 %copy-start.1 = (bf16[1,1,1024,128]{3,2,1,0:T(8,128)(2,1)S(1)}, bf16[1,1,1024,128]{3,2,1,0:T(8,128)(2,1)}, u32[]{:S(2)}) copy-start(bf16[1,1,1024,128]{3,2,1,0:T(8,128)(2,1)} %param.5) | copy-start | bytes 786436
  14.7 0.9 %copy-start.2 = (bf16[1,64,1024]{2,1,0:T(8,128)(2,1)S(1)}, bf16[1,64,1024]{2,1,0:T(8,128)(2,1)}, u32[]{:S(2)}) copy-start(bf16[1,64,1024]{2,1,0:T(8,128)(2,1)} %param.7) | copy-start | bytes 393220
  19.5 4.9 %collective-permute-start.7 = (bf16[256,128]{1,0:T(8,128)(2,1)S(1)}, bf16[256,128]{1,0:T(8,128)(2,1)S(1)}, u32[]{:S(2)}, u32[]{:S(2)}) collective-permute-start(bf16[256,128]{1,0:T(8,128)(2,1)S(1)} %get-tuple-element.20), channel_id=1, source_target_pairs={{0,1},{1,0},{2,3},{3,2},{4,5},{5,4},{6,7},{7,6},{8,9},{9,8},{10,11... | collective-permute-start | bytes 196616 | tf_op jit(solution)/shard_map/ppermute | solution.py:27
  20.8 3.7 %collective-permute-start.8 = (bf16[256,128]{1,0:T(8,128)(2,1)S(1)}, bf16[256,128]{1,0:T(8,128)(2,1)S(1)}, u32[]{:S(2)}, u32[]{:S(2)}) collective-permute-start(bf16[256,128]{1,0:T(8,128)(2,1)S(1)} %get-tuple-element.21), channel_id=1, source_target_pairs={{0,2},{1,3},{2,0},{3,1},{4,6},{5,7},{6,4},{7,5},{8,10},{9,11},{10,... | collective-permute-start | bytes 196616 | tf_op jit(solution)/shard_map/ppermute | solution.py:27
  21.5 4.6 %collective-permute-start.9 = (bf16[256,128]{1,0:T(8,128)(2,1)S(1)}, bf16[256,128]{1,0:T(8,128)(2,1)S(1)}, u32[]{:S(2)}, u32[]{:S(2)}) collective-permute-start(bf16[256,128]{1,0:T(8,128)(2,1)S(1)} %get-tuple-element.22), channel_id=1, source_target_pairs={{0,3},{1,2},{2,1},{3,0},{4,7},{5,6},{6,5},{7,4},{8,11},{9,10},{10,... | collective-permute-start | bytes 196616 | tf_op jit(solution)/shard_map/ppermute | solution.py:27
  27.4 7.6 %collective-permute-start.10 = (bf16[1024,128]{1,0:T(8,128)(2,1)S(1)}, bf16[1024,128]{1,0:T(8,128)(2,1)S(1)}, u32[]{:S(2)}, u32[]{:S(2)}) collective-permute-start(bf16[1024,128]{1,0:T(8,128)(2,1)S(1)} %advance.2), channel_id=1, source_target_pairs={{0,16},{1,17},{2,18},{3,19},{4,20},{5,21},{6,22},{7,23},{8,24},{9,... | collective-permute-start | bytes 786440 | tf_op jit(solution)/shard_map/ppermute | solution.py:37
  30.4 6.1 %collective-permute-start.11 = (bf16[1024,128]{1,0:T(8,128)(2,1)S(1)}, bf16[1024,128]{1,0:T(8,128)(2,1)S(1)}, u32[]{:S(2)}, u32[]{:S(2)}) collective-permute-start(bf16[1024,128]{1,0:T(8,128)(2,1)S(1)} %advance.2), channel_id=1, source_target_pairs={{0,17},{1,16},{2,19},{3,18},{4,21},{5,20},{6,23},{7,22},{8,25},{9,... | collective-permute-start | bytes 786440 | tf_op jit(solution)/shard_map/ppermute | solution.py:37
  30.5 13.5 %collective-permute-start.14 = (bf16[1280,128]{1,0:T(8,128)(2,1)S(1)}, bf16[1280,128]{1,0:T(8,128)(2,1)S(1)}, u32[]{:S(2)}, u32[]{:S(2)}) collective-permute-start(bf16[1280,128]{1,0:T(8,128)(2,1)S(1)} %get-tuple-element.23), channel_id=1, source_target_pairs={{16,4},{17,5},{18,6},{19,7},{20,0},{21,1},{22,2},{23,3},{24,12},{2... | collective-permute-start | bytes 983048 | tf_op jit(solution)/shard_map/ppermute | solution.py:45
  32.5 11.5 %collective-permute-start.15 = (bf16[1280,128]{1,0:T(8,128)(2,1)S(1)}, bf16[1280,128]{1,0:T(8,128)(2,1)S(1)}, u32[]{:S(2)}, u32[]{:S(2)}) collective-permute-start(bf16[1280,128]{1,0:T(8,128)(2,1)S(1)} %get-tuple-element.24), channel_id=1, source_target_pairs={{16,8},{17,9},{18,10},{19,11},{20,12},{21,13},{22,14},{23,15},{24,... | collective-permute-start | bytes 983048 | tf_op jit(solution)/shard_map/ppermute | solution.py:45
  33.5 10.5 %collective-permute-start.16 = (bf16[1280,128]{1,0:T(8,128)(2,1)S(1)}, bf16[1280,128]{1,0:T(8,128)(2,1)S(1)}, u32[]{:S(2)}, u32[]{:S(2)}) collective-permute-start(bf16[1280,128]{1,0:T(8,128)(2,1)S(1)} %get-tuple-element.25), channel_id=1, source_target_pairs={{16,12},{17,13},{18,14},{19,15},{20,8},{21,9},{22,10},{23,11},{24,... | collective-permute-start | bytes 983048 | tf_op jit(solution)/shard_map/ppermute | solution.py:45
  35.0 8.9 %collective-permute-start.12 = (bf16[1024,128]{1,0:T(8,128)(2,1)S(1)}, bf16[1024,128]{1,0:T(8,128)(2,1)S(1)}, u32[]{:S(2)}, u32[]{:S(2)}) collective-permute-start(bf16[1024,128]{1,0:T(8,128)(2,1)S(1)} %advance.2), channel_id=1, source_target_pairs={{0,18},{1,19},{2,16},{3,17},{4,22},{5,23},{6,20},{7,21},{8,26},{9,... | collective-permute-start | bytes 786440 | tf_op jit(solution)/shard_map/ppermute | solution.py:37
  36.5 7.5 %collective-permute-start.13 = (bf16[1024,128]{1,0:T(8,128)(2,1)S(1)}, bf16[1024,128]{1,0:T(8,128)(2,1)S(1)}, u32[]{:S(2)}, u32[]{:S(2)}) collective-permute-start(bf16[1024,128]{1,0:T(8,128)(2,1)S(1)} %advance.2), channel_id=1, source_target_pairs={{0,19},{1,18},{2,17},{3,16},{4,23},{5,22},{6,21},{7,20},{8,27},{9,... | collective-permute-start | bytes 786440 | tf_op jit(solution)/shard_map/ppermute | solution.py:37
  44.5 9.9 %collective-permute-start.17 = (bf16[64,1024]{1,0:T(8,128)(2,1)S(1)}, bf16[64,1024]{1,0:T(8,128)(2,1)S(1)}, u32[]{:S(2)}, u32[]{:S(2)}) collective-permute-start(bf16[64,1024]{1,0:T(8,128)(2,1)S(1)} %get-tuple-element.27), channel_id=1, source_target_pairs={{0,1},{1,0},{2,3},{3,2},{4,5},{5,4},{6,7},{7,6},{8,9},{9,8},{10,11... | collective-permute-start | bytes 393224 | tf_op jit(solution)/shard_map/ppermute | solution.py:55
  50.1 7.5 %collective-permute-start.18 = (bf16[64,1024]{1,0:T(8,128)(2,1)S(1)}, bf16[64,1024]{1,0:T(8,128)(2,1)S(1)}, u32[]{:S(2)}, u32[]{:S(2)}) collective-permute-start(bf16[64,1024]{1,0:T(8,128)(2,1)S(1)} %get-tuple-element.28), channel_id=1, source_target_pairs={{0,2},{1,3},{2,0},{3,1},{4,6},{5,7},{6,4},{7,5},{8,10},{9,11},{10,... | collective-permute-start | bytes 393224 | tf_op jit(solution)/shard_map/ppermute | solution.py:55
  50.1 7.5 %collective-permute-start.19 = (bf16[64,1024]{1,0:T(8,128)(2,1)S(1)}, bf16[64,1024]{1,0:T(8,128)(2,1)S(1)}, u32[]{:S(2)}, u32[]{:S(2)}) collective-permute-start(bf16[64,1024]{1,0:T(8,128)(2,1)S(1)} %get-tuple-element.29), channel_id=1, source_target_pairs={{0,3},{1,2},{2,1},{3,0},{4,7},{5,6},{6,5},{7,4},{8,11},{9,10},{10,... | collective-permute-start | bytes 393224 | tf_op jit(solution)/shard_map/ppermute | solution.py:55

commit v3 on v2

--- a/solution.py
+++ b/solution.py
@@ -11,7 +11,8 @@
 VMEM = pl.BlockSpec(memory_space=pltpu.VMEM)
 MIB = 1 << 20
 STAGE_LIMIT = 47 * MIB
-HALVES = 1
+HALVES = 2
+JOINED = (1,)
 TWO_STEP = False
 
 
@@ -179,6 +180,7 @@
 def advance_kernel(line, plane, counts, *refs):
     top, moved, refs = refs[0], refs[1 : 1 + counts[0]], refs[1 + counts[0] :]
     pieces, weights, outs, diff = refs[:plane], refs[plane], refs[plane + 1 : -1], refs[-1]
+    outs, whole = outs[: counts[1]], outs[-1]
     me = lax.axis_index("freq")
     first = lax.axis_index("depth") == 0
     rows = top.shape[0] // (line * plane)
@@ -200,10 +202,7 @@
         if not moved:
             diff[...] = jnp.zeros_like(diff)
             return
-        tall = top.shape[0] // len(moved)
-        for h, part in enumerate(moved):
-            diff[h * tall : (h + 1) * tall, :] = part[...]
-        subtract(diff)
+        subtract(moved[0])
 
     straight = diff[...]
     half = cols // 2
@@ -211,19 +210,25 @@
     tall = top.shape[0] // counts[1]
     for h, out in enumerate(outs):
         part = slice(h * tall, (h + 1) * tall)
-        out[...] = (
+        below = (
             jnp.dot(weights[0, part, :], straight, preferred_element_type=jnp.float32)
             + jnp.dot(weights[1, part, :], turned, preferred_element_type=jnp.float32)
         ).astype(jnp.bfloat16)
+        out[...] = below
+        if counts[1] > 1:
+            whole[part, :] = below
 
 
 def advance(top, moved, pieces, weights, line, plane, parts):
     nx, cols = top.shape
+    outs = [jax.ShapeDtypeStruct((nx // parts, cols), jnp.bfloat16)] * parts
+    if parts > 1:
+        outs.append(jax.ShapeDtypeStruct((nx, cols), jnp.bfloat16))
     return pl.pallas_call(
         functools.partial(advance_kernel, line, plane, (len(moved), parts)),
-        out_shape=[jax.ShapeDtypeStruct((nx // parts, cols), jnp.bfloat16)] * parts,
+        out_shape=outs,
         in_specs=[VMEM] * (2 + len(moved) + plane),
-        out_specs=[VMEM] * parts,
+        out_specs=[VMEM] * len(outs),
         scratch_shapes=[pltpu.VMEM((nx, cols), jnp.bfloat16)],
         compiler_params=params(24 * MIB),
         cost_estimate=pl.CostEstimate(flops=4 * nx * nx * cols, bytes_accessed=4 * nx * nx, transcendentals=0),
@@ -239,9 +244,10 @@
     return jnp.concatenate([ref[pl.ds(pl.multiple_of(s, rows), rows), :] for s in starts], axis=0)
 
 
-def picture_kernel(line, plane, part, *refs):
+def picture_kernel(line, plane, part, joined, *refs):
     ups, fields, refs = refs[:plane], refs[plane : 2 * plane], refs[2 * plane :]
-    top, loads, outs = refs[0], refs[1:line], refs[line:]
+    top, loads, refs = refs[0], refs[1:line], refs[line:]
+    earlier, outs = (refs[: len(joined)], refs[len(joined) :]) if part.start else ((), refs)
     me = lax.axis_index("freq")
     first = lax.axis_index("depth") == 0
     nx = top.shape[0]
@@ -251,7 +257,10 @@
         total = lax.dot_general(left, right, (((1,), (1,)), ((), ())), preferred_element_type=jnp.float32)
         for k, out in enumerate(outs):
             if k < count:
-                out[...] = total[k * rows : (k + 1) * rows].astype(out.dtype)
+                out[:, part if k in joined else slice(None)] = total[k * rows : (k + 1) * rows].astype(out.dtype)
+
+    for k, before in zip(joined, earlier):
+        outs[k][:, : part.start] = before[...]
 
     @pl.when(first)
     def _():
@@ -266,52 +275,55 @@
     def _():
         starts = [(me ^ (z * plane)) * rows for z in range(line)]
         lefts = [stacked_rows(up, starts, rows) for up in ups]
-        write(side_by_side(lefts), side_by_side([f[...] for f in fields]), line)
-
-
-def picture_parts(ups, fields, top, loads, plane, line, h):
+        write(side_by_side(lefts), side_by_side([fields[0][part, :]] + [f[...] for f in fields[1:]]), line)
+
+
+def picture_parts(ups, fields, top, loads, plane, line, h, earlier):
     nx, cols = top.shape
     rows = nx // (line * plane)
-    wide = fields[0].shape[0]
+    wide = nx // HALVES
     count = max(line, plane)
     out_shape = [jax.ShapeDtypeStruct((rows, wide), jnp.float32)]
-    out_shape += [jax.ShapeDtypeStruct((rows, wide), jnp.bfloat16)] * (count - 1)
+    for k in range(1, count):
+        out_shape.append(jax.ShapeDtypeStruct((rows, wide * (h + 1) if k in JOINED else wide), jnp.bfloat16))
+    before = [earlier[k] for k in JOINED] if h else []
     return pl.pallas_call(
-        functools.partial(picture_kernel, line, plane, slice(h * wide, (h + 1) * wide)),
+        functools.partial(picture_kernel, line, plane, slice(h * wide, (h + 1) * wide), JOINED),
         out_shape=out_shape,
-        in_specs=[VMEM] * (2 * plane + line),
+        in_specs=[VMEM] * (2 * plane + line + len(before)),
         out_specs=[VMEM] * count,
         compiler_params=params(24 * MIB),
         cost_estimate=pl.CostEstimate(
             flops=2 * line * rows * wide * cols * plane, bytes_accessed=4 * nx * cols * plane, transcendentals=0
         ),
         name="picture_parts",
-    )(*ups, *fields, top, *loads)
-
-
-def sum_kernel(scale, halves, count, *refs):
-    out = refs[-1]
+    )(*ups, *fields, top, *loads, *before)
+
+
+def sum_kernel(scale, counts, *refs):
+    joined, refs, out = refs[: counts[0]], refs[counts[0] : -1], refs[-1]
     wide = refs[0].shape[1]
-    for h in range(halves):
-        part = refs[h * count : (h + 1) * count]
+    for h in range(len(refs) // counts[1]):
+        part = refs[h * counts[1] : (h + 1) * counts[1]]
+        at = slice(h * wide, (h + 1) * wide)
         total = part[0][...]
-        for ref in part[1:]:
-            total = total + ref[...].astype(jnp.float32)
-        out[:, h * wide : (h + 1) * wide] = total * scale
-
-
-def summed(parts, scale):
+        for value in [ref[...] for ref in part[1:]] + [ref[:, at] for ref in joined]:
+            total = total + value.astype(jnp.float32)
+        out[:, at] = total * scale
+
+
+def summed(joined, parts, scale):
     halves, count = len(parts), len(parts[0])
     rows, wide = parts[0][0].shape
     return pl.pallas_call(
-        functools.partial(sum_kernel, scale, halves, count),
+        functools.partial(sum_kernel, scale, (len(joined), count)),
         out_shape=jax.ShapeDtypeStruct((rows, halves * wide), jnp.float32),
-        in_specs=[VMEM] * (halves * count),
+        in_specs=[VMEM] * (len(joined) + halves * count),
         out_specs=VMEM,
         compiler_params=params(8 * MIB),
         cost_estimate=pl.CostEstimate(flops=rows * wide * 8, bytes_accessed=rows * wide * 16, transcendentals=0),
         name="sum_parts",
-    )(*[ref for part in parts for ref in part])
+    )(*joined, *[ref for part in parts for ref in part])
 
 
 def local(p_top, upgoing, extrapolator, reflectivity):
@@ -336,16 +348,18 @@
 
     moved = []
     for _ in range(1, sections):
-        below = advance(top, moved, pieces, weights, line, plane, HALVES)
-        moved = [lower(half, 0) for half in below]
+        *halves, below = advance(top, moved, pieces, weights, line, plane, HALVES)
+        moved = [lower(below, 0)]
     scale = (float(upper.shape[1]) * devices) ** (-0.5)
-    sums = []
+    parts, sums = None, []
     for h in range(HALVES):
-        fields = [moved[h]] + [lower(below[h], q) for q in range(1, plane)]
-        parts = picture_parts(ups, fields, top, loads, plane, line, h)
-        sums.append([parts[0]] + [reduce_step(parts[k], k, plane, line) for k in range(1, len(parts))])
+        fields = moved + [lower(halves[h], q) for q in range(1, plane)]
+        parts = picture_parts(ups, fields, top, loads, plane, line, h, parts)
+        alone = [k for k in range(1, len(parts)) if k not in JOINED]
+        sums.append([parts[0]] + [reduce_step(parts[k], k, plane, line) for k in alone])
+    joined = [reduce_step(parts[k], k, plane, line) for k in JOINED]
     (below,) = advance(top, moved, pieces, weights, line, plane, 1)
-    return (below[None, None], summed(sums, scale)[None])
+    return (below[None, None], summed(joined, sums, scale)[None])
 
 
 def solution(mesh):

time: 58.6 us -> 60.1 us (1.026)
  the two profiles are of different devices: /device:TPU:1 before, /device:TPU:8 now
where the time goes in v3:
time: 60.1 us; the launch traced here: 59.9 us
  starting transfers between devices  27 us (45%)
  waiting for transfers between devices  21 us (35%)
  Pallas kernels  8.41 us (14%)
  local copies, waits for them, and re-layouts  2.8 us (5%)
  between operations  0.75 us (1%)
    ppermute x9, starting transfers between devices, swap(): return lax.ppermute(value, 'freq', [(i, i ^ by) for i in range(devices)])  11.7 us
    ppermute x9, waiting for transfers between devices, swap(): return lax.ppermute(value, 'freq', [(i, i ^ by) for i in range(devices)])  8.39 us
    ppermute x8, starting transfers between devices, lower(): return lax.ppermute(value, ('depth', 'freq'), pairs)  6.78 us
    ppermute x3, waiting for transfers between devices, raise_top(): return lax.ppermute(value, ('depth', 'freq'), pairs)  6.52 us
    ppermute x5, starting transfers between devices, reduce_step(): return lax.ppermute(value, ('depth', 'freq'), pairs)  5.57 us
    ppermute x8, waiting for transfers between devices, lower(): return lax.ppermute(value, ('depth', 'freq'), pairs)  3.51 us
    pallas_call x2, Pallas kernels, advance(): pl.pallas_call(functools.partial(advance_kernel, line, plane, (len(moved)...  3.44 us
    ppermute x3, starting transfers between devices, raise_top(): return lax.ppermute(value, ('depth', 'freq'), pairs)  2.89 us
  transfers between devices with their start and end apart: 25, of which 11 were waited for; matrix products, arithmetic and copies ran while one was open for 0% of the time, Pallas kernels for 9%

profile of v3, /device:TPU:8, one launch (start us, length us, event | category | flops | bytes accessed | tf_op | source)
XLA Modules:
  0.0 59.9 jit_solution(10197689623880703604)
XLA Ops:
  0.6 0.1 collective-permute-start
  0.7 2.7 %collective-permute-start.2 = (bf16[64,1024]{1,0:T(8,128)(2,1)}, bf16[64,1024]{1,0:T(8,128)(2,1)S(1)}, u32[]{:S(2)}, u32[]{:S(2)}) collective-permute-start(bf16[64,1024]{1,0:T(8,128)(2,1)} %bitcast.12), channel_id=1, source_target_pairs={{0,8},{1,9},{2,10},{3,11},{4,12},{5,13},{6,14},{7,15},{8,0},{9,1},... | collective-permute-start | bytes 393224 | tf_op jit(solution)/shard_map/ppermute | solution.py:28
  3.4 1.5 %collective-permute-start.4 = (bf16[1024,128]{1,0:T(8,128)(2,1)}, bf16[1024,128]{1,0:T(8,128)(2,1)S(1)}, u32[]{:S(2)}, u32[]{:S(2)}) collective-permute-start(bf16[1024,128]{1,0:T(8,128)(2,1)} %bitcast.8), channel_id=1, source_target_pairs={{0,1},{1,0},{2,3},{3,2},{4,5},{5,4},{6,7},{7,6},{8,9},{9,8},{10,11... | collective-permute-start | bytes 786440 | tf_op jit(solution)/shard_map/ppermute | solution.py:28
  4.9 1.5 %collective-permute-start.5 = (bf16[1024,128]{1,0:T(8,128)(2,1)}, bf16[1024,128]{1,0:T(8,128)(2,1)S(1)}, u32[]{:S(2)}, u32[]{:S(2)}) collective-permute-start(bf16[1024,128]{1,0:T(8,128)(2,1)} %bitcast.9), channel_id=1, source_target_pairs={{0,2},{1,3},{2,0},{3,1},{4,6},{5,7},{6,4},{7,5},{8,10},{9,11},{10,... | collective-permute-start | bytes 786440 | tf_op jit(solution)/shard_map/ppermute | solution.py:28
  6.4 0.5 collective-permute-start.6
  6.9 2.9 %collective-permute-done.2.refs_2_ = bf16[64,1024]{1,0:T(8,128)(2,1)S(1)} collective-permute-done((bf16[64,1024]{1,0:T(8,128)(2,1)}, bf16[64,1024]{1,0:T(8,128)(2,1)S(1)}, u32[]{:S(2)}, u32[]{:S(2)}) %collective-permute-start.2) | collective-permute-done | bytes 131104 | tf_op jit(solution)/shard_map/ppermute | solution.py:28
  9.7 1.2 %collective-permute-start.1 = (bf16[64,1024]{1,0:T(8,128)(2,1)}, bf16[64,1024]{1,0:T(8,128)(2,1)S(1)}, u32[]{:S(2)}, u32[]{:S(2)}) collective-permute-start(bf16[64,1024]{1,0:T(8,128)(2,1)} %bitcast.13), channel_id=1, source_target_pairs={{0,4},{1,5},{2,6},{3,7},{4,0},{5,1},{6,2},{7,3},{8,12},{9,13},{10,... | collective-permute-start | bytes 393224 | tf_op jit(solution)/shard_map/ppermute | solution.py:28
  10.9 0.0 collective-permute-done.refs_3_
  10.9 0.8 %collective-permute-start.3 = (bf16[64,1024]{1,0:T(8,128)(2,1)S(1)}, bf16[64,1024]{1,0:T(8,128)(2,1)S(1)}, u32[]{:S(2)}, u32[]{:S(2)}) collective-permute-start(bf16[64,1024]{1,0:T(8,128)(2,1)S(1)} %collective-permute-done.2.refs_2_), channel_id=1, source_target_pairs={{0,4},{1,5},{2,6},{3,7},{4,0},{5,1},{6,2},{7,3},{8,12},{9,13},{10,... | collective-permute-start | bytes 393224 | tf_op jit(solution)/shard_map/ppermute | solution.py:28
  11.8 0.0 copy-start
  11.8 0.9 %copy-done = bf16[1,1024,128]{2,1,0:T(8,128)(2,1)S(1)} copy-done((bf16[1,1024,128]{2,1,0:T(8,128)(2,1)S(1)}, bf16[1,1024,128]{2,1,0:T(8,128)(2,1)}, u32[]{:S(2)}) %copy-start) | copy-done | bytes 262168
  12.7 0.0 copy-start.1
  12.7 0.9 %copy-done.1 = bf16[1,1,1024,128]{3,2,1,0:T(8,128)(2,1)S(1)} copy-done((bf16[1,1,1024,128]{3,2,1,0:T(8,128)(2,1)S(1)}, bf16[1,1,1024,128]{3,2,1,0:T(8,128)(2,1)}, u32[]{:S(2)}) %copy-start.1) | copy-done | bytes 262168
  13.7 0.0 copy-start.2
  13.7 0.9 %copy-done.2 = bf16[1,64,1024]{2,1,0:T(8,128)(2,1)S(1)} copy-done((bf16[1,64,1024]{2,1,0:T(8,128)(2,1)S(1)}, bf16[1,64,1024]{2,1,0:T(8,128)(2,1)}, u32[]{:S(2)}) %copy-start.2) | copy-done | bytes 131096
  14.6 0.6 %stage_inputs.1 = (bf16[1024,128]{1,0:T(8,128)(2,1)S(1)}, bf16[1024,128]{1,0:T(8,128)(2,1)S(1)}, bf16[64,1024]{1,0:T(8,128)(2,1)S(1)}, bf16[1280,128]{1,0:T(8,12...) custom-call(bf16[1024,128]{1,0:T(8,128)(2,1)S(1)} %bitcast.6, bf16[1024,128]{1,0:T(8,128)(2,1)S(1)} %bitcast.11, ...), custom_call_target="tpu_custom_call" | custom-call | bytes 3276800 | tf_op jit(solution)/shard_map/stage_inputs/pallas_call | solution.py:110
  15.2 1.1 %collective-permute-done.1.refs_1_ = bf16[64,1024]{1,0:T(8,128)(2,1)S(1)} collective-permute-done((bf16[64,1024]{1,0:T(8,128)(2,1)}, bf16[64,1024]{1,0:T(8,128)(2,1)S(1)}, u32[]{:S(2)}, u32[]{:S(2)}) %collective-permute-start.1) | collective-permute-done | bytes 131104 | tf_op jit(solution)/shard_map/ppermute | solution.py:28
  16.3 1.9 %collective-permute-done.3.refs_3_ = bf16[64,1024]{1,0:T(8,128)(2,1)S(1)} collective-permute-done((bf16[64,1024]{1,0:T(8,128)(2,1)S(1)}, bf16[64,1024]{1,0:T(8,128)(2,1)S(1)}, u32[]{:S(2)}, u32[]{:S(2)}) %collective-permute-start.3) | collective-permute-done | bytes 131104 | tf_op jit(solution)/shard_map/ppermute | solution.py:28
  18.2 0.0 collective-permute-done.4.refs_5_.refs_1_
  18.2 0.5 collective-permute-done.5.refs_6_.refs_2_
  18.8 0.0 collective-permute-done.6.refs_7_.refs_3_
  18.8 0.7 %rq_pieces.1 = (f32[256,128]{1,0:T(8,128)S(1)}, bf16[256,128]{1,0:T(8,128)(2,1)S(1)}, bf16[256,128]{1,0:T(8,128)(2,1)S(1)}, bf16[256,128]{1,0:T(8,128)(2,1)S(1)}) custom-call(bf16[64,1024]{1,0:T(8,128)(2,1)S(1)} %get-tuple-element.24.refs_0_, bf16[64,1024]{1,0:T(8,128)(2,1)S(1)} %collective-permute-done.1.refs_1_, ...), custom_call_target="tpu_custom_call" | custom-call | flops 268435456 | bytes 1572864 | tf_op jit(solution)/shard_map/rq_pieces/pallas_call | solution.py:144
  19.5 1.3 %collective-permute-start.7 = (bf16[256,128]{1,0:T(8,128)(2,1)S(1)}, bf16[256,128]{1,0:T(8,128)(2,1)S(1)}, u32[]{:S(2)}, u32[]{:S(2)}) collective-permute-start(bf16[256,128]{1,0:T(8,128)(2,1)S(1)} %get-tuple-element.27), channel_id=1, source_target_pairs={{0,1},{1,0},{2,3},{3,2},{4,5},{5,4},{6,7},{7,6},{8,9},{9,8},{10,11... | collective-permute-start | bytes 196616 | tf_op jit(solution)/shard_map/ppermute | solution.py:28
  20.8 1.2 %collective-permute-start.8 = (bf16[256,128]{1,0:T(8,128)(2,1)S(1)}, bf16[256,128]{1,0:T(8,128)(2,1)S(1)}, u32[]{:S(2)}, u32[]{:S(2)}) collective-permute-start(bf16[256,128]{1,0:T(8,128)(2,1)S(1)} %get-tuple-element.28), channel_id=1, source_target_pairs={{0,2},{1,3},{2,0},{3,1},{4,6},{5,7},{6,4},{7,5},{8,10},{9,11},{10,... | collective-permute-start | bytes 196616 | tf_op jit(solution)/shard_map/ppermute | solution.py:28
  22.0 1.0 %collective-permute-start.9 = (bf16[256,128]{1,0:T(8,128)(2,1)S(1)}, bf16[256,128]{1,0:T(8,128)(2,1)S(1)}, u32[]{:S(2)}, u32[]{:S(2)}) collective-permute-start(bf16[256,128]{1,0:T(8,128)(2,1)S(1)} %get-tuple-element.29), channel_id=1, source_target_pairs={{0,3},{1,2},{2,1},{3,0},{4,7},{5,6},{6,5},{7,4},{8,11},{9,10},{10,... | collective-permute-start | bytes 196616 | tf_op jit(solution)/shard_map/ppermute | solution.py:28
  23.0 2.2 %stage_weights.1.refs_5_.refs_6_ = bf16[2,1024,1024]{2,1,0:T(8,128)(2,1)S(1)} custom-call(bf16[2,1024,1024]{2,1,0:T(8,128)(2,1)} %bitcast.15), custom_call_target="tpu_custom_call" | custom-call | bytes 8388608 | tf_op jit(solution)/shard_map/stage_weights/pallas_call | solution.py:79
  25.2 0.0 collective-permute-done.7.refs_2_.refs_3_
  25.2 0.4 collective-permute-done.8.refs_3_.refs_4_
  25.6 1.5 %collective-permute-done.9.refs_4_.refs_5_ = bf16[256,128]{1,0:T(8,128)(2,1)S(1)} collective-permute-done((bf16[256,128]{1,0:T(8,128)(2,1)S(1)}, bf16[256,128]{1,0:T(8,128)(2,1)S(1)}, u32[]{:S(2)}, u32[]{:S(2)}) %collective-permute-start.9) | collective-permute-done | bytes 65568 | tf_op jit(solution)/shard_map/ppermute | solution.py:28
  27.2 1.4 %advance.2 = (bf16[512,128]{1,0:T(8,128)(2,1)S(1)}, bf16[512,128]{1,0:T(8,128)(2,1)S(1)}, bf16[1024,128]{1,0:T(8,128)(2,1)S(1)}) custom-call(bf16[1024,128]{1,0:T(8,128)(2,1)S(1)} %get-tuple-element.23.refs_0_.refs_8_, f32[256,128]{1,0:T(8,128)S(1)} %get-tuple-element.26.refs_1_.refs_2_, bf16[256,128]{1,0:T(8,128)(2,1)S(1)} %collective-permute-done.7.refs_2_.refs_3_, ...), custom_call_target="tpu_custom_call" | custom-call | flops 536870912 | bytes 4194304 | tf_op jit(solution)/shard_map/advance/pallas_call | solution.py:227
  28.6 0.1 collective-permute-start.17
  28.6 0.5 collective-permute-start.14
  29.1 0.5 collective-permute-start.18
  29.6 0.0 collective-permute-start.10
  29.7 0.5 collective-permute-start.15
  30.2 1.0 %collective-permute-done.17.refs_5_ = bf16[512,128]{1,0:T(8,128)(2,1)S(1)} collective-permute-done((bf16[512,128]{1,0:T(8,128)(2,1)S(1)}, bf16[512,128]{1,0:T(8,128)(2,1)S(1)}, u32[]{:S(2)}, u32[]{:S(2)}) %collective-permute-start.17) | collective-permute-done | bytes 131104 | tf_op jit(solution)/shard_map/ppermute | solution.py:38
  31.1 1.9 %collective-permute-start.16 = (bf16[1280,128]{1,0:T(8,128)(2,1)S(1)}, bf16[1280,128]{1,0:T(8,128)(2,1)S(1)}, u32[]{:S(2)}, u32[]{:S(2)}) collective-permute-start(bf16[1280,128]{1,0:T(8,128)(2,1)S(1)} %get-tuple-element.34), channel_id=1, source_target_pairs={{16,12},{17,13},{18,14},{19,15},{20,8},{21,9},{22,10},{23,11},{24,... | collective-permute-start | bytes 983048 | tf_op jit(solution)/shard_map/ppermute | solution.py:46
  33.0 0.0 collective-permute-done.18.refs_6_
  33.0 1.5 %collective-permute-start.19 = (bf16[512,128]{1,0:T(8,128)(2,1)S(1)}, bf16[512,128]{1,0:T(8,128)(2,1)S(1)}, u32[]{:S(2)}, u32[]{:S(2)}) collective-permute-start(bf16[512,128]{1,0:T(8,128)(2,1)S(1)} %get-tuple-element.35), channel_id=1, source_target_pairs={{0,19},{1,18},{2,17},{3,16},{4,23},{5,22},{6,21},{7,20},{8,27},{9,... | collective-permute-start | bytes 393224 | tf_op jit(solution)/shard_map/ppermute | solution.py:38
  34.5 2.5 %collective-permute-done.19.refs_7_ = bf16[512,128]{1,0:T(8,128)(2,1)S(1)} collective-permute-done((bf16[512,128]{1,0:T(8,128)(2,1)S(1)}, bf16[512,128]{1,0:T(8,128)(2,1)S(1)}, u32[]{:S(2)}, u32[]{:S(2)}) %collective-permute-start.19) | collective-permute-done | bytes 131104 | tf_op jit(solution)/shard_map/ppermute | solution.py:38
  37.1 3.1 %collective-permute-start.11 = (bf16[512,128]{1,0:T(8,128)(2,1)S(1)}, bf16[512,128]{1,0:T(8,128)(2,1)S(1)}, u32[]{:S(2)}, u32[]{:S(2)}) collective-permute-start(bf16[512,128]{1,0:T(8,128)(2,1)S(1)} %get-tuple-element.31), channel_id=1, source_target_pairs={{0,17},{1,16},{2,19},{3,18},{4,21},{5,20},{6,23},{7,22},{8,25},{9,... | collective-permute-start | bytes 393224 | tf_op jit(solution)/shard_map/ppermute | solution.py:38
  40.2 0.0 collective-permute-done.10.refs_1_.refs_4_
  40.2 0.0 collective-permute-start.12
  40.2 0.0 collective-permute-done.14.refs_9_
  40.2 1.5 %collective-permute-start.13 = (bf16[512,128]{1,0:T(8,128)(2,1)S(1)}, bf16[512,128]{1,0:T(8,128)(2,1)S(1)}, u32[]{:S(2)}, u32[]{:S(2)}) collective-permute-start(bf16[512,128]{1,0:T(8,128)(2,1)S(1)} %get-tuple-element.31), channel_id=1, source_target_pairs={{0,19},{1,18},{2,17},{3,16},{4,23},{5,22},{6,21},{7,20},{8,27},{9,... | collective-permute-start | bytes 393224 | tf_op jit(solution)/shard_map/ppermute | solution.py:38
  41.7 0.0 collective-permute-done.15.refs_10_
  41.7 6.5 %collective-permute-done.16.refs_11_ = bf16[1280,128]{1,0:T(8,128)(2,1)S(1)} collective-permute-done((bf16[1280,128]{1,0:T(8,128)(2,1)S(1)}, bf16[1280,128]{1,0:T(8,128)(2,1)S(1)}, u32[]{:S(2)}, u32[]{:S(2)}) %collective-permute-start.16) | collective-permute-done | bytes 327712 | tf_op jit(solution)/shard_map/ppermute | solution.py:46
  48.2 0.3 picture_parts.2
  48.5 0.0 collective-permute-done.11.refs_5_
  48.5 0.0 collective-permute-done.12.refs_6_
  48.6 0.0 collective-permute-done.13.refs_7_
  48.6 0.4 picture_parts.3
  48.9 0.6 %collective-permute-start.20 = (bf16[64,1024]{1,0:T(8,128)(2,1)S(1)}, bf16[64,1024]{1,0:T(8,128)(2,1)S(1)}, u32[]{:S(2)}, u32[]{:S(2)}) collective-permute-start(bf16[64,1024]{1,0:T(8,128)(2,1)S(1)} %get-tuple-element.37), channel_id=1, source_target_pairs={{0,1},{1,0},{2,3},{3,2},{4,5},{5,4},{6,7},{7,6},{8,9},{9,8},{10,11... | collective-permute-start | bytes 393224 | tf_op jit(solution)/shard_map/ppermute | solution.py:56
  49.6 1.5 %collective-permute-start.21 = (bf16[64,512]{1,0:T(8,128)(2,1)S(1)}, bf16[64,512]{1,0:T(8,128)(2,1)S(1)}, u32[]{:S(2)}, u32[]{:S(2)}) collective-permute-start(bf16[64,512]{1,0:T(8,128)(2,1)S(1)} %get-tuple-element.39), channel_id=1, source_target_pairs={{0,2},{1,3},{2,0},{3,1},{4,6},{5,7},{6,4},{7,5},{8,10},{9,11},{10,... | collective-permute-start | bytes 196616 | tf_op jit(solution)/shard_map/ppermute | solution.py:56
  51.0 1.5 %collective-permute-start.22 = (bf16[64,512]{1,0:T(8,128)(2,1)S(1)}, bf16[64,512]{1,0:T(8,128)(2,1)S(1)}, u32[]{:S(2)}, u32[]{:S(2)}) collective-permute-start(bf16[64,512]{1,0:T(8,128)(2,1)S(1)} %get-tuple-element.40), channel_id=1, source_target_pairs={{0,3},{1,2},{2,1},{3,0},{4,7},{5,6},{6,5},{7,4},{8,11},{9,10},{10,... | collective-permute-start | bytes 196616 | tf_op jit(solution)/shard_map/ppermute | solution.py:56
  52.5 1.5 %collective-permute-start.23 = (bf16[64,512]{1,0:T(8,128)(2,1)S(1)}, bf16[64,512]{1,0:T(8,128)(2,1)S(1)}, u32[]{:S(2)}, u32[]{:S(2)}) collective-permute-start(bf16[64,512]{1,0:T(8,128)(2,1)S(1)} %get-tuple-element.42), channel_id=1, source_target_pairs={{0,2},{1,3},{2,0},{3,1},{4,6},{5,7},{6,4},{7,5},{8,10},{9,11},{10,... | collective-permute-start | bytes 196616 | tf_op jit(solution)/shard_map/ppermute | solution.py:56
  54.0 0.5 collective-permute-start.24
  54.5 2.1 %advance.3 = bf16[1024,128]{1,0:T(8,128)(2,1)} custom-call(bf16[1024,128]{1,0:T(8,128)(2,1)S(1)} %get-tuple-element.23.refs_0_.refs_8_, bf16[1024,128]{1,0:T(8,128)(2,1)S(1)} %collective-permute-done.10.refs_1_.refs_4_, f32[256,128]{1,0:T(8,128)S(1)} %get-tuple-element.26.refs_1_.refs_2_, bf16[256,128]{1,0:T(8,128)(2,1)S(1)} %collective-permute-done.7.refs_2_.refs_3_, ...), custom_call_target="tpu_custom_call" | custom-call | flops 536870912 | bytes 4194304 | tf_op jit(solution)/shard_map/advance/pallas_call | solution.py:227
  56.6 0.0 collective-permute-done.21.refs_2_
  56.6 0.0 collective-permute-done.22.refs_3_
  56.6 0.3 collective-permute-done.23.refs_5_
  56.9 2.2 %collective-permute-done.24.refs_6_ = bf16[64,512]{1,0:T(8,128)(2,1)S(1)} collective-permute-done((bf16[64,512]{1,0:T(8,128)(2,1)S(1)}, bf16[64,512]{1,0:T(8,128)(2,1)S(1)}, u32[]{:S(2)}, u32[]{:S(2)}) %collective-permute-start.24) | collective-permute-done | bytes 65568 | tf_op jit(solution)/shard_map/ppermute | solution.py:56
  59.1 0.0 collective-permute-done.20.refs_0_
  59.1 0.8 %sum_parts.1 = f32[64,1024]{1,0:T(8,128)} custom-call(bf16[64,1024]{1,0:T(8,128)(2,1)S(1)} %collective-permute-done.20.refs_0_, f32[64,512]{1,0:T(8,128)S(1)} %get-tuple-element.38.refs_1_, bf16[64,512]{1,0:T(8,128)(2,1)S(1)} %collective-permute-done.21.refs_2_, bf16[64,512]{1,0:T(8,128)(2,1)S(1)} %collective-permute-done.22.refs_3_, ...), custom_call_target="tpu_custom_call" | custom-call | flops 262144 | bytes 524288 | tf_op jit(solution)/shard_map/sum_parts/pallas_call | solution.py:318
Async XLA Ops:
  0.6 10.3 %collective-permute-start = (bf16[1024,128]{1,0:T(8,128)(2,1)}, bf16[1024,128]{1,0:T(8,128)(2,1)S(1)}, u32[]{:S(2)}, u32[]{:S(2)}) collective-permute-start(bf16[1024,128]{1,0:T(8,128)(2,1)} %bitcast.7), channel_id=1, source_target_pairs={{0,16},{1,17},{2,18},{3,19},{4,20},{5,21},{6,22},{7,23},{8,24},{9,... | collective-permute-start | bytes 786440 | tf_op jit(solution)/shard_map/ppermute | solution.py:38
  0.7 9.0 %collective-permute-start.2 = (bf16[64,1024]{1,0:T(8,128)(2,1)}, bf16[64,1024]{1,0:T(8,128)(2,1)S(1)}, u32[]{:S(2)}, u32[]{:S(2)}) collective-permute-start(bf16[64,1024]{1,0:T(8,128)(2,1)} %bitcast.12), channel_id=1, source_target_pairs={{0,8},{1,9},{2,10},{3,11},{4,12},{5,13},{6,14},{7,15},{8,0},{9,1},... | collective-permute-start | bytes 393224 | tf_op jit(solution)/shard_map/ppermute | solution.py:28
  3.4 14.9 %collective-permute-start.4 = (bf16[1024,128]{1,0:T(8,128)(2,1)}, bf16[1024,128]{1,0:T(8,128)(2,1)S(1)}, u32[]{:S(2)}, u32[]{:S(2)}) collective-permute-start(bf16[1024,128]{1,0:T(8,128)(2,1)} %bitcast.8), channel_id=1, source_target_pairs={{0,1},{1,0},{2,3},{3,2},{4,5},{5,4},{6,7},{7,6},{8,9},{9,8},{10,11... | collective-permute-start | bytes 786440 | tf_op jit(solution)/shard_map/ppermute | solution.py:28
  4.9 13.9 %collective-permute-start.5 = (bf16[1024,128]{1,0:T(8,128)(2,1)}, bf16[1024,128]{1,0:T(8,128)(2,1)S(1)}, u32[]{:S(2)}, u32[]{:S(2)}) collective-permute-start(bf16[1024,128]{1,0:T(8,128)(2,1)} %bitcast.9), channel_id=1, source_target_pairs={{0,2},{1,3},{2,0},{3,1},{4,6},{5,7},{6,4},{7,5},{8,10},{9,11},{10,... | collective-permute-start | bytes 786440 | tf_op jit(solution)/shard_map/ppermute | solution.py:28
  6.4 12.4 %collective-permute-start.6 = (bf16[1024,128]{1,0:T(8,128)(2,1)}, bf16[1024,128]{1,0:T(8,128)(2,1)S(1)}, u32[]{:S(2)}, u32[]{:S(2)}) collective-permute-start(bf16[1024,128]{1,0:T(8,128)(2,1)} %bitcast.10), channel_id=1, source_target_pairs={{0,3},{1,2},{2,1},{3,0},{4,7},{5,6},{6,5},{7,4},{8,11},{9,10},{10,... | collective-permute-start | bytes 786440 | tf_op jit(solution)/shard_map/ppermute | solution.py:28
  9.7 6.6 %collective-permute-start.1 = (bf16[64,1024]{1,0:T(8,128)(2,1)}, bf16[64,1024]{1,0:T(8,128)(2,1)S(1)}, u32[]{:S(2)}, u32[]{:S(2)}) collective-permute-start(bf16[64,1024]{1,0:T(8,128)(2,1)} %bitcast.13), channel_id=1, source_target_pairs={{0,4},{1,5},{2,6},{3,7},{4,0},{5,1},{6,2},{7,3},{8,12},{9,13},{10,... | collective-permute-start | bytes 393224 | tf_op jit(solution)/shard_map/ppermute | solution.py:28
  10.9 7.3 %collective-permute-start.3 = (bf16[64,1024]{1,0:T(8,128)(2,1)S(1)}, bf16[64,1024]{1,0:T(8,128)(2,1)S(1)}, u32[]{:S(2)}, u32[]{:S(2)}) collective-permute-start(bf16[64,1024]{1,0:T(8,128)(2,1)S(1)} %collective-permute-done.2.refs_2_), channel_id=1, source_target_pairs={{0,4},{1,5},{2,6},{3,7},{4,0},{5,1},{6,2},{7,3},{8,12},{9,13},{10,... | collective-permute-start | bytes 393224 | tf_op jit(solution)/shard_map/ppermute | solution.py:28
  11.8 0.9 %copy-start = (bf16[1,1024,128]{2,1,0:T(8,128)(2,1)S(1)}, bf16[1,1024,128]{2,1,0:T(8,128)(2,1)}, u32[]{:S(2)}) copy-start(bf16[1,1024,128]{2,1,0:T(8,128)(2,1)} %param.4) | copy-start | bytes 786436
  12.7 0.9 %copy-start.1 = (bf16[1,1,1024,128]{3,2,1,0:T(8,128)(2,1)S(1)}, bf16[1,1,1024,128]{3,2,1,0:T(8,128)(2,1)}, u32[]{:S(2)}) copy-start(bf16[1,1,1024,128]{3,2,1,0:T(8,128)(2,1)} %param.5) | copy-start | bytes 786436
  13.7 0.9 %copy-start.2 = (bf16[1,64,1024]{2,1,0:T(8,128)(2,1)S(1)}, bf16[1,64,1024]{2,1,0:T(8,128)(2,1)}, u32[]{:S(2)}) copy-start(bf16[1,64,1024]{2,1,0:T(8,128)(2,1)} %param.7) | copy-start | bytes 393220
  19.5 5.8 %collective-permute-start.7 = (bf16[256,128]{1,0:T(8,128)(2,1)S(1)}, bf16[256,128]{1,0:T(8,128)(2,1)S(1)}, u32[]{:S(2)}, u32[]{:S(2)}) collective-permute-start(bf16[256,128]{1,0:T(8,128)(2,1)S(1)} %get-tuple-element.27), channel_id=1, source_target_pairs={{0,1},{1,0},{2,3},{3,2},{4,5},{5,4},{6,7},{7,6},{8,9},{9,8},{10,11... | collective-permute-start | bytes 196616 | tf_op jit(solution)/shard_map/ppermute | solution.py:28
  20.8 4.9 %collective-permute-start.8 = (bf16[256,128]{1,0:T(8,128)(2,1)S(1)}, bf16[256,128]{1,0:T(8,128)(2,1)S(1)}, u32[]{:S(2)}, u32[]{:S(2)}) collective-permute-start(bf16[256,128]{1,0:T(8,128)(2,1)S(1)} %get-tuple-element.28), channel_id=1, source_target_pairs={{0,2},{1,3},{2,0},{3,1},{4,6},{5,7},{6,4},{7,5},{8,10},{9,11},{10,... | collective-permute-start | bytes 196616 | tf_op jit(solution)/shard_map/ppermute | solution.py:28
  22.0 5.2 %collective-permute-start.9 = (bf16[256,128]{1,0:T(8,128)(2,1)S(1)}, bf16[256,128]{1,0:T(8,128)(2,1)S(1)}, u32[]{:S(2)}, u32[]{:S(2)}) collective-permute-start(bf16[256,128]{1,0:T(8,128)(2,1)S(1)} %get-tuple-element.29), channel_id=1, source_target_pairs={{0,3},{1,2},{2,1},{3,0},{4,7},{5,6},{6,5},{7,4},{8,11},{9,10},{10,... | collective-permute-start | bytes 196616 | tf_op jit(solution)/shard_map/ppermute | solution.py:28
  28.6 2.6 %collective-permute-start.17 = (bf16[512,128]{1,0:T(8,128)(2,1)S(1)}, bf16[512,128]{1,0:T(8,128)(2,1)S(1)}, u32[]{:S(2)}, u32[]{:S(2)}) collective-permute-start(bf16[512,128]{1,0:T(8,128)(2,1)S(1)} %get-tuple-element.35), channel_id=1, source_target_pairs={{0,17},{1,16},{2,19},{3,18},{4,21},{5,20},{6,23},{7,22},{8,25},{9,... | collective-permute-start | bytes 393224 | tf_op jit(solution)/shard_map/ppermute | solution.py:38
  28.6 11.6 %collective-permute-start.14 = (bf16[1280,128]{1,0:T(8,128)(2,1)S(1)}, bf16[1280,128]{1,0:T(8,128)(2,1)S(1)}, u32[]{:S(2)}, u32[]{:S(2)}) collective-permute-start(bf16[1280,128]{1,0:T(8,128)(2,1)S(1)} %get-tuple-element.32), channel_id=1, source_target_pairs={{16,4},{17,5},{18,6},{19,7},{20,0},{21,1},{22,2},{23,3},{24,12},{2... | collective-permute-start | bytes 983048 | tf_op jit(solution)/shard_map/ppermute | solution.py:46
  29.1 3.9 %collective-permute-start.18 = (bf16[512,128]{1,0:T(8,128)(2,1)S(1)}, bf16[512,128]{1,0:T(8,128)(2,1)S(1)}, u32[]{:S(2)}, u32[]{:S(2)}) collective-permute-start(bf16[512,128]{1,0:T(8,128)(2,1)S(1)} %get-tuple-element.35), channel_id=1, source_target_pairs={{0,18},{1,19},{2,16},{3,17},{4,22},{5,23},{6,20},{7,21},{8,26},{9,... | collective-permute-start | bytes 393224 | tf_op jit(solution)/shard_map/ppermute | solution.py:38
  29.6 10.5 %collective-permute-start.10 = (bf16[1024,128]{1,0:T(8,128)(2,1)S(1)}, bf16[1024,128]{1,0:T(8,128)(2,1)S(1)}, u32[]{:S(2)}, u32[]{:S(2)}) collective-permute-start(bf16[1024,128]{1,0:T(8,128)(2,1)S(1)} %get-tuple-element.30), channel_id=1, source_target_pairs={{0,16},{1,17},{2,18},{3,19},{4,20},{5,21},{6,22},{7,23},{8,24},{9,... | collective-permute-start | bytes 786440 | tf_op jit(solution)/shard_map/ppermute | solution.py:38
  29.7 12.0 %collective-permute-start.15 = (bf16[1280,128]{1,0:T(8,128)(2,1)S(1)}, bf16[1280,128]{1,0:T(8,128)(2,1)S(1)}, u32[]{:S(2)}, u32[]{:S(2)}) collective-permute-start(bf16[1280,128]{1,0:T(8,128)(2,1)S(1)} %get-tuple-element.33), channel_id=1, source_target_pairs={{16,8},{17,9},{18,10},{19,11},{20,12},{21,13},{22,14},{23,15},{24,... | collective-permute-start | bytes 983048 | tf_op jit(solution)/shard_map/ppermute | solution.py:46
  31.1 17.1 %collective-permute-start.16 = (bf16[1280,128]{1,0:T(8,128)(2,1)S(1)}, bf16[1280,128]{1,0:T(8,128)(2,1)S(1)}, u32[]{:S(2)}, u32[]{:S(2)}) collective-permute-start(bf16[1280,128]{1,0:T(8,128)(2,1)S(1)} %get-tuple-element.34), channel_id=1, source_target_pairs={{16,12},{17,13},{18,14},{19,15},{20,8},{21,9},{22,10},{23,11},{24,... | collective-permute-start | bytes 983048 | tf_op jit(solution)/shard_map/ppermute | solution.py:46
  33.0 4.0 %collective-permute-start.19 = (bf16[512,128]{1,0:T(8,128)(2,1)S(1)}, bf16[512,128]{1,0:T(8,128)(2,1)S(1)}, u32[]{:S(2)}, u32[]{:S(2)}) collective-permute-start(bf16[512,128]{1,0:T(8,128)(2,1)S(1)} %get-tuple-element.35), channel_id=1, source_target_pairs={{0,19},{1,18},{2,17},{3,16},{4,23},{5,22},{6,21},{7,20},{8,27},{9,... | collective-permute-start | bytes 393224 | tf_op jit(solution)/shard_map/ppermute | solution.py:38
  37.1 11.5 %collective-permute-start.11 = (bf16[512,128]{1,0:T(8,128)(2,1)S(1)}, bf16[512,128]{1,0:T(8,128)(2,1)S(1)}, u32[]{:S(2)}, u32[]{:S(2)}) collective-permute-start(bf16[512,128]{1,0:T(8,128)(2,1)S(1)} %get-tuple-element.31), channel_id=1, source_target_pairs={{0,17},{1,16},{2,19},{3,18},{4,21},{5,20},{6,23},{7,22},{8,25},{9,... | collective-permute-start | bytes 393224 | tf_op jit(solution)/shard_map/ppermute | solution.py:38
  40.2 8.4 %collective-permute-start.12 = (bf16[512,128]{1,0:T(8,128)(2,1)S(1)}, bf16[512,128]{1,0:T(8,128)(2,1)S(1)}, u32[]{:S(2)}, u32[]{:S(2)}) collective-permute-start(bf16[512,128]{1,0:T(8,128)(2,1)S(1)} %get-tuple-element.31), channel_id=1, source_target_pairs={{0,18},{1,19},{2,16},{3,17},{4,22},{5,23},{6,20},{7,21},{8,26},{9,... | collective-permute-start | bytes 393224 | tf_op jit(solution)/shard_map/ppermute | solution.py:38
  40.2 8.4 %collective-permute-start.13 = (bf16[512,128]{1,0:T(8,128)(2,1)S(1)}, bf16[512,128]{1,0:T(8,128)(2,1)S(1)}, u32[]{:S(2)}, u32[]{:S(2)}) collective-permute-start(bf16[512,128]{1,0:T(8,128)(2,1)S(1)} %get-tuple-element.31), channel_id=1, source_target_pairs={{0,19},{1,18},{2,17},{3,16},{4,23},{5,22},{6,21},{7,20},{8,27},{9,... | collective-permute-start | bytes 393224 | tf_op jit(solution)/shard_map/ppermute | solution.py:38
  48.9 10.2 %collective-permute-start.20 = (bf16[64,1024]{1,0:T(8,128)(2,1)S(1)}, bf16[64,1024]{1,0:T(8,128)(2,1)S(1)}, u32[]{:S(2)}, u32[]{:S(2)}) collective-permute-start(bf16[64,1024]{1,0:T(8,128)(2,1)S(1)} %get-tuple-element.37), channel_id=1, source_target_pairs={{0,1},{1,0},{2,3},{3,2},{4,5},{5,4},{6,7},{7,6},{8,9},{9,8},{10,11... | collective-permute-start | bytes 393224 | tf_op jit(solution)/shard_map/ppermute | solution.py:56
  49.6 7.0 %collective-permute-start.21 = (bf16[64,512]{1,0:T(8,128)(2,1)S(1)}, bf16[64,512]{1,0:T(8,128)(2,1)S(1)}, u32[]{:S(2)}, u32[]{:S(2)}) collective-permute-start(bf16[64,512]{1,0:T(8,128)(2,1)S(1)} %get-tuple-element.39), channel_id=1, source_target_pairs={{0,2},{1,3},{2,0},{3,1},{4,6},{5,7},{6,4},{7,5},{8,10},{9,11},{10,... | collective-permute-start | bytes 196616 | tf_op jit(solution)/shard_map/ppermute | solution.py:56
  51.0 5.6 %collective-permute-start.22 = (bf16[64,512]{1,0:T(8,128)(2,1)S(1)}, bf16[64,512]{1,0:T(8,128)(2,1)S(1)}, u32[]{:S(2)}, u32[]{:S(2)}) collective-permute-start(bf16[64,512]{1,0:T(8,128)(2,1)S(1)} %get-tuple-element.40), channel_id=1, source_target_pairs={{0,3},{1,2},{2,1},{3,0},{4,7},{5,6},{6,5},{7,4},{8,11},{9,10},{10,... | collective-permute-start | bytes 196616 | tf_op jit(solution)/shard_map/ppermute | solution.py:56
  52.5 4.4 %collective-permute-start.23 = (bf16[64,512]{1,0:T(8,128)(2,1)S(1)}, bf16[64,512]{1,0:T(8,128)(2,1)S(1)}, u32[]{:S(2)}, u32[]{:S(2)}) collective-permute-start(bf16[64,512]{1,0:T(8,128)(2,1)S(1)} %get-tuple-element.42), channel_id=1, source_target_pairs={{0,2},{1,3},{2,0},{3,1},{4,6},{5,7},{6,4},{7,5},{8,10},{9,11},{10,... | collective-permute-start | bytes 196616 | tf_op jit(solution)/shard_map/ppermute | solution.py:56
  54.0 5.2 %collective-permute-start.24 = (bf16[64,512]{1,0:T(8,128)(2,1)S(1)}, bf16[64,512]{1,0:T(8,128)(2,1)S(1)}, u32[]{:S(2)}, u32[]{:S(2)}) collective-permute-start(bf16[64,512]{1,0:T(8,128)(2,1)S(1)} %get-tuple-element.43), channel_id=1, source_target_pairs={{0,3},{1,2},{2,1},{3,0},{4,7},{5,6},{6,5},{7,4},{8,11},{9,10},{10,... | collective-permute-start | bytes 196616 | tf_op jit(solution)/shard_map/ppermute | solution.py:56

commit v4 on v3

--- a/solution.py
+++ b/solution.py
@@ -13,7 +13,6 @@
 STAGE_LIMIT = 47 * MIB
 HALVES = 2
 JOINED = (1,)
-TWO_STEP = False
 
 
 def plane_size(devices):
@@ -120,40 +119,37 @@
     return outs[:count], outs[count:]
 
 
-def pieces_kernel(line, cuts, *refs):
-    blocks, refs = refs[:line], refs[line:]
-    ups, outs, joined = refs[: sum(cuts)], refs[sum(cuts) : sum(cuts) + len(cuts)], list(refs[sum(cuts) + len(cuts) :])
+def side_by_side(parts):
+    return jnp.concatenate(parts, axis=1)
+
+
+def pieces_kernel(line, plane, *refs):
+    blocks, ups, outs = refs[:line], refs[line : line + plane], refs[line + plane :]
     rows = jnp.concatenate([b[...] for b in blocks], axis=0)
-    for cut, out in zip(cuts, outs):
-        parts, ups = ups[:cut], ups[cut:]
-        up = parts[0][...] if cut == 1 else jnp.concatenate([p[...] for p in parts], axis=0)
-        if cut > 1:
-            joined.pop(0)[...] = up
-        out[...] = jnp.dot(rows, up, preferred_element_type=jnp.float32).astype(out.dtype)
+    cols = ups[0].shape[1]
+    products = jnp.dot(rows, side_by_side([up[...] for up in ups]), preferred_element_type=jnp.float32)
+    for q, out in enumerate(outs):
+        out[...] = products[:, q * cols : (q + 1) * cols].astype(out.dtype)
 
 
 def rq_pieces(blocks, ups):
     line, plane = len(blocks), len(ups)
-    cuts = [len(parts) for parts in ups]
     rows, nx = blocks[0].shape
-    cols = ups[0][0].shape[1]
+    cols = ups[0].shape[1]
     tall = line * rows
     out_shape = [jax.ShapeDtypeStruct((tall, cols), jnp.float32)]
     out_shape += [jax.ShapeDtypeStruct((tall, cols), jnp.bfloat16)] * (plane - 1)
-    out_shape += [jax.ShapeDtypeStruct((nx, cols), jnp.bfloat16)] * sum(cut > 1 for cut in cuts)
-    outs = pl.pallas_call(
-        functools.partial(pieces_kernel, line, cuts),
+    return pl.pallas_call(
+        functools.partial(pieces_kernel, line, plane),
         out_shape=out_shape,
-        in_specs=[VMEM] * (line + sum(cuts)),
-        out_specs=[VMEM] * len(out_shape),
+        in_specs=[VMEM] * (line + plane),
+        out_specs=[VMEM] * plane,
         compiler_params=params(16 * MIB),
         cost_estimate=pl.CostEstimate(
             flops=2 * tall * nx * cols * plane, bytes_accessed=2 * nx * (tall + plane * cols), transcendentals=0
         ),
         name="rq_pieces",
-    )(*blocks, *[part for parts in ups for part in parts])
-    joined = list(outs[plane:])
-    return list(outs[:plane]), [parts[0] if len(parts) == 1 else joined.pop(0) for parts in ups]
+    )(*blocks, *ups)
 
 
 def gather_line(value, plane, line):
@@ -162,19 +158,6 @@
         far = z & (z - 1) if z.bit_count() == 2 else 0
         found[z] = swap(found[far], (z ^ far) * plane)
     return [found[z] for z in range(line)]
-
-
-def gather_plane(value, plane):
-    found = {0: [value]}
-    tall = value.shape[0] // 2
-    for q in range(1, plane):
-        if not TWO_STEP or q.bit_count() != 2:
-            found[q] = [swap(value, q)]
-    for q in range(1, plane):
-        if TWO_STEP and q.bit_count() == 2:
-            low, high = q & -q, q & (q - 1)
-            found[q] = [swap(found[high][0][:tall], low), swap(found[low][0][tall:], high)]
-    return [found[q] for q in range(plane)]
 
 
 def advance_kernel(line, plane, counts, *refs):
@@ -236,10 +219,6 @@
     )(top, *moved, *pieces, weights)
 
 
-def side_by_side(parts):
-    return jnp.concatenate(parts, axis=1)
-
-
 def stacked_rows(ref, starts, rows):
     return jnp.concatenate([ref[pl.ds(pl.multiple_of(s, rows), rows), :] for s in starts], axis=0)
 
@@ -338,12 +317,12 @@
 
     blocks = gather_line(own_rows, plane, line)
     other = lower(upper, 0)
-    ups = gather_plane(upper, plane)
+    ups = [upper] + [swap(upper, q) for q in range(1, plane)]
     weights = stage_weights(weights)
     (top, upper, own_rows), loads = stage((top, upper, own_rows), other, plane, line)
     loads = [raise_top(load, z * plane) for z, load in enumerate(loads, 1)]
-    blocks, ups = [own_rows] + blocks[1:], [[upper]] + ups[1:]
-    pieces, ups = rq_pieces(blocks, ups)
+    blocks, ups = [own_rows] + blocks[1:], [upper] + ups[1:]
+    pieces = rq_pieces(blocks, ups)
     pieces = [pieces[0]] + [swap(pieces[q], q) for q in range(1, plane)]
 
     moved = []

time: 60.1 us -> 59.8 us (level)
  no operation moved by 1% of the time
where the time goes in v4:
time: 59.8 us; the launch traced here: 59.6 us
  starting transfers between devices  26.9 us (45%)
  waiting for transfers between devices  21 us (35%)
  Pallas kernels  8.15 us (14%)
  local copies, waits for them, and re-layouts  2.8 us (5%)
  between operations  0.75 us (1%)
    ppermute x9, starting transfers between devices, swap(): return lax.ppermute(value, 'freq', [(i, i ^ by) for i in range(devices)])  11.7 us
    ppermute x9, waiting for transfers between devices, swap(): return lax.ppermute(value, 'freq', [(i, i ^ by) for i in range(devices)])  8.39 us
    ppermute x8, starting transfers between devices, lower(): return lax.ppermute(value, ('depth', 'freq'), pairs)  6.78 us
    ppermute x3, waiting for transfers between devices, raise_top(): return lax.ppermute(value, ('depth', 'freq'), pairs)  6.53 us
    ppermute x5, starting transfers between devices, reduce_step(): return lax.ppermute(value, ('depth', 'freq'), pairs)  5.55 us
    ppermute x8, waiting for transfers between devices, lower(): return lax.ppermute(value, ('depth', 'freq'), pairs)  3.51 us
    pallas_call x2, Pallas kernels, advance(): pl.pallas_call(functools.partial(advance_kernel, line, plane, (len(moved)...  3.44 us
    ppermute x3, starting transfers between devices, raise_top(): return lax.ppermute(value, ('depth', 'freq'), pairs)  2.89 us
  transfers between devices with their start and end apart: 25, of which 11 were waited for; matrix products, arithmetic and copies ran while one was open for 0% of the time, Pallas kernels for 9%

profile of v4, /device:TPU:8, one launch (start us, length us, event | category | flops | bytes accessed | tf_op | source)
XLA Modules:
  0.0 59.6 jit_solution(9832120897024660610)
XLA Ops:
  0.6 0.1 collective-permute-start
  0.7 2.7 %collective-permute-start.2 = (bf16[64,1024]{1,0:T(8,128)(2,1)}, bf16[64,1024]{1,0:T(8,128)(2,1)S(1)}, u32[]{:S(2)}, u32[]{:S(2)}) collective-permute-start(bf16[64,1024]{1,0:T(8,128)(2,1)} %bitcast.12), channel_id=1, source_target_pairs={{0,8},{1,9},{2,10},{3,11},{4,12},{5,13},{6,14},{7,15},{8,0},{9,1},... | collective-permute-start | bytes 393224 | tf_op jit(solution)/shard_map/ppermute | solution.py:27
  3.4 1.5 %collective-permute-start.4 = (bf16[1024,128]{1,0:T(8,128)(2,1)}, bf16[1024,128]{1,0:T(8,128)(2,1)S(1)}, u32[]{:S(2)}, u32[]{:S(2)}) collective-permute-start(bf16[1024,128]{1,0:T(8,128)(2,1)} %bitcast.8), channel_id=1, source_target_pairs={{0,1},{1,0},{2,3},{3,2},{4,5},{5,4},{6,7},{7,6},{8,9},{9,8},{10,11... | collective-permute-start | bytes 786440 | tf_op jit(solution)/shard_map/ppermute | solution.py:27
  4.9 1.5 %collective-permute-start.5 = (bf16[1024,128]{1,0:T(8,128)(2,1)}, bf16[1024,128]{1,0:T(8,128)(2,1)S(1)}, u32[]{:S(2)}, u32[]{:S(2)}) collective-permute-start(bf16[1024,128]{1,0:T(8,128)(2,1)} %bitcast.9), channel_id=1, source_target_pairs={{0,2},{1,3},{2,0},{3,1},{4,6},{5,7},{6,4},{7,5},{8,10},{9,11},{10,... | collective-permute-start | bytes 786440 | tf_op jit(solution)/shard_map/ppermute | solution.py:27
  6.4 0.5 collective-permute-start.6
  6.9 2.9 %collective-permute-done.2.refs_2_ = bf16[64,1024]{1,0:T(8,128)(2,1)S(1)} collective-permute-done((bf16[64,1024]{1,0:T(8,128)(2,1)}, bf16[64,1024]{1,0:T(8,128)(2,1)S(1)}, u32[]{:S(2)}, u32[]{:S(2)}) %collective-permute-start.2) | collective-permute-done | bytes 131104 | tf_op jit(solution)/shard_map/ppermute | solution.py:27
  9.7 1.2 %collective-permute-start.1 = (bf16[64,1024]{1,0:T(8,128)(2,1)}, bf16[64,1024]{1,0:T(8,128)(2,1)S(1)}, u32[]{:S(2)}, u32[]{:S(2)}) collective-permute-start(bf16[64,1024]{1,0:T(8,128)(2,1)} %bitcast.13), channel_id=1, source_target_pairs={{0,4},{1,5},{2,6},{3,7},{4,0},{5,1},{6,2},{7,3},{8,12},{9,13},{10,... | collective-permute-start | bytes 393224 | tf_op jit(solution)/shard_map/ppermute | solution.py:27
  10.9 0.0 collective-permute-done.refs_3_
  10.9 0.8 %collective-permute-start.3 = (bf16[64,1024]{1,0:T(8,128)(2,1)S(1)}, bf16[64,1024]{1,0:T(8,128)(2,1)S(1)}, u32[]{:S(2)}, u32[]{:S(2)}) collective-permute-start(bf16[64,1024]{1,0:T(8,128)(2,1)S(1)} %collective-permute-done.2.refs_2_), channel_id=1, source_target_pairs={{0,4},{1,5},{2,6},{3,7},{4,0},{5,1},{6,2},{7,3},{8,12},{9,13},{10,... | collective-permute-start | bytes 393224 | tf_op jit(solution)/shard_map/ppermute | solution.py:27
  11.8 0.0 copy-start
  11.8 0.9 %copy-done = bf16[1,1024,128]{2,1,0:T(8,128)(2,1)S(1)} copy-done((bf16[1,1024,128]{2,1,0:T(8,128)(2,1)S(1)}, bf16[1,1024,128]{2,1,0:T(8,128)(2,1)}, u32[]{:S(2)}) %copy-start) | copy-done | bytes 262168
  12.7 0.0 copy-start.1
  12.7 0.9 %copy-done.1 = bf16[1,1,1024,128]{3,2,1,0:T(8,128)(2,1)S(1)} copy-done((bf16[1,1,1024,128]{3,2,1,0:T(8,128)(2,1)S(1)}, bf16[1,1,1024,128]{3,2,1,0:T(8,128)(2,1)}, u32[]{:S(2)}) %copy-start.1) | copy-done | bytes 262168
  13.7 0.0 copy-start.2
  13.7 0.9 %copy-done.2 = bf16[1,64,1024]{2,1,0:T(8,128)(2,1)S(1)} copy-done((bf16[1,64,1024]{2,1,0:T(8,128)(2,1)S(1)}, bf16[1,64,1024]{2,1,0:T(8,128)(2,1)}, u32[]{:S(2)}) %copy-start.2) | copy-done | bytes 131096
  14.6 0.6 %stage_inputs.1 = (bf16[1024,128]{1,0:T(8,128)(2,1)S(1)}, bf16[1024,128]{1,0:T(8,128)(2,1)S(1)}, bf16[64,1024]{1,0:T(8,128)(2,1)S(1)}, bf16[1280,128]{1,0:T(8,12...) custom-call(bf16[1024,128]{1,0:T(8,128)(2,1)S(1)} %bitcast.6, bf16[1024,128]{1,0:T(8,128)(2,1)S(1)} %bitcast.11, ...), custom_call_target="tpu_custom_call" | custom-call | bytes 3276800 | tf_op jit(solution)/shard_map/stage_inputs/pallas_call | solution.py:109
  15.2 1.1 %collective-permute-done.1.refs_1_ = bf16[64,1024]{1,0:T(8,128)(2,1)S(1)} collective-permute-done((bf16[64,1024]{1,0:T(8,128)(2,1)}, bf16[64,1024]{1,0:T(8,128)(2,1)S(1)}, u32[]{:S(2)}, u32[]{:S(2)}) %collective-permute-start.1) | collective-permute-done | bytes 131104 | tf_op jit(solution)/shard_map/ppermute | solution.py:27
  16.3 1.9 %collective-permute-done.3.refs_3_ = bf16[64,1024]{1,0:T(8,128)(2,1)S(1)} collective-permute-done((bf16[64,1024]{1,0:T(8,128)(2,1)S(1)}, bf16[64,1024]{1,0:T(8,128)(2,1)S(1)}, u32[]{:S(2)}, u32[]{:S(2)}) %collective-permute-start.3) | collective-permute-done | bytes 131104 | tf_op jit(solution)/shard_map/ppermute | solution.py:27
  18.2 0.0 collective-permute-done.4.refs_5_.refs_1_
  18.2 0.5 collective-permute-done.5.refs_6_.refs_2_
  18.8 0.0 collective-permute-done.6.refs_7_.refs_3_
  18.8 0.4 rq_pieces.1
  19.2 1.3 %collective-permute-start.7 = (bf16[256,128]{1,0:T(8,128)(2,1)S(1)}, bf16[256,128]{1,0:T(8,128)(2,1)S(1)}, u32[]{:S(2)}, u32[]{:S(2)}) collective-permute-start(bf16[256,128]{1,0:T(8,128)(2,1)S(1)} %get-tuple-element.27), channel_id=1, source_target_pairs={{0,1},{1,0},{2,3},{3,2},{4,5},{5,4},{6,7},{7,6},{8,9},{9,8},{10,11... | collective-permute-start | bytes 196616 | tf_op jit(solution)/shard_map/ppermute | solution.py:27
  20.5 1.2 %collective-permute-start.8 = (bf16[256,128]{1,0:T(8,128)(2,1)S(1)}, bf16[256,128]{1,0:T(8,128)(2,1)S(1)}, u32[]{:S(2)}, u32[]{:S(2)}) collective-permute-start(bf16[256,128]{1,0:T(8,128)(2,1)S(1)} %get-tuple-element.28), channel_id=1, source_target_pairs={{0,2},{1,3},{2,0},{3,1},{4,6},{5,7},{6,4},{7,5},{8,10},{9,11},{10,... | collective-permute-start | bytes 196616 | tf_op jit(solution)/shard_map/ppermute | solution.py:27
  21.8 1.0 %collective-permute-start.9 = (bf16[256,128]{1,0:T(8,128)(2,1)S(1)}, bf16[256,128]{1,0:T(8,128)(2,1)S(1)}, u32[]{:S(2)}, u32[]{:S(2)}) collective-permute-start(bf16[256,128]{1,0:T(8,128)(2,1)S(1)} %get-tuple-element.29), channel_id=1, source_target_pairs={{0,3},{1,2},{2,1},{3,0},{4,7},{5,6},{6,5},{7,4},{8,11},{9,10},{10,... | collective-permute-start | bytes 196616 | tf_op jit(solution)/shard_map/ppermute | solution.py:27
  22.8 2.2 %stage_weights.1.refs_5_.refs_6_ = bf16[2,1024,1024]{2,1,0:T(8,128)(2,1)S(1)} custom-call(bf16[2,1024,1024]{2,1,0:T(8,128)(2,1)} %bitcast.15), custom_call_target="tpu_custom_call" | custom-call | bytes 8388608 | tf_op jit(solution)/shard_map/stage_weights/pallas_call | solution.py:78
  25.0 0.0 collective-permute-done.7.refs_2_.refs_3_
  25.0 0.4 collective-permute-done.8.refs_3_.refs_4_
  25.4 1.5 %collective-permute-done.9.refs_4_.refs_5_ = bf16[256,128]{1,0:T(8,128)(2,1)S(1)} collective-permute-done((bf16[256,128]{1,0:T(8,128)(2,1)S(1)}, bf16[256,128]{1,0:T(8,128)(2,1)S(1)}, u32[]{:S(2)}, u32[]{:S(2)}) %collective-permute-start.9) | collective-permute-done | bytes 65568 | tf_op jit(solution)/shard_map/ppermute | solution.py:27
  26.9 1.4 %advance.2 = (bf16[512,128]{1,0:T(8,128)(2,1)S(1)}, bf16[512,128]{1,0:T(8,128)(2,1)S(1)}, bf16[1024,128]{1,0:T(8,128)(2,1)S(1)}) custom-call(bf16[1024,128]{1,0:T(8,128)(2,1)S(1)} %get-tuple-element.23.refs_0_.refs_8_, f32[256,128]{1,0:T(8,128)S(1)} %get-tuple-element.26.refs_1_.refs_2_, bf16[256,128]{1,0:T(8,128)(2,1)S(1)} %collective-permute-done.7.refs_2_.refs_3_, ...), custom_call_target="tpu_custom_call" | custom-call | flops 536870912 | bytes 4194304 | tf_op jit(solution)/shard_map/advance/pallas_call | solution.py:210
  28.3 0.1 collective-permute-start.17
  28.4 0.5 collective-permute-start.14
  28.9 0.5 collective-permute-start.18
  29.4 0.0 collective-permute-start.10
  29.4 0.5 collective-permute-start.15
  29.9 1.0 %collective-permute-done.17.refs_5_ = bf16[512,128]{1,0:T(8,128)(2,1)S(1)} collective-permute-done((bf16[512,128]{1,0:T(8,128)(2,1)S(1)}, bf16[512,128]{1,0:T(8,128)(2,1)S(1)}, u32[]{:S(2)}, u32[]{:S(2)}) %collective-permute-start.17) | collective-permute-done | bytes 131104 | tf_op jit(solution)/shard_map/ppermute | solution.py:37
  30.9 1.9 %collective-permute-start.16 = (bf16[1280,128]{1,0:T(8,128)(2,1)S(1)}, bf16[1280,128]{1,0:T(8,128)(2,1)S(1)}, u32[]{:S(2)}, u32[]{:S(2)}) collective-permute-start(bf16[1280,128]{1,0:T(8,128)(2,1)S(1)} %get-tuple-element.34), channel_id=1, source_target_pairs={{16,12},{17,13},{18,14},{19,15},{20,8},{21,9},{22,10},{23,11},{24,... | collective-permute-start | bytes 983048 | tf_op jit(solution)/shard_map/ppermute | solution.py:45
  32.8 0.0 collective-permute-done.18.refs_6_
  32.8 1.5 %collective-permute-start.19 = (bf16[512,128]{1,0:T(8,128)(2,1)S(1)}, bf16[512,128]{1,0:T(8,128)(2,1)S(1)}, u32[]{:S(2)}, u32[]{:S(2)}) collective-permute-start(bf16[512,128]{1,0:T(8,128)(2,1)S(1)} %get-tuple-element.35), channel_id=1, source_target_pairs={{0,19},{1,18},{2,17},{3,16},{4,23},{5,22},{6,21},{7,20},{8,27},{9,... | collective-permute-start | bytes 393224 | tf_op jit(solution)/shard_map/ppermute | solution.py:37
  34.3 2.5 %collective-permute-done.19.refs_7_ = bf16[512,128]{1,0:T(8,128)(2,1)S(1)} collective-permute-done((bf16[512,128]{1,0:T(8,128)(2,1)S(1)}, bf16[512,128]{1,0:T(8,128)(2,1)S(1)}, u32[]{:S(2)}, u32[]{:S(2)}) %collective-permute-start.19) | collective-permute-done | bytes 131104 | tf_op jit(solution)/shard_map/ppermute | solution.py:37
  36.8 3.1 %collective-permute-start.11 = (bf16[512,128]{1,0:T(8,128)(2,1)S(1)}, bf16[512,128]{1,0:T(8,128)(2,1)S(1)}, u32[]{:S(2)}, u32[]{:S(2)}) collective-permute-start(bf16[512,128]{1,0:T(8,128)(2,1)S(1)} %get-tuple-element.31), channel_id=1, source_target_pairs={{0,17},{1,16},{2,19},{3,18},{4,21},{5,20},{6,23},{7,22},{8,25},{9,... | collective-permute-start | bytes 393224 | tf_op jit(solution)/shard_map/ppermute | solution.py:37
  39.9 0.0 collective-permute-done.10.refs_1_.refs_4_
  39.9 0.0 collective-permute-start.12
  39.9 0.0 collective-permute-done.14.refs_9_
  39.9 1.5 %collective-permute-start.13 = (bf16[512,128]{1,0:T(8,128)(2,1)S(1)}, bf16[512,128]{1,0:T(8,128)(2,1)S(1)}, u32[]{:S(2)}, u32[]{:S(2)}) collective-permute-start(bf16[512,128]{1,0:T(8,128)(2,1)S(1)} %get-tuple-element.31), channel_id=1, source_target_pairs={{0,19},{1,18},{2,17},{3,16},{4,23},{5,22},{6,21},{7,20},{8,27},{9,... | collective-permute-start | bytes 393224 | tf_op jit(solution)/shard_map/ppermute | solution.py:37
  41.4 0.0 collective-permute-done.15.refs_10_
  41.4 6.5 %collective-permute-done.16.refs_11_ = bf16[1280,128]{1,0:T(8,128)(2,1)S(1)} collective-permute-done((bf16[1280,128]{1,0:T(8,128)(2,1)S(1)}, bf16[1280,128]{1,0:T(8,128)(2,1)S(1)}, u32[]{:S(2)}, u32[]{:S(2)}) %collective-permute-start.16) | collective-permute-done | bytes 327712 | tf_op jit(solution)/shard_map/ppermute | solution.py:45
  47.9 0.3 picture_parts.2
  48.3 0.0 collective-permute-done.11.refs_5_
  48.3 0.0 collective-permute-done.12.refs_6_
  48.3 0.0 collective-permute-done.13.refs_7_
  48.3 0.4 picture_parts.3
  48.7 0.6 collective-permute-start.20
  49.3 1.5 %collective-permute-start.21 = (bf16[64,512]{1,0:T(8,128)(2,1)S(1)}, bf16[64,512]{1,0:T(8,128)(2,1)S(1)}, u32[]{:S(2)}, u32[]{:S(2)}) collective-permute-start(bf16[64,512]{1,0:T(8,128)(2,1)S(1)} %get-tuple-element.39), channel_id=1, source_target_pairs={{0,2},{1,3},{2,0},{3,1},{4,6},{5,7},{6,4},{7,5},{8,10},{9,11},{10,... | collective-permute-start | bytes 196616 | tf_op jit(solution)/shard_map/ppermute | solution.py:55
  50.7 1.5 %collective-permute-start.22 = (bf16[64,512]{1,0:T(8,128)(2,1)S(1)}, bf16[64,512]{1,0:T(8,128)(2,1)S(1)}, u32[]{:S(2)}, u32[]{:S(2)}) collective-permute-start(bf16[64,512]{1,0:T(8,128)(2,1)S(1)} %get-tuple-element.40), channel_id=1, source_target_pairs={{0,3},{1,2},{2,1},{3,0},{4,7},{5,6},{6,5},{7,4},{8,11},{9,10},{10,... | collective-permute-start | bytes 196616 | tf_op jit(solution)/shard_map/ppermute | solution.py:55
  52.2 1.5 %collective-permute-start.23 = (bf16[64,512]{1,0:T(8,128)(2,1)S(1)}, bf16[64,512]{1,0:T(8,128)(2,1)S(1)}, u32[]{:S(2)}, u32[]{:S(2)}) collective-permute-start(bf16[64,512]{1,0:T(8,128)(2,1)S(1)} %get-tuple-element.42), channel_id=1, source_target_pairs={{0,2},{1,3},{2,0},{3,1},{4,6},{5,7},{6,4},{7,5},{8,10},{9,11},{10,... | collective-permute-start | bytes 196616 | tf_op jit(solution)/shard_map/ppermute | solution.py:55
  53.7 0.5 collective-permute-start.24
  54.2 2.1 %advance.3 = bf16[1024,128]{1,0:T(8,128)(2,1)} custom-call(bf16[1024,128]{1,0:T(8,128)(2,1)S(1)} %get-tuple-element.23.refs_0_.refs_8_, bf16[1024,128]{1,0:T(8,128)(2,1)S(1)} %collective-permute-done.10.refs_1_.refs_4_, f32[256,128]{1,0:T(8,128)S(1)} %get-tuple-element.26.refs_1_.refs_2_, bf16[256,128]{1,0:T(8,128)(2,1)S(1)} %collective-permute-done.7.refs_2_.refs_3_, ...), custom_call_target="tpu_custom_call" | custom-call | flops 536870912 | bytes 4194304 | tf_op jit(solution)/shard_map/advance/pallas_call | solution.py:210
  56.3 0.0 collective-permute-done.21.refs_2_
  56.3 0.0 collective-permute-done.22.refs_3_
  56.3 0.3 collective-permute-done.23.refs_5_
  56.6 2.3 %collective-permute-done.24.refs_6_ = bf16[64,512]{1,0:T(8,128)(2,1)S(1)} collective-permute-done((bf16[64,512]{1,0:T(8,128)(2,1)S(1)}, bf16[64,512]{1,0:T(8,128)(2,1)S(1)}, u32[]{:S(2)}, u32[]{:S(2)}) %collective-permute-start.24) | collective-permute-done | bytes 65568 | tf_op jit(solution)/shard_map/ppermute | solution.py:55
  58.9 0.0 collective-permute-done.20.refs_0_
  58.9 0.8 %sum_parts.1 = f32[64,1024]{1,0:T(8,128)} custom-call(bf16[64,1024]{1,0:T(8,128)(2,1)S(1)} %collective-permute-done.20.refs_0_, f32[64,512]{1,0:T(8,128)S(1)} %get-tuple-element.38.refs_1_, bf16[64,512]{1,0:T(8,128)(2,1)S(1)} %collective-permute-done.21.refs_2_, bf16[64,512]{1,0:T(8,128)(2,1)S(1)} %collective-permute-done.22.refs_3_, ...), custom_call_target="tpu_custom_call" | custom-call | flops 262144 | bytes 524288 | tf_op jit(solution)/shard_map/sum_parts/pallas_call | solution.py:297
Async XLA Ops:
  0.6 10.3 %collective-permute-start = (bf16[1024,128]{1,0:T(8,128)(2,1)}, bf16[1024,128]{1,0:T(8,128)(2,1)S(1)}, u32[]{:S(2)}, u32[]{:S(2)}) collective-permute-start(bf16[1024,128]{1,0:T(8,128)(2,1)} %bitcast.7), channel_id=1, source_target_pairs={{0,16},{1,17},{2,18},{3,19},{4,20},{5,21},{6,22},{7,23},{8,24},{9,... | collective-permute-start | bytes 786440 | tf_op jit(solution)/shard_map/ppermute | solution.py:37
  0.7 9.0 %collective-permute-start.2 = (bf16[64,1024]{1,0:T(8,128)(2,1)}, bf16[64,1024]{1,0:T(8,128)(2,1)S(1)}, u32[]{:S(2)}, u32[]{:S(2)}) collective-permute-start(bf16[64,1024]{1,0:T(8,128)(2,1)} %bitcast.12), channel_id=1, source_target_pairs={{0,8},{1,9},{2,10},{3,11},{4,12},{5,13},{6,14},{7,15},{8,0},{9,1},... | collective-permute-start | bytes 393224 | tf_op jit(solution)/shard_map/ppermute | solution.py:27
  3.4 14.9 %collective-permute-start.4 = (bf16[1024,128]{1,0:T(8,128)(2,1)}, bf16[1024,128]{1,0:T(8,128)(2,1)S(1)}, u32[]{:S(2)}, u32[]{:S(2)}) collective-permute-start(bf16[1024,128]{1,0:T(8,128)(2,1)} %bitcast.8), channel_id=1, source_target_pairs={{0,1},{1,0},{2,3},{3,2},{4,5},{5,4},{6,7},{7,6},{8,9},{9,8},{10,11... | collective-permute-start | bytes 786440 | tf_op jit(solution)/shard_map/ppermute | solution.py:27
  4.9 13.9 %collective-permute-start.5 = (bf16[1024,128]{1,0:T(8,128)(2,1)}, bf16[1024,128]{1,0:T(8,128)(2,1)S(1)}, u32[]{:S(2)}, u32[]{:S(2)}) collective-permute-start(bf16[1024,128]{1,0:T(8,128)(2,1)} %bitcast.9), channel_id=1, source_target_pairs={{0,2},{1,3},{2,0},{3,1},{4,6},{5,7},{6,4},{7,5},{8,10},{9,11},{10,... | collective-permute-start | bytes 786440 | tf_op jit(solution)/shard_map/ppermute | solution.py:27
  6.4 12.4 %collective-permute-start.6 = (bf16[1024,128]{1,0:T(8,128)(2,1)}, bf16[1024,128]{1,0:T(8,128)(2,1)S(1)}, u32[]{:S(2)}, u32[]{:S(2)}) collective-permute-start(bf16[1024,128]{1,0:T(8,128)(2,1)} %bitcast.10), channel_id=1, source_target_pairs={{0,3},{1,2},{2,1},{3,0},{4,7},{5,6},{6,5},{7,4},{8,11},{9,10},{10,... | collective-permute-start | bytes 786440 | tf_op jit(solution)/shard_map/ppermute | solution.py:27
  9.7 6.6 %collective-permute-start.1 = (bf16[64,1024]{1,0:T(8,128)(2,1)}, bf16[64,1024]{1,0:T(8,128)(2,1)S(1)}, u32[]{:S(2)}, u32[]{:S(2)}) collective-permute-start(bf16[64,1024]{1,0:T(8,128)(2,1)} %bitcast.13), channel_id=1, source_target_pairs={{0,4},{1,5},{2,6},{3,7},{4,0},{5,1},{6,2},{7,3},{8,12},{9,13},{10,... | collective-permute-start | bytes 393224 | tf_op jit(solution)/shard_map/ppermute | solution.py:27
  10.9 7.3 %collective-permute-start.3 = (bf16[64,1024]{1,0:T(8,128)(2,1)S(1)}, bf16[64,1024]{1,0:T(8,128)(2,1)S(1)}, u32[]{:S(2)}, u32[]{:S(2)}) collective-permute-start(bf16[64,1024]{1,0:T(8,128)(2,1)S(1)} %collective-permute-done.2.refs_2_), channel_id=1, source_target_pairs={{0,4},{1,5},{2,6},{3,7},{4,0},{5,1},{6,2},{7,3},{8,12},{9,13},{10,... | collective-permute-start | bytes 393224 | tf_op jit(solution)/shard_map/ppermute | solution.py:27
  11.8 0.9 %copy-start = (bf16[1,1024,128]{2,1,0:T(8,128)(2,1)S(1)}, bf16[1,1024,128]{2,1,0:T(8,128)(2,1)}, u32[]{:S(2)}) copy-start(bf16[1,1024,128]{2,1,0:T(8,128)(2,1)} %param.4) | copy-start | bytes 786436
  12.7 0.9 %copy-start.1 = (bf16[1,1,1024,128]{3,2,1,0:T(8,128)(2,1)S(1)}, bf16[1,1,1024,128]{3,2,1,0:T(8,128)(2,1)}, u32[]{:S(2)}) copy-start(bf16[1,1,1024,128]{3,2,1,0:T(8,128)(2,1)} %param.5) | copy-start | bytes 786436
  13.7 0.9 %copy-start.2 = (bf16[1,64,1024]{2,1,0:T(8,128)(2,1)S(1)}, bf16[1,64,1024]{2,1,0:T(8,128)(2,1)}, u32[]{:S(2)}) copy-start(bf16[1,64,1024]{2,1,0:T(8,128)(2,1)} %param.7) | copy-start | bytes 393220
  19.2 5.8 %collective-permute-start.7 = (bf16[256,128]{1,0:T(8,128)(2,1)S(1)}, bf16[256,128]{1,0:T(8,128)(2,1)S(1)}, u32[]{:S(2)}, u32[]{:S(2)}) collective-permute-start(bf16[256,128]{1,0:T(8,128)(2,1)S(1)} %get-tuple-element.27), channel_id=1, source_target_pairs={{0,1},{1,0},{2,3},{3,2},{4,5},{5,4},{6,7},{7,6},{8,9},{9,8},{10,11... | collective-permute-start | bytes 196616 | tf_op jit(solution)/shard_map/ppermute | solution.py:27
  20.5 4.9 %collective-permute-start.8 = (bf16[256,128]{1,0:T(8,128)(2,1)S(1)}, bf16[256,128]{1,0:T(8,128)(2,1)S(1)}, u32[]{:S(2)}, u32[]{:S(2)}) collective-permute-start(bf16[256,128]{1,0:T(8,128)(2,1)S(1)} %get-tuple-element.28), channel_id=1, source_target_pairs={{0,2},{1,3},{2,0},{3,1},{4,6},{5,7},{6,4},{7,5},{8,10},{9,11},{10,... | collective-permute-start | bytes 196616 | tf_op jit(solution)/shard_map/ppermute | solution.py:27
  21.8 5.2 %collective-permute-start.9 = (bf16[256,128]{1,0:T(8,128)(2,1)S(1)}, bf16[256,128]{1,0:T(8,128)(2,1)S(1)}, u32[]{:S(2)}, u32[]{:S(2)}) collective-permute-start(bf16[256,128]{1,0:T(8,128)(2,1)S(1)} %get-tuple-element.29), channel_id=1, source_target_pairs={{0,3},{1,2},{2,1},{3,0},{4,7},{5,6},{6,5},{7,4},{8,11},{9,10},{10,... | collective-permute-start | bytes 196616 | tf_op jit(solution)/shard_map/ppermute | solution.py:27
  28.3 2.6 %collective-permute-start.17 = (bf16[512,128]{1,0:T(8,128)(2,1)S(1)}, bf16[512,128]{1,0:T(8,128)(2,1)S(1)}, u32[]{:S(2)}, u32[]{:S(2)}) collective-permute-start(bf16[512,128]{1,0:T(8,128)(2,1)S(1)} %get-tuple-element.35), channel_id=1, source_target_pairs={{0,17},{1,16},{2,19},{3,18},{4,21},{5,20},{6,23},{7,22},{8,25},{9,... | collective-permute-start | bytes 393224 | tf_op jit(solution)/shard_map/ppermute | solution.py:37
  28.4 11.6 %collective-permute-start.14 = (bf16[1280,128]{1,0:T(8,128)(2,1)S(1)}, bf16[1280,128]{1,0:T(8,128)(2,1)S(1)}, u32[]{:S(2)}, u32[]{:S(2)}) collective-permute-start(bf16[1280,128]{1,0:T(8,128)(2,1)S(1)} %get-tuple-element.32), channel_id=1, source_target_pairs={{16,4},{17,5},{18,6},{19,7},{20,0},{21,1},{22,2},{23,3},{24,12},{2... | collective-permute-start | bytes 983048 | tf_op jit(solution)/shard_map/ppermute | solution.py:45
  28.9 3.9 %collective-permute-start.18 = (bf16[512,128]{1,0:T(8,128)(2,1)S(1)}, bf16[512,128]{1,0:T(8,128)(2,1)S(1)}, u32[]{:S(2)}, u32[]{:S(2)}) collective-permute-start(bf16[512,128]{1,0:T(8,128)(2,1)S(1)} %get-tuple-element.35), channel_id=1, source_target_pairs={{0,18},{1,19},{2,16},{3,17},{4,22},{5,23},{6,20},{7,21},{8,26},{9,... | collective-permute-start | bytes 393224 | tf_op jit(solution)/shard_map/ppermute | solution.py:37
  29.4 10.5 %collective-permute-start.10 = (bf16[1024,128]{1,0:T(8,128)(2,1)S(1)}, bf16[1024,128]{1,0:T(8,128)(2,1)S(1)}, u32[]{:S(2)}, u32[]{:S(2)}) collective-permute-start(bf16[1024,128]{1,0:T(8,128)(2,1)S(1)} %get-tuple-element.30), channel_id=1, source_target_pairs={{0,16},{1,17},{2,18},{3,19},{4,20},{5,21},{6,22},{7,23},{8,24},{9,... | collective-permute-start | bytes 786440 | tf_op jit(solution)/shard_map/ppermute | solution.py:37
  29.4 12.0 %collective-permute-start.15 = (bf16[1280,128]{1,0:T(8,128)(2,1)S(1)}, bf16[1280,128]{1,0:T(8,128)(2,1)S(1)}, u32[]{:S(2)}, u32[]{:S(2)}) collective-permute-start(bf16[1280,128]{1,0:T(8,128)(2,1)S(1)} %get-tuple-element.33), channel_id=1, source_target_pairs={{16,8},{17,9},{18,10},{19,11},{20,12},{21,13},{22,14},{23,15},{24,... | collective-permute-start | bytes 983048 | tf_op jit(solution)/shard_map/ppermute | solution.py:45
  30.9 17.1 %collective-permute-start.16 = (bf16[1280,128]{1,0:T(8,128)(2,1)S(1)}, bf16[1280,128]{1,0:T(8,128)(2,1)S(1)}, u32[]{:S(2)}, u32[]{:S(2)}) collective-permute-start(bf16[1280,128]{1,0:T(8,128)(2,1)S(1)} %get-tuple-element.34), channel_id=1, source_target_pairs={{16,12},{17,13},{18,14},{19,15},{20,8},{21,9},{22,10},{23,11},{24,... | collective-permute-start | bytes 983048 | tf_op jit(solution)/shard_map/ppermute | solution.py:45
  32.8 4.0 %collective-permute-start.19 = (bf16[512,128]{1,0:T(8,128)(2,1)S(1)}, bf16[512,128]{1,0:T(8,128)(2,1)S(1)}, u32[]{:S(2)}, u32[]{:S(2)}) collective-permute-start(bf16[512,128]{1,0:T(8,128)(2,1)S(1)} %get-tuple-element.35), channel_id=1, source_target_pairs={{0,19},{1,18},{2,17},{3,16},{4,23},{5,22},{6,21},{7,20},{8,27},{9,... | collective-permute-start | bytes 393224 | tf_op jit(solution)/shard_map/ppermute | solution.py:37
  36.8 11.5 %collective-permute-start.11 = (bf16[512,128]{1,0:T(8,128)(2,1)S(1)}, bf16[512,128]{1,0:T(8,128)(2,1)S(1)}, u32[]{:S(2)}, u32[]{:S(2)}) collective-permute-start(bf16[512,128]{1,0:T(8,128)(2,1)S(1)} %get-tuple-element.31), channel_id=1, source_target_pairs={{0,17},{1,16},{2,19},{3,18},{4,21},{5,20},{6,23},{7,22},{8,25},{9,... | collective-permute-start | bytes 393224 | tf_op jit(solution)/shard_map/ppermute | solution.py:37
  39.9 8.4 %collective-permute-start.12 = (bf16[512,128]{1,0:T(8,128)(2,1)S(1)}, bf16[512,128]{1,0:T(8,128)(2,1)S(1)}, u32[]{:S(2)}, u32[]{:S(2)}) collective-permute-start(bf16[512,128]{1,0:T(8,128)(2,1)S(1)} %get-tuple-element.31), channel_id=1, source_target_pairs={{0,18},{1,19},{2,16},{3,17},{4,22},{5,23},{6,20},{7,21},{8,26},{9,... | collective-permute-start | bytes 393224 | tf_op jit(solution)/shard_map/ppermute | solution.py:37
  39.9 8.4 %collective-permute-start.13 = (bf16[512,128]{1,0:T(8,128)(2,1)S(1)}, bf16[512,128]{1,0:T(8,128)(2,1)S(1)}, u32[]{:S(2)}, u32[]{:S(2)}) collective-permute-start(bf16[512,128]{1,0:T(8,128)(2,1)S(1)} %get-tuple-element.31), channel_id=1, source_target_pairs={{0,19},{1,18},{2,17},{3,16},{4,23},{5,22},{6,21},{7,20},{8,27},{9,... | collective-permute-start | bytes 393224 | tf_op jit(solution)/shard_map/ppermute | solution.py:37
  48.7 10.2 %collective-permute-start.20 = (bf16[64,1024]{1,0:T(8,128)(2,1)S(1)}, bf16[64,1024]{1,0:T(8,128)(2,1)S(1)}, u32[]{:S(2)}, u32[]{:S(2)}) collective-permute-start(bf16[64,1024]{1,0:T(8,128)(2,1)S(1)} %get-tuple-element.37), channel_id=1, source_target_pairs={{0,1},{1,0},{2,3},{3,2},{4,5},{5,4},{6,7},{7,6},{8,9},{9,8},{10,11... | collective-permute-start | bytes 393224 | tf_op jit(solution)/shard_map/ppermute | solution.py:55
  49.3 7.0 %collective-permute-start.21 = (bf16[64,512]{1,0:T(8,128)(2,1)S(1)}, bf16[64,512]{1,0:T(8,128)(2,1)S(1)}, u32[]{:S(2)}, u32[]{:S(2)}) collective-permute-start(bf16[64,512]{1,0:T(8,128)(2,1)S(1)} %get-tuple-element.39), channel_id=1, source_target_pairs={{0,2},{1,3},{2,0},{3,1},{4,6},{5,7},{6,4},{7,5},{8,10},{9,11},{10,... | collective-permute-start | bytes 196616 | tf_op jit(solution)/shard_map/ppermute | solution.py:55
  50.7 5.6 %collective-permute-start.22 = (bf16[64,512]{1,0:T(8,128)(2,1)S(1)}, bf16[64,512]{1,0:T(8,128)(2,1)S(1)}, u32[]{:S(2)}, u32[]{:S(2)}) collective-permute-start(bf16[64,512]{1,0:T(8,128)(2,1)S(1)} %get-tuple-element.40), channel_id=1, source_target_pairs={{0,3},{1,2},{2,1},{3,0},{4,7},{5,6},{6,5},{7,4},{8,11},{9,10},{10,... | collective-permute-start | bytes 196616 | tf_op jit(solution)/shard_map/ppermute | solution.py:55
  52.2 4.4 %collective-permute-start.23 = (bf16[64,512]{1,0:T(8,128)(2,1)S(1)}, bf16[64,512]{1,0:T(8,128)(2,1)S(1)}, u32[]{:S(2)}, u32[]{:S(2)}) collective-permute-start(bf16[64,512]{1,0:T(8,128)(2,1)S(1)} %get-tuple-element.42), channel_id=1, source_target_pairs={{0,2},{1,3},{2,0},{3,1},{4,6},{5,7},{6,4},{7,5},{8,10},{9,11},{10,... | collective-permute-start | bytes 196616 | tf_op jit(solution)/shard_map/ppermute | solution.py:55
  53.7 5.2 %collective-permute-start.24 = (bf16[64,512]{1,0:T(8,128)(2,1)S(1)}, bf16[64,512]{1,0:T(8,128)(2,1)S(1)}, u32[]{:S(2)}, u32[]{:S(2)}) collective-permute-start(bf16[64,512]{1,0:T(8,128)(2,1)S(1)} %get-tuple-element.43), channel_id=1, source_target_pairs={{0,3},{1,2},{2,1},{3,0},{4,7},{5,6},{6,5},{7,4},{8,11},{9,10},{10,... | collective-permute-start | bytes 196616 | tf_op jit(solution)/shard_map/ppermute | solution.py:55

commit v5 on v4

--- a/solution.py
+++ b/solution.py
@@ -162,6 +162,7 @@
 
 def advance_kernel(line, plane, counts, *refs):
     top, moved, refs = refs[0], refs[1 : 1 + counts[0]], refs[1 + counts[0] :]
+    ready, refs = refs[: counts[2]], refs[counts[2] :]
     pieces, weights, outs, diff = refs[:plane], refs[plane], refs[plane + 1 : -1], refs[-1]
     outs, whole = outs[: counts[1]], outs[-1]
     me = lax.axis_index("freq")
@@ -187,36 +188,46 @@
             return
         subtract(moved[0])
 
-    straight = diff[...]
-    half = cols // 2
-    turned = jnp.concatenate([-straight[:, half:], straight[:, :half]], axis=1)
-    tall = top.shape[0] // counts[1]
-    for h, out in enumerate(outs):
-        part = slice(h * tall, (h + 1) * tall)
-        below = (
-            jnp.dot(weights[0, part, :], straight, preferred_element_type=jnp.float32)
-            + jnp.dot(weights[1, part, :], turned, preferred_element_type=jnp.float32)
-        ).astype(jnp.bfloat16)
-        out[...] = below
-        if counts[1] > 1:
-            whole[part, :] = below
-
-
-def advance(top, moved, pieces, weights, line, plane, parts):
+    def extrapolate():
+        straight = diff[...]
+        half = cols // 2
+        turned = jnp.concatenate([-straight[:, half:], straight[:, :half]], axis=1)
+        tall = top.shape[0] // counts[1]
+        for h, out in enumerate(outs):
+            part = slice(h * tall, (h + 1) * tall)
+            below = (
+                jnp.dot(weights[0, part, :], straight, preferred_element_type=jnp.float32)
+                + jnp.dot(weights[1, part, :], turned, preferred_element_type=jnp.float32)
+            ).astype(jnp.bfloat16)
+            out[...] = below
+            if counts[1] > 1:
+                whole[part, :] = below
+
+    if not ready:
+        extrapolate()
+        return
+    pl.when(jnp.logical_not(first))(extrapolate)
+
+    @pl.when(first)
+    def _():
+        outs[0][...] = ready[0][...]
+
+
+def advance(top, moved, ready, pieces, weights, line, plane, parts):
     nx, cols = top.shape
     outs = [jax.ShapeDtypeStruct((nx // parts, cols), jnp.bfloat16)] * parts
     if parts > 1:
         outs.append(jax.ShapeDtypeStruct((nx, cols), jnp.bfloat16))
     return pl.pallas_call(
-        functools.partial(advance_kernel, line, plane, (len(moved), parts)),
+        functools.partial(advance_kernel, line, plane, (len(moved), parts, len(ready))),
         out_shape=outs,
-        in_specs=[VMEM] * (2 + len(moved) + plane),
+        in_specs=[VMEM] * (2 + len(moved) + len(ready) + plane),
         out_specs=[VMEM] * len(outs),
         scratch_shapes=[pltpu.VMEM((nx, cols), jnp.bfloat16)],
         compiler_params=params(24 * MIB),
         cost_estimate=pl.CostEstimate(flops=4 * nx * nx * cols, bytes_accessed=4 * nx * nx, transcendentals=0),
         name="advance",
-    )(top, *moved, *pieces, weights)
+    )(top, *moved, *ready, *pieces, weights)
 
 
 def stacked_rows(ref, starts, rows):
@@ -327,7 +338,7 @@
 
     moved = []
     for _ in range(1, sections):
-        *halves, below = advance(top, moved, pieces, weights, line, plane, HALVES)
+        *halves, below = advance(top, moved, [], pieces, weights, line, plane, HALVES)
         moved = [lower(below, 0)]
     scale = (float(upper.shape[1]) * devices) ** (-0.5)
     parts, sums = None, []
@@ -337,7 +348,7 @@
         alone = [k for k in range(1, len(parts)) if k not in JOINED]
         sums.append([parts[0]] + [reduce_step(parts[k], k, plane, line) for k in alone])
     joined = [reduce_step(parts[k], k, plane, line) for k in JOINED]
-    (below,) = advance(top, moved, pieces, weights, line, plane, 1)
+    (below,) = advance(top, moved, [below], pieces, weights, line, plane, 1)
     return (below[None, None], summed(joined, sums, scale)[None])
 
 

time: 59.8 us -> 59.8 us (level)
  waiting for transfers between devices: 21 us -> 22.3 us
  Pallas kernels: 8.15 us -> 6.86 us
    ppermute x5, waiting for transfers between devices: 2.57 us -> 3.86 us  [reduce_step(): return lax.ppermute(value, ('depth', 'freq'), pairs)]
    pallas_call x2, Pallas kernels: 3.44 us -> 2.15 us  [advance(): pl.pallas_call(functools.partial(advance_kernel, line, plane, (len(moved)...]
  transfers between devices with their start and end apart: 25 -> 25, of which waited for: 11 -> 12; matrix products, arithmetic and copies ran while one was open for 0% -> 0% of each run, Pallas kernels for 9% -> 7%
where the time goes in v5:
time: 59.8 us; the launch traced here: 59.6 us
  starting transfers between devices  26.9 us (45%)
  waiting for transfers between devices  22.3 us (37%)
  Pallas kernels  6.86 us (11%)
  local copies, waits for them, and re-layouts  2.8 us (5%)
  between operations  0.75 us (1%)
    ppermute x9, starting transfers between devices, swap(): return lax.ppermute(value, 'freq', [(i, i ^ by) for i in range(devices)])  11.7 us
    ppermute x9, waiting for transfers between devices, swap(): return lax.ppermute(value, 'freq', [(i, i ^ by) for i in range(devices)])  8.39 us
    ppermute x8, starting transfers between devices, lower(): return lax.ppermute(value, ('depth', 'freq'), pairs)  6.78 us
    ppermute x3, waiting for transfers between devices, raise_top(): return lax.ppermute(value, ('depth', 'freq'), pairs)  6.53 us
    ppermute x5, starting transfers between devices, reduce_step(): return lax.ppermute(value, ('depth', 'freq'), pairs)  5.55 us
    ppermute x5, waiting for transfers between devices, reduce_step(): return lax.ppermute(value, ('depth', 'freq'), pairs)  3.86 us
    ppermute x8, waiting for transfers between devices, lower(): return lax.ppermute(value, ('depth', 'freq'), pairs)  3.51 us
    ppermute x3, starting transfers between devices, raise_top(): return lax.ppermute(value, ('depth', 'freq'), pairs)  2.89 us
  transfers between devices with their start and end apart: 25, of which 12 were waited for; matrix products, arithmetic and copies ran while one was open for 0% of the time, Pallas kernels for 7%

profile of v5, /device:TPU:8, one launch (start us, length us, event | category | flops | bytes accessed | tf_op | source)
XLA Modules:
  0.0 59.6 jit_solution(10848529232953677197)
XLA Ops:
  0.6 0.1 collective-permute-start
  0.7 2.7 %collective-permute-start.2 = (bf16[64,1024]{1,0:T(8,128)(2,1)}, bf16[64,1024]{1,0:T(8,128)(2,1)S(1)}, u32[]{:S(2)}, u32[]{:S(2)}) collective-permute-start(bf16[64,1024]{1,0:T(8,128)(2,1)} %bitcast.12), channel_id=1, source_target_pairs={{0,8},{1,9},{2,10},{3,11},{4,12},{5,13},{6,14},{7,15},{8,0},{9,1},... | collective-permute-start | bytes 393224 | tf_op jit(solution)/shard_map/ppermute | solution.py:27
  3.4 1.5 %collective-permute-start.4 = (bf16[1024,128]{1,0:T(8,128)(2,1)}, bf16[1024,128]{1,0:T(8,128)(2,1)S(1)}, u32[]{:S(2)}, u32[]{:S(2)}) collective-permute-start(bf16[1024,128]{1,0:T(8,128)(2,1)} %bitcast.8), channel_id=1, source_target_pairs={{0,1},{1,0},{2,3},{3,2},{4,5},{5,4},{6,7},{7,6},{8,9},{9,8},{10,11... | collective-permute-start | bytes 786440 | tf_op jit(solution)/shard_map/ppermute | solution.py:27
  4.9 1.5 %collective-permute-start.5 = (bf16[1024,128]{1,0:T(8,128)(2,1)}, bf16[1024,128]{1,0:T(8,128)(2,1)S(1)}, u32[]{:S(2)}, u32[]{:S(2)}) collective-permute-start(bf16[1024,128]{1,0:T(8,128)(2,1)} %bitcast.9), channel_id=1, source_target_pairs={{0,2},{1,3},{2,0},{3,1},{4,6},{5,7},{6,4},{7,5},{8,10},{9,11},{10,... | collective-permute-start | bytes 786440 | tf_op jit(solution)/shard_map/ppermute | solution.py:27
  6.4 0.5 collective-permute-start.6
  6.9 2.9 %collective-permute-done.2.refs_2_ = bf16[64,1024]{1,0:T(8,128)(2,1)S(1)} collective-permute-done((bf16[64,1024]{1,0:T(8,128)(2,1)}, bf16[64,1024]{1,0:T(8,128)(2,1)S(1)}, u32[]{:S(2)}, u32[]{:S(2)}) %collective-permute-start.2) | collective-permute-done | bytes 131104 | tf_op jit(solution)/shard_map/ppermute | solution.py:27
  9.7 1.2 %collective-permute-start.1 = (bf16[64,1024]{1,0:T(8,128)(2,1)}, bf16[64,1024]{1,0:T(8,128)(2,1)S(1)}, u32[]{:S(2)}, u32[]{:S(2)}) collective-permute-start(bf16[64,1024]{1,0:T(8,128)(2,1)} %bitcast.13), channel_id=1, source_target_pairs={{0,4},{1,5},{2,6},{3,7},{4,0},{5,1},{6,2},{7,3},{8,12},{9,13},{10,... | collective-permute-start | bytes 393224 | tf_op jit(solution)/shard_map/ppermute | solution.py:27
  10.9 0.0 collective-permute-done.refs_3_
  10.9 0.8 %collective-permute-start.3 = (bf16[64,1024]{1,0:T(8,128)(2,1)S(1)}, bf16[64,1024]{1,0:T(8,128)(2,1)S(1)}, u32[]{:S(2)}, u32[]{:S(2)}) collective-permute-start(bf16[64,1024]{1,0:T(8,128)(2,1)S(1)} %collective-permute-done.2.refs_2_), channel_id=1, source_target_pairs={{0,4},{1,5},{2,6},{3,7},{4,0},{5,1},{6,2},{7,3},{8,12},{9,13},{10,... | collective-permute-start | bytes 393224 | tf_op jit(solution)/shard_map/ppermute | solution.py:27
  11.8 0.0 copy-start
  11.8 0.9 %copy-done = bf16[1,1024,128]{2,1,0:T(8,128)(2,1)S(1)} copy-done((bf16[1,1024,128]{2,1,0:T(8,128)(2,1)S(1)}, bf16[1,1024,128]{2,1,0:T(8,128)(2,1)}, u32[]{:S(2)}) %copy-start) | copy-done | bytes 262168
  12.7 0.0 copy-start.1
  12.7 0.9 %copy-done.1 = bf16[1,1,1024,128]{3,2,1,0:T(8,128)(2,1)S(1)} copy-done((bf16[1,1,1024,128]{3,2,1,0:T(8,128)(2,1)S(1)}, bf16[1,1,1024,128]{3,2,1,0:T(8,128)(2,1)}, u32[]{:S(2)}) %copy-start.1) | copy-done | bytes 262168
  13.7 0.0 copy-start.2
  13.7 0.9 %copy-done.2 = bf16[1,64,1024]{2,1,0:T(8,128)(2,1)S(1)} copy-done((bf16[1,64,1024]{2,1,0:T(8,128)(2,1)S(1)}, bf16[1,64,1024]{2,1,0:T(8,128)(2,1)}, u32[]{:S(2)}) %copy-start.2) | copy-done | bytes 131096
  14.6 0.6 %stage_inputs.1 = (bf16[1024,128]{1,0:T(8,128)(2,1)S(1)}, bf16[1024,128]{1,0:T(8,128)(2,1)S(1)}, bf16[64,1024]{1,0:T(8,128)(2,1)S(1)}, bf16[1280,128]{1,0:T(8,12...) custom-call(bf16[1024,128]{1,0:T(8,128)(2,1)S(1)} %bitcast.6, bf16[1024,128]{1,0:T(8,128)(2,1)S(1)} %bitcast.11, ...), custom_call_target="tpu_custom_call" | custom-call | bytes 3276800 | tf_op jit(solution)/shard_map/stage_inputs/pallas_call | solution.py:109
  15.2 1.1 %collective-permute-done.1.refs_1_ = bf16[64,1024]{1,0:T(8,128)(2,1)S(1)} collective-permute-done((bf16[64,1024]{1,0:T(8,128)(2,1)}, bf16[64,1024]{1,0:T(8,128)(2,1)S(1)}, u32[]{:S(2)}, u32[]{:S(2)}) %collective-permute-start.1) | collective-permute-done | bytes 131104 | tf_op jit(solution)/shard_map/ppermute | solution.py:27
  16.3 1.9 %collective-permute-done.3.refs_3_ = bf16[64,1024]{1,0:T(8,128)(2,1)S(1)} collective-permute-done((bf16[64,1024]{1,0:T(8,128)(2,1)S(1)}, bf16[64,1024]{1,0:T(8,128)(2,1)S(1)}, u32[]{:S(2)}, u32[]{:S(2)}) %collective-permute-start.3) | collective-permute-done | bytes 131104 | tf_op jit(solution)/shard_map/ppermute | solution.py:27
  18.2 0.0 collective-permute-done.4.refs_5_.refs_1_
  18.2 0.5 collective-permute-done.5.refs_6_.refs_2_
  18.8 0.0 collective-permute-done.6.refs_7_.refs_3_
  18.8 0.4 rq_pieces.1
  19.2 1.3 %collective-permute-start.7 = (bf16[256,128]{1,0:T(8,128)(2,1)S(1)}, bf16[256,128]{1,0:T(8,128)(2,1)S(1)}, u32[]{:S(2)}, u32[]{:S(2)}) collective-permute-start(bf16[256,128]{1,0:T(8,128)(2,1)S(1)} %get-tuple-element.27), channel_id=1, source_target_pairs={{0,1},{1,0},{2,3},{3,2},{4,5},{5,4},{6,7},{7,6},{8,9},{9,8},{10,11... | collective-permute-start | bytes 196616 | tf_op jit(solution)/shard_map/ppermute | solution.py:27
  20.5 1.2 %collective-permute-start.8 = (bf16[256,128]{1,0:T(8,128)(2,1)S(1)}, bf16[256,128]{1,0:T(8,128)(2,1)S(1)}, u32[]{:S(2)}, u32[]{:S(2)}) collective-permute-start(bf16[256,128]{1,0:T(8,128)(2,1)S(1)} %get-tuple-element.28), channel_id=1, source_target_pairs={{0,2},{1,3},{2,0},{3,1},{4,6},{5,7},{6,4},{7,5},{8,10},{9,11},{10,... | collective-permute-start | bytes 196616 | tf_op jit(solution)/shard_map/ppermute | solution.py:27
  21.8 1.0 %collective-permute-start.9 = (bf16[256,128]{1,0:T(8,128)(2,1)S(1)}, bf16[256,128]{1,0:T(8,128)(2,1)S(1)}, u32[]{:S(2)}, u32[]{:S(2)}) collective-permute-start(bf16[256,128]{1,0:T(8,128)(2,1)S(1)} %get-tuple-element.29), channel_id=1, source_target_pairs={{0,3},{1,2},{2,1},{3,0},{4,7},{5,6},{6,5},{7,4},{8,11},{9,10},{10,... | collective-permute-start | bytes 196616 | tf_op jit(solution)/shard_map/ppermute | solution.py:27
  22.8 2.2 %stage_weights.1.refs_5_.refs_7_ = bf16[2,1024,1024]{2,1,0:T(8,128)(2,1)S(1)} custom-call(bf16[2,1024,1024]{2,1,0:T(8,128)(2,1)} %bitcast.15), custom_call_target="tpu_custom_call" | custom-call | bytes 8388608 | tf_op jit(solution)/shard_map/stage_weights/pallas_call | solution.py:78
  25.0 0.0 collective-permute-done.7.refs_2_.refs_4_
  25.0 0.4 collective-permute-done.8.refs_3_.refs_5_
  25.4 1.5 %collective-permute-done.9.refs_4_.refs_6_ = bf16[256,128]{1,0:T(8,128)(2,1)S(1)} collective-permute-done((bf16[256,128]{1,0:T(8,128)(2,1)S(1)}, bf16[256,128]{1,0:T(8,128)(2,1)S(1)}, u32[]{:S(2)}, u32[]{:S(2)}) %collective-permute-start.9) | collective-permute-done | bytes 65568 | tf_op jit(solution)/shard_map/ppermute | solution.py:27
  26.9 1.4 %advance.2 = (bf16[512,128]{1,0:T(8,128)(2,1)S(1)}, bf16[512,128]{1,0:T(8,128)(2,1)S(1)}, bf16[1024,128]{1,0:T(8,128)(2,1)S(1)}) custom-call(bf16[1024,128]{1,0:T(8,128)(2,1)S(1)} %get-tuple-element.23.refs_0_.refs_8_, f32[256,128]{1,0:T(8,128)S(1)} %get-tuple-element.26.refs_1_.refs_3_, bf16[256,128]{1,0:T(8,128)(2,1)S(1)} %collective-permute-done.7.refs_2_.refs_4_, ...), custom_call_target="tpu_custom_call" | custom-call | flops 536870912 | bytes 4194304 | tf_op jit(solution)/shard_map/advance/pallas_call | solution.py:221
  28.3 0.1 collective-permute-start.17
  28.4 0.5 collective-permute-start.14
  28.9 0.5 collective-permute-start.18
  29.4 0.0 collective-permute-start.10
  29.4 0.5 collective-permute-start.15
  29.9 1.0 %collective-permute-done.17.refs_5_ = bf16[512,128]{1,0:T(8,128)(2,1)S(1)} collective-permute-done((bf16[512,128]{1,0:T(8,128)(2,1)S(1)}, bf16[512,128]{1,0:T(8,128)(2,1)S(1)}, u32[]{:S(2)}, u32[]{:S(2)}) %collective-permute-start.17) | collective-permute-done | bytes 131104 | tf_op jit(solution)/shard_map/ppermute | solution.py:37
  30.9 1.9 %collective-permute-start.16 = (bf16[1280,128]{1,0:T(8,128)(2,1)S(1)}, bf16[1280,128]{1,0:T(8,128)(2,1)S(1)}, u32[]{:S(2)}, u32[]{:S(2)}) collective-permute-start(bf16[1280,128]{1,0:T(8,128)(2,1)S(1)} %get-tuple-element.34), channel_id=1, source_target_pairs={{16,12},{17,13},{18,14},{19,15},{20,8},{21,9},{22,10},{23,11},{24,... | collective-permute-start | bytes 983048 | tf_op jit(solution)/shard_map/ppermute | solution.py:45
  32.8 0.0 collective-permute-done.18.refs_6_
  32.8 1.5 %collective-permute-start.19 = (bf16[512,128]{1,0:T(8,128)(2,1)S(1)}, bf16[512,128]{1,0:T(8,128)(2,1)S(1)}, u32[]{:S(2)}, u32[]{:S(2)}) collective-permute-start(bf16[512,128]{1,0:T(8,128)(2,1)S(1)} %get-tuple-element.35), channel_id=1, source_target_pairs={{0,19},{1,18},{2,17},{3,16},{4,23},{5,22},{6,21},{7,20},{8,27},{9,... | collective-permute-start | bytes 393224 | tf_op jit(solution)/shard_map/ppermute | solution.py:37
  34.3 2.5 %collective-permute-done.19.refs_7_ = bf16[512,128]{1,0:T(8,128)(2,1)S(1)} collective-permute-done((bf16[512,128]{1,0:T(8,128)(2,1)S(1)}, bf16[512,128]{1,0:T(8,128)(2,1)S(1)}, u32[]{:S(2)}, u32[]{:S(2)}) %collective-permute-start.19) | collective-permute-done | bytes 131104 | tf_op jit(solution)/shard_map/ppermute | solution.py:37
  36.8 3.1 %collective-permute-start.11 = (bf16[512,128]{1,0:T(8,128)(2,1)S(1)}, bf16[512,128]{1,0:T(8,128)(2,1)S(1)}, u32[]{:S(2)}, u32[]{:S(2)}) collective-permute-start(bf16[512,128]{1,0:T(8,128)(2,1)S(1)} %get-tuple-element.31), channel_id=1, source_target_pairs={{0,17},{1,16},{2,19},{3,18},{4,21},{5,20},{6,23},{7,22},{8,25},{9,... | collective-permute-start | bytes 393224 | tf_op jit(solution)/shard_map/ppermute | solution.py:37
  39.9 0.0 collective-permute-done.10.refs_1_.refs_4_
  39.9 0.0 collective-permute-start.12
  39.9 0.0 collective-permute-done.14.refs_9_
  39.9 1.5 %collective-permute-start.13 = (bf16[512,128]{1,0:T(8,128)(2,1)S(1)}, bf16[512,128]{1,0:T(8,128)(2,1)S(1)}, u32[]{:S(2)}, u32[]{:S(2)}) collective-permute-start(bf16[512,128]{1,0:T(8,128)(2,1)S(1)} %get-tuple-element.31), channel_id=1, source_target_pairs={{0,19},{1,18},{2,17},{3,16},{4,23},{5,22},{6,21},{7,20},{8,27},{9,... | collective-permute-start | bytes 393224 | tf_op jit(solution)/shard_map/ppermute | solution.py:37
  41.4 0.0 collective-permute-done.15.refs_10_
  41.4 6.5 %collective-permute-done.16.refs_11_ = bf16[1280,128]{1,0:T(8,128)(2,1)S(1)} collective-permute-done((bf16[1280,128]{1,0:T(8,128)(2,1)S(1)}, bf16[1280,128]{1,0:T(8,128)(2,1)S(1)}, u32[]{:S(2)}, u32[]{:S(2)}) %collective-permute-start.16) | collective-permute-done | bytes 327712 | tf_op jit(solution)/shard_map/ppermute | solution.py:45
  47.9 0.3 picture_parts.2
  48.3 0.0 collective-permute-done.11.refs_5_
  48.3 0.0 collective-permute-done.12.refs_6_
  48.3 0.0 collective-permute-done.13.refs_7_
  48.3 0.4 picture_parts.3
  48.7 0.6 collective-permute-start.20
  49.3 1.5 %collective-permute-start.21 = (bf16[64,512]{1,0:T(8,128)(2,1)S(1)}, bf16[64,512]{1,0:T(8,128)(2,1)S(1)}, u32[]{:S(2)}, u32[]{:S(2)}) collective-permute-start(bf16[64,512]{1,0:T(8,128)(2,1)S(1)} %get-tuple-element.39), channel_id=1, source_target_pairs={{0,2},{1,3},{2,0},{3,1},{4,6},{5,7},{6,4},{7,5},{8,10},{9,11},{10,... | collective-permute-start | bytes 196616 | tf_op jit(solution)/shard_map/ppermute | solution.py:55
  50.7 1.5 %collective-permute-start.22 = (bf16[64,512]{1,0:T(8,128)(2,1)S(1)}, bf16[64,512]{1,0:T(8,128)(2,1)S(1)}, u32[]{:S(2)}, u32[]{:S(2)}) collective-permute-start(bf16[64,512]{1,0:T(8,128)(2,1)S(1)} %get-tuple-element.40), channel_id=1, source_target_pairs={{0,3},{1,2},{2,1},{3,0},{4,7},{5,6},{6,5},{7,4},{8,11},{9,10},{10,... | collective-permute-start | bytes 196616 | tf_op jit(solution)/shard_map/ppermute | solution.py:55
  52.2 1.5 %collective-permute-start.23 = (bf16[64,512]{1,0:T(8,128)(2,1)S(1)}, bf16[64,512]{1,0:T(8,128)(2,1)S(1)}, u32[]{:S(2)}, u32[]{:S(2)}) collective-permute-start(bf16[64,512]{1,0:T(8,128)(2,1)S(1)} %get-tuple-element.42), channel_id=1, source_target_pairs={{0,2},{1,3},{2,0},{3,1},{4,6},{5,7},{6,4},{7,5},{8,10},{9,11},{10,... | collective-permute-start | bytes 196616 | tf_op jit(solution)/shard_map/ppermute | solution.py:55
  53.7 0.5 collective-permute-start.24
  54.2 0.8 %advance.3 = bf16[1024,128]{1,0:T(8,128)(2,1)} custom-call(bf16[1024,128]{1,0:T(8,128)(2,1)S(1)} %get-tuple-element.23.refs_0_.refs_8_, bf16[1024,128]{1,0:T(8,128)(2,1)S(1)} %collective-permute-done.10.refs_1_.refs_4_, bf16[1024,128]{1,0:T(8,128)(2,1)S(1)} %get-tuple-element.30.refs_2_, f32[256,128]{1,0:T(8,128)S(1)} %get-tuple-element.26.refs_1_.refs_3_, ...), custom_call_target="tpu_custom_call" | custom-call | flops 536870912 | bytes 4194304 | tf_op jit(solution)/shard_map/advance/pallas_call | solution.py:221
  55.0 0.0 collective-permute-done.21.refs_2_
  55.0 0.9 %collective-permute-done.22.refs_3_ = bf16[64,512]{1,0:T(8,128)(2,1)S(1)} collective-permute-done((bf16[64,512]{1,0:T(8,128)(2,1)S(1)}, bf16[64,512]{1,0:T(8,128)(2,1)S(1)}, u32[]{:S(2)}, u32[]{:S(2)}) %collective-permute-start.22) | collective-permute-done | bytes 65568 | tf_op jit(solution)/shard_map/ppermute | solution.py:55
  55.9 0.7 %collective-permute-done.23.refs_5_ = bf16[64,512]{1,0:T(8,128)(2,1)S(1)} collective-permute-done((bf16[64,512]{1,0:T(8,128)(2,1)S(1)}, bf16[64,512]{1,0:T(8,128)(2,1)S(1)}, u32[]{:S(2)}, u32[]{:S(2)}) %collective-permute-start.23) | collective-permute-done | bytes 65568 | tf_op jit(solution)/shard_map/ppermute | solution.py:55
  56.6 2.3 %collective-permute-done.24.refs_6_ = bf16[64,512]{1,0:T(8,128)(2,1)S(1)} collective-permute-done((bf16[64,512]{1,0:T(8,128)(2,1)S(1)}, bf16[64,512]{1,0:T(8,128)(2,1)S(1)}, u32[]{:S(2)}, u32[]{:S(2)}) %collective-permute-start.24) | collective-permute-done | bytes 65568 | tf_op jit(solution)/shard_map/ppermute | solution.py:55
  58.9 0.0 collective-permute-done.20.refs_0_
  58.9 0.8 %sum_parts.1 = f32[64,1024]{1,0:T(8,128)} custom-call(bf16[64,1024]{1,0:T(8,128)(2,1)S(1)} %collective-permute-done.20.refs_0_, f32[64,512]{1,0:T(8,128)S(1)} %get-tuple-element.38.refs_1_, bf16[64,512]{1,0:T(8,128)(2,1)S(1)} %collective-permute-done.21.refs_2_, bf16[64,512]{1,0:T(8,128)(2,1)S(1)} %collective-permute-done.22.refs_3_, ...), custom_call_target="tpu_custom_call" | custom-call | flops 262144 | bytes 524288 | tf_op jit(solution)/shard_map/sum_parts/pallas_call | solution.py:308
Async XLA Ops:
  0.6 10.3 %collective-permute-start = (bf16[1024,128]{1,0:T(8,128)(2,1)}, bf16[1024,128]{1,0:T(8,128)(2,1)S(1)}, u32[]{:S(2)}, u32[]{:S(2)}) collective-permute-start(bf16[1024,128]{1,0:T(8,128)(2,1)} %bitcast.7), channel_id=1, source_target_pairs={{0,16},{1,17},{2,18},{3,19},{4,20},{5,21},{6,22},{7,23},{8,24},{9,... | collective-permute-start | bytes 786440 | tf_op jit(solution)/shard_map/ppermute | solution.py:37
  0.7 9.0 %collective-permute-start.2 = (bf16[64,1024]{1,0:T(8,128)(2,1)}, bf16[64,1024]{1,0:T(8,128)(2,1)S(1)}, u32[]{:S(2)}, u32[]{:S(2)}) collective-permute-start(bf16[64,1024]{1,0:T(8,128)(2,1)} %bitcast.12), channel_id=1, source_target_pairs={{0,8},{1,9},{2,10},{3,11},{4,12},{5,13},{6,14},{7,15},{8,0},{9,1},... | collective-permute-start | bytes 393224 | tf_op jit(solution)/shard_map/ppermute | solution.py:27
  3.4 14.9 %collective-permute-start.4 = (bf16[1024,128]{1,0:T(8,128)(2,1)}, bf16[1024,128]{1,0:T(8,128)(2,1)S(1)}, u32[]{:S(2)}, u32[]{:S(2)}) collective-permute-start(bf16[1024,128]{1,0:T(8,128)(2,1)} %bitcast.8), channel_id=1, source_target_pairs={{0,1},{1,0},{2,3},{3,2},{4,5},{5,4},{6,7},{7,6},{8,9},{9,8},{10,11... | collective-permute-start | bytes 786440 | tf_op jit(solution)/shard_map/ppermute | solution.py:27
  4.9 13.9 %collective-permute-start.5 = (bf16[1024,128]{1,0:T(8,128)(2,1)}, bf16[1024,128]{1,0:T(8,128)(2,1)S(1)}, u32[]{:S(2)}, u32[]{:S(2)}) collective-permute-start(bf16[1024,128]{1,0:T(8,128)(2,1)} %bitcast.9), channel_id=1, source_target_pairs={{0,2},{1,3},{2,0},{3,1},{4,6},{5,7},{6,4},{7,5},{8,10},{9,11},{10,... | collective-permute-start | bytes 786440 | tf_op jit(solution)/shard_map/ppermute | solution.py:27
  6.4 12.4 %collective-permute-start.6 = (bf16[1024,128]{1,0:T(8,128)(2,1)}, bf16[1024,128]{1,0:T(8,128)(2,1)S(1)}, u32[]{:S(2)}, u32[]{:S(2)}) collective-permute-start(bf16[1024,128]{1,0:T(8,128)(2,1)} %bitcast.10), channel_id=1, source_target_pairs={{0,3},{1,2},{2,1},{3,0},{4,7},{5,6},{6,5},{7,4},{8,11},{9,10},{10,... | collective-permute-start | bytes 786440 | tf_op jit(solution)/shard_map/ppermute | solution.py:27
  9.7 6.6 %collective-permute-start.1 = (bf16[64,1024]{1,0:T(8,128)(2,1)}, bf16[64,1024]{1,0:T(8,128)(2,1)S(1)}, u32[]{:S(2)}, u32[]{:S(2)}) collective-permute-start(bf16[64,1024]{1,0:T(8,128)(2,1)} %bitcast.13), channel_id=1, source_target_pairs={{0,4},{1,5},{2,6},{3,7},{4,0},{5,1},{6,2},{7,3},{8,12},{9,13},{10,... | collective-permute-start | bytes 393224 | tf_op jit(solution)/shard_map/ppermute | solution.py:27
  10.9 7.3 %collective-permute-start.3 = (bf16[64,1024]{1,0:T(8,128)(2,1)S(1)}, bf16[64,1024]{1,0:T(8,128)(2,1)S(1)}, u32[]{:S(2)}, u32[]{:S(2)}) collective-permute-start(bf16[64,1024]{1,0:T(8,128)(2,1)S(1)} %collective-permute-done.2.refs_2_), channel_id=1, source_target_pairs={{0,4},{1,5},{2,6},{3,7},{4,0},{5,1},{6,2},{7,3},{8,12},{9,13},{10,... | collective-permute-start | bytes 393224 | tf_op jit(solution)/shard_map/ppermute | solution.py:27
  11.8 0.9 %copy-start = (bf16[1,1024,128]{2,1,0:T(8,128)(2,1)S(1)}, bf16[1,1024,128]{2,1,0:T(8,128)(2,1)}, u32[]{:S(2)}) copy-start(bf16[1,1024,128]{2,1,0:T(8,128)(2,1)} %param.4) | copy-start | bytes 786436
  12.7 0.9 %copy-start.1 = (bf16[1,1,1024,128]{3,2,1,0:T(8,128)(2,1)S(1)}, bf16[1,1,1024,128]{3,2,1,0:T(8,128)(2,1)}, u32[]{:S(2)}) copy-start(bf16[1,1,1024,128]{3,2,1,0:T(8,128)(2,1)} %param.5) | copy-start | bytes 786436
  13.7 0.9 %copy-start.2 = (bf16[1,64,1024]{2,1,0:T(8,128)(2,1)S(1)}, bf16[1,64,1024]{2,1,0:T(8,128)(2,1)}, u32[]{:S(2)}) copy-start(bf16[1,64,1024]{2,1,0:T(8,128)(2,1)} %param.7) | copy-start | bytes 393220
  19.2 5.8 %collective-permute-start.7 = (bf16[256,128]{1,0:T(8,128)(2,1)S(1)}, bf16[256,128]{1,0:T(8,128)(2,1)S(1)}, u32[]{:S(2)}, u32[]{:S(2)}) collective-permute-start(bf16[256,128]{1,0:T(8,128)(2,1)S(1)} %get-tuple-element.27), channel_id=1, source_target_pairs={{0,1},{1,0},{2,3},{3,2},{4,5},{5,4},{6,7},{7,6},{8,9},{9,8},{10,11... | collective-permute-start | bytes 196616 | tf_op jit(solution)/shard_map/ppermute | solution.py:27
  20.5 4.9 %collective-permute-start.8 = (bf16[256,128]{1,0:T(8,128)(2,1)S(1)}, bf16[256,128]{1,0:T(8,128)(2,1)S(1)}, u32[]{:S(2)}, u32[]{:S(2)}) collective-permute-start(bf16[256,128]{1,0:T(8,128)(2,1)S(1)} %get-tuple-element.28), channel_id=1, source_target_pairs={{0,2},{1,3},{2,0},{3,1},{4,6},{5,7},{6,4},{7,5},{8,10},{9,11},{10,... | collective-permute-start | bytes 196616 | tf_op jit(solution)/shard_map/ppermute | solution.py:27
  21.8 5.2 %collective-permute-start.9 = (bf16[256,128]{1,0:T(8,128)(2,1)S(1)}, bf16[256,128]{1,0:T(8,128)(2,1)S(1)}, u32[]{:S(2)}, u32[]{:S(2)}) collective-permute-start(bf16[256,128]{1,0:T(8,128)(2,1)S(1)} %get-tuple-element.29), channel_id=1, source_target_pairs={{0,3},{1,2},{2,1},{3,0},{4,7},{5,6},{6,5},{7,4},{8,11},{9,10},{10,... | collective-permute-start | bytes 196616 | tf_op jit(solution)/shard_map/ppermute | solution.py:27
  28.3 2.6 %collective-permute-start.17 = (bf16[512,128]{1,0:T(8,128)(2,1)S(1)}, bf16[512,128]{1,0:T(8,128)(2,1)S(1)}, u32[]{:S(2)}, u32[]{:S(2)}) collective-permute-start(bf16[512,128]{1,0:T(8,128)(2,1)S(1)} %get-tuple-element.35), channel_id=1, source_target_pairs={{0,17},{1,16},{2,19},{3,18},{4,21},{5,20},{6,23},{7,22},{8,25},{9,... | collective-permute-start | bytes 393224 | tf_op jit(solution)/shard_map/ppermute | solution.py:37
  28.4 11.6 %collective-permute-start.14 = (bf16[1280,128]{1,0:T(8,128)(2,1)S(1)}, bf16[1280,128]{1,0:T(8,128)(2,1)S(1)}, u32[]{:S(2)}, u32[]{:S(2)}) collective-permute-start(bf16[1280,128]{1,0:T(8,128)(2,1)S(1)} %get-tuple-element.32), channel_id=1, source_target_pairs={{16,4},{17,5},{18,6},{19,7},{20,0},{21,1},{22,2},{23,3},{24,12},{2... | collective-permute-start | bytes 983048 | tf_op jit(solution)/shard_map/ppermute | solution.py:45
  28.9 3.9 %collective-permute-start.18 = (bf16[512,128]{1,0:T(8,128)(2,1)S(1)}, bf16[512,128]{1,0:T(8,128)(2,1)S(1)}, u32[]{:S(2)}, u32[]{:S(2)}) collective-permute-start(bf16[512,128]{1,0:T(8,128)(2,1)S(1)} %get-tuple-element.35), channel_id=1, source_target_pairs={{0,18},{1,19},{2,16},{3,17},{4,22},{5,23},{6,20},{7,21},{8,26},{9,... | collective-permute-start | bytes 393224 | tf_op jit(solution)/shard_map/ppermute | solution.py:37
  29.4 10.5 %collective-permute-start.10 = (bf16[1024,128]{1,0:T(8,128)(2,1)S(1)}, bf16[1024,128]{1,0:T(8,128)(2,1)S(1)}, u32[]{:S(2)}, u32[]{:S(2)}) collective-permute-start(bf16[1024,128]{1,0:T(8,128)(2,1)S(1)} %get-tuple-element.30.refs_2_), channel_id=1, source_target_pairs={{0,16},{1,17},{2,18},{3,19},{4,20},{5,21},{6,22},{7,23},{8,24},{9,... | collective-permute-start | bytes 786440 | tf_op jit(solution)/shard_map/ppermute | solution.py:37
  29.4 12.0 %collective-permute-start.15 = (bf16[1280,128]{1,0:T(8,128)(2,1)S(1)}, bf16[1280,128]{1,0:T(8,128)(2,1)S(1)}, u32[]{:S(2)}, u32[]{:S(2)}) collective-permute-start(bf16[1280,128]{1,0:T(8,128)(2,1)S(1)} %get-tuple-element.33), channel_id=1, source_target_pairs={{16,8},{17,9},{18,10},{19,11},{20,12},{21,13},{22,14},{23,15},{24,... | collective-permute-start | bytes 983048 | tf_op jit(solution)/shard_map/ppermute | solution.py:45
  30.9 17.1 %collective-permute-start.16 = (bf16[1280,128]{1,0:T(8,128)(2,1)S(1)}, bf16[1280,128]{1,0:T(8,128)(2,1)S(1)}, u32[]{:S(2)}, u32[]{:S(2)}) collective-permute-start(bf16[1280,128]{1,0:T(8,128)(2,1)S(1)} %get-tuple-element.34), channel_id=1, source_target_pairs={{16,12},{17,13},{18,14},{19,15},{20,8},{21,9},{22,10},{23,11},{24,... | collective-permute-start | bytes 983048 | tf_op jit(solution)/shard_map/ppermute | solution.py:45
  32.8 4.0 %collective-permute-start.19 = (bf16[512,128]{1,0:T(8,128)(2,1)S(1)}, bf16[512,128]{1,0:T(8,128)(2,1)S(1)}, u32[]{:S(2)}, u32[]{:S(2)}) collective-permute-start(bf16[512,128]{1,0:T(8,128)(2,1)S(1)} %get-tuple-element.35), channel_id=1, source_target_pairs={{0,19},{1,18},{2,17},{3,16},{4,23},{5,22},{6,21},{7,20},{8,27},{9,... | collective-permute-start | bytes 393224 | tf_op jit(solution)/shard_map/ppermute | solution.py:37
  36.8 11.5 %collective-permute-start.11 = (bf16[512,128]{1,0:T(8,128)(2,1)S(1)}, bf16[512,128]{1,0:T(8,128)(2,1)S(1)}, u32[]{:S(2)}, u32[]{:S(2)}) collective-permute-start(bf16[512,128]{1,0:T(8,128)(2,1)S(1)} %get-tuple-element.31), channel_id=1, source_target_pairs={{0,17},{1,16},{2,19},{3,18},{4,21},{5,20},{6,23},{7,22},{8,25},{9,... | collective-permute-start | bytes 393224 | tf_op jit(solution)/shard_map/ppermute | solution.py:37
  39.9 8.4 %collective-permute-start.12 = (bf16[512,128]{1,0:T(8,128)(2,1)S(1)}, bf16[512,128]{1,0:T(8,128)(2,1)S(1)}, u32[]{:S(2)}, u32[]{:S(2)}) collective-permute-start(bf16[512,128]{1,0:T(8,128)(2,1)S(1)} %get-tuple-element.31), channel_id=1, source_target_pairs={{0,18},{1,19},{2,16},{3,17},{4,22},{5,23},{6,20},{7,21},{8,26},{9,... | collective-permute-start | bytes 393224 | tf_op jit(solution)/shard_map/ppermute | solution.py:37
  39.9 8.4 %collective-permute-start.13 = (bf16[512,128]{1,0:T(8,128)(2,1)S(1)}, bf16[512,128]{1,0:T(8,128)(2,1)S(1)}, u32[]{:S(2)}, u32[]{:S(2)}) collective-permute-start(bf16[512,128]{1,0:T(8,128)(2,1)S(1)} %get-tuple-element.31), channel_id=1, source_target_pairs={{0,19},{1,18},{2,17},{3,16},{4,23},{5,22},{6,21},{7,20},{8,27},{9,... | collective-permute-start | bytes 393224 | tf_op jit(solution)/shard_map/ppermute | solution.py:37
  48.7 10.2 %collective-permute-start.20 = (bf16[64,1024]{1,0:T(8,128)(2,1)S(1)}, bf16[64,1024]{1,0:T(8,128)(2,1)S(1)}, u32[]{:S(2)}, u32[]{:S(2)}) collective-permute-start(bf16[64,1024]{1,0:T(8,128)(2,1)S(1)} %get-tuple-element.37), channel_id=1, source_target_pairs={{0,1},{1,0},{2,3},{3,2},{4,5},{5,4},{6,7},{7,6},{8,9},{9,8},{10,11... | collective-permute-start | bytes 393224 | tf_op jit(solution)/shard_map/ppermute | solution.py:55
  49.3 5.7 %collective-permute-start.21 = (bf16[64,512]{1,0:T(8,128)(2,1)S(1)}, bf16[64,512]{1,0:T(8,128)(2,1)S(1)}, u32[]{:S(2)}, u32[]{:S(2)}) collective-permute-start(bf16[64,512]{1,0:T(8,128)(2,1)S(1)} %get-tuple-element.39), channel_id=1, source_target_pairs={{0,2},{1,3},{2,0},{3,1},{4,6},{5,7},{6,4},{7,5},{8,10},{9,11},{10,... | collective-permute-start | bytes 196616 | tf_op jit(solution)/shard_map/ppermute | solution.py:55
  50.7 5.2 %collective-permute-start.22 = (bf16[64,512]{1,0:T(8,128)(2,1)S(1)}, bf16[64,512]{1,0:T(8,128)(2,1)S(1)}, u32[]{:S(2)}, u32[]{:S(2)}) collective-permute-start(bf16[64,512]{1,0:T(8,128)(2,1)S(1)} %get-tuple-element.40), channel_id=1, source_target_pairs={{0,3},{1,2},{2,1},{3,0},{4,7},{5,6},{6,5},{7,4},{8,11},{9,10},{10,... | collective-permute-start | bytes 196616 | tf_op jit(solution)/shard_map/ppermute | solution.py:55
  52.2 4.4 %collective-permute-start.23 = (bf16[64,512]{1,0:T(8,128)(2,1)S(1)}, bf16[64,512]{1,0:T(8,128)(2,1)S(1)}, u32[]{:S(2)}, u32[]{:S(2)}) collective-permute-start(bf16[64,512]{1,0:T(8,128)(2,1)S(1)} %get-tuple-element.42), channel_id=1, source_target_pairs={{0,2},{1,3},{2,0},{3,1},{4,6},{5,7},{6,4},{7,5},{8,10},{9,11},{10,... | collective-permute-start | bytes 196616 | tf_op jit(solution)/shard_map/ppermute | solution.py:55
  53.7 5.2 %collective-permute-start.24 = (bf16[64,512]{1,0:T(8,128)(2,1)S(1)}, bf16[64,512]{1,0:T(8,128)(2,1)S(1)}, u32[]{:S(2)}, u32[]{:S(2)}) collective-permute-start(bf16[64,512]{1,0:T(8,128)(2,1)S(1)} %get-tuple-element.43), channel_id=1, source_target_pairs={{0,3},{1,2},{2,1},{3,0},{4,7},{5,6},{6,5},{7,4},{8,11},{9,10},{10,... | collective-permute-start | bytes 196616 | tf_op jit(solution)/shard_map/ppermute | solution.py:55
